TPU v7x, 32 devices: a whole 2x2x4 slice. The times are simulated.
32 devices in a mesh: section: 8 (over z, x), dp: 4 (over y, core).
Axes of the slice: x: 2, y: 2, z: 4, core: 2. Of those that a mesh axis runs over, the one named last changes fastest.
Arguments:
- act_in: bfloat16 [8, 128, 2048], P('section', None, 'dp'), may hold values from -6 to 6
- saved_act: bfloat16 [8, 128, 2048], P('section', None, 'dp'), may hold values from -6 to 6
- cotangent: bfloat16 [8, 128, 2048], P('section', None, 'dp'), may hold values from -6 to 6
- weight_xz: bfloat16 [8, 2048, 8192], P('section', 'dp'), may hold values from -0.125 to 0.125
- weight_bcdt: bfloat16 [8, 320, 2048], P('section', None, 'dp'), may hold values from -0.125 to 0.125
- weight_out: bfloat16 [8, 4096, 2048], P('section', None, 'dp'), may hold values from -0.09375 to 0.09375
- conv_x: float32 [8, 4, 4096], P('section', None, 'dp'), may hold values from -3 to 3
- conv_bc: float32 [8, 4, 256], P('section'), may hold values from -3 to 3
- dt_bias: float32 [8, 64], P('section', 'dp'), may hold values from -8 to -2
- a_log: float32 [8, 64], P('section', 'dp'), may hold values from 0 to 2.7
- d_skip: float32 [8, 64], P('section', 'dp'), may hold values from 0.5 to 1.5
- norm_gain: float32 [8, 4096], P('section', 'dp'), may hold values from 0.1 to 1.9
Outputs:
- next_act: bfloat16 [8, 128, 2048], P('section', None, 'dp')
- prev_grad: bfloat16 [8, 128, 2048], P('section', None, 'dp')
- grad_xz: float32 [8, 2048, 8192], P('section', 'dp')
- grad_bcdt: float32 [8, 320, 2048], P('section', None, 'dp')
- grad_out: float32 [8, 4096, 2048], P('section', None, 'dp')
All inputs are finite; a program needn't handle non-finite values.
Results may differ from a plain program's by a relative error of at most 0.0084.
Values may be sent and summed in bfloat16 or wider, within the bound.
A program may use at most 128 MiB of HBM per device.

v0:
```python
import jax
import jax.numpy as jnp
from jax import lax
from jax.sharding import PartitionSpec as P

D = 2048
HEAD_DIM = 64
NSTATE = 128
HEADS = 64
SEQ = 128
INNER = 4096


def from_behind(x, axis, by):
    length = lax.axis_size(axis)
    return lax.ppermute(x, axis, [(i, (i + by) % length) for i in range(length)])


def causal_conv(values, kernel_taps):
    kernel = kernel_taps.shape[0]
    length = values.shape[1]
    padded = jnp.pad(values, ((0, 0), (kernel - 1, 0), (0, 0)))
    running = jnp.zeros_like(values)
    for offset in range(kernel):
        running = running + kernel_taps[offset] * padded[:, offset : offset + length]
    return running


def map_scores(maps):
    input_map = maps[:, :, :NSTATE]
    output_map = maps[:, :, NSTATE:]
    return lax.dot_general(
        output_map, input_map, (((2,), (2,)), ((0,), (0,))), preferred_element_type=jnp.float32
    )


def map_grads(d_scores, maps):
    values = maps.astype(jnp.float32)
    input_map = values[:, :, :NSTATE]
    output_map = values[:, :, NSTATE:]
    d_input = jnp.einsum("bts,btn->bsn", d_scores, output_map, precision=lax.Precision.HIGHEST)
    d_output = jnp.einsum("bts,bsn->btn", d_scores, input_map, precision=lax.Precision.HIGHEST)
    return jnp.concatenate([d_input, d_output], axis=2)


def mixer(proj_x, proj_z, proj_dt, scores, conv_taps, dt_offset, log_rate, skip_gain):
    batch, length, width = proj_x.shape
    nheads = dt_offset.shape[0]
    head_width = width // nheads
    xconv = jax.nn.silu(causal_conv(proj_x, conv_taps))
    steps = jax.nn.softplus(proj_dt + dt_offset)
    cumul = jnp.cumsum(steps * -jnp.exp(log_rate), axis=1)
    position = jnp.arange(length)
    causal = (position[:, None] >= position[None, :])[None, None]
    heads_cum = jnp.swapaxes(cumul, 1, 2)
    spread = heads_cum[:, :, :, None] - heads_cum[:, :, None, :]
    decay = jnp.where(causal, jnp.exp(jnp.where(causal, spread, 0.0)), 0.0)
    weights = decay * scores[:, None] * jnp.swapaxes(steps, 1, 2)[:, :, None, :]
    heads_in = xconv.reshape(batch, length, nheads, head_width)
    result = jnp.einsum("bhts,bshp->bthp", weights, heads_in, precision=lax.Precision.HIGHEST)
    result = result + skip_gain[None, None, :, None] * heads_in
    gate_in = jax.nn.silu(proj_z.reshape(batch, length, nheads, head_width))
    return (result * gate_in).reshape(batch * length, width)


def times_transposed(left, right):
    return lax.dot_general(
        left, right, (((1,), (1,)), ((), ())), preferred_element_type=jnp.float32
    )


def transposed_times(left, right):
    return lax.dot_general(
        left, right, (((0,), (0,)), ((), ())), preferred_element_type=jnp.float32
    )


def feature_sum(values):
    return lax.psum(jnp.sum(values, axis=1), "dp")


def gate_sum(values):
    return lax.psum(jnp.sum(values, axis=1), "dp")


def send_along(row_block, direction):
    return from_behind(row_block, "section", direction)


def per_device(
    act_in,
    saved_act,
    cotangent,
    weight_xz,
    weight_bcdt,
    weight_out,
    conv_x,
    conv_bc,
    dt_bias,
    a_log,
    d_skip,
    norm_gain,
):
    input_rows = act_in[0]
    saved_rows = saved_act[0]
    cot_rows = cotangent[0]
    local_xz = weight_xz[0]
    local_bcdt = weight_bcdt[0]
    local_out = weight_out[0]
    taps_x = conv_x[0]
    taps_bc = conv_bc[0]
    dt_offset = dt_bias[0]
    log_rate = a_log[0]
    skip_gain = d_skip[0]
    gain_local = norm_gain[0]
    own_heads = dt_offset.shape[0]
    head_first = lax.axis_index("dp") * own_heads
    map_cols = 2 * NSTATE

    def whole_act(pre_part):
        batches = pre_part.shape[0] // SEQ
        conv_in = pre_part.reshape(batches, SEQ, map_cols)
        return jax.nn.silu(causal_conv(conv_in, taps_bc)).reshape(pre_part.shape)

    def project(rows):
        values = rows.astype(jnp.float32)
        scales = lax.rsqrt(feature_sum(values * values)[:, None] / D + 1e-05)
        normed = (values * scales).astype(jnp.bfloat16)
        part_xz = jnp.dot(normed, local_xz, preferred_element_type=jnp.float32)
        part_bcdt = times_transposed(normed, local_bcdt)
        own_xz = lax.psum_scatter(part_xz, "dp", scatter_dimension=1, tiled=True)
        whole_cols = lax.psum(part_bcdt, "dp")
        pre_part = whole_cols[:, :map_cols]
        maps = whole_act(pre_part).astype(jnp.bfloat16)
        own_dt = lax.dynamic_slice_in_dim(whole_cols[:, map_cols:], head_first, own_heads, 1)
        return (values, normed, scales, own_xz, pre_part, maps, own_dt)

    def gate_parts(projected):
        own_xz = projected[3]
        maps = projected[5]
        own_dt = projected[6]
        batches = own_xz.shape[0] // SEQ
        width = own_heads * HEAD_DIM
        split_xz = own_xz.reshape(batches, SEQ, own_heads, 2, HEAD_DIM)
        mix_x = split_xz[:, :, :, 0].reshape(batches, SEQ, width)
        mix_z = split_xz[:, :, :, 1].reshape(batches, SEQ, width)
        maps_three = maps.reshape(batches, SEQ, map_cols)
        scores = map_scores(maps_three)

        def local_mix(in_x, in_z, in_dt, in_scores):
            return mixer(in_x, in_z, in_dt, in_scores, taps_x, dt_offset, log_rate, skip_gain)

        gated, mix_back = jax.vjp(
            local_mix, mix_x, mix_z, own_dt.reshape(batches, SEQ, own_heads), scores
        )
        inverse = lax.rsqrt(gate_sum(gated * gated)[:, None] / INNER + 1e-05)
        mixed_in = (gated * inverse * gain_local).astype(jnp.bfloat16)
        return (gated, mix_back, inverse, mixed_in, maps_three)

    forward_proj = project(input_rows)
    back_proj = project(saved_rows)
    forward_mixed = gate_parts(forward_proj)[3]
    mixed = jnp.dot(
        lax.all_gather(forward_mixed, "dp", axis=1, tiled=True),
        local_out,
        preferred_element_type=jnp.float32,
    )
    section_out = (input_rows.astype(jnp.float32) + mixed).astype(jnp.bfloat16)
    next_act = send_along(section_out, 1)
    values, normed, scales, own_xz, pre_part, maps, own_dt = back_proj
    gated, mix_back, inverse, mixed_in, maps_three = gate_parts(back_proj)
    row_count = values.shape[0]
    grad_out = transposed_times(lax.all_gather(mixed_in, "dp", axis=1, tiled=True), cot_rows)
    d_mixed = lax.psum_scatter(
        times_transposed(cot_rows, local_out), "dp", scatter_dimension=1, tiled=True
    )
    dots = gate_sum(d_mixed * gain_local * gated)
    d_gated = (
        inverse * gain_local * d_mixed
        - gated * (inverse * inverse * inverse) * dots[:, None] / INNER
    )
    d_px, d_pz, d_pdt, d_scores = mix_back(d_gated)
    d_maps = map_grads(d_scores, maps_three).reshape(row_count, map_cols)
    d_dt_full = lax.dynamic_update_slice_in_dim(
        jnp.zeros((row_count, HEADS), jnp.float32),
        d_pdt.reshape(row_count, own_heads),
        head_first,
        1,
    )
    map_part = jnp.concatenate([d_maps, d_dt_full], axis=1)
    summed = lax.psum(map_part, "dp")
    conv_out, conv_back = jax.vjp(whole_act, pre_part)
    d_pre = conv_back(summed[:, :map_cols])[0]
    round_bcdt = jnp.concatenate([d_pre, summed[:, map_cols:]], axis=1).astype(jnp.bfloat16)
    own_round = (
        jnp.stack(
            [
                d_px.reshape(row_count, own_heads, HEAD_DIM),
                d_pz.reshape(row_count, own_heads, HEAD_DIM),
            ],
            axis=2,
        )
        .reshape(row_count, own_heads * 2 * HEAD_DIM)
        .astype(jnp.bfloat16)
    )
    round_xz = lax.all_gather(own_round, "dp", axis=1, tiled=True)
    grad_xz = transposed_times(normed, round_xz)
    grad_bcdt = transposed_times(round_bcdt, normed)
    d_normed = times_transposed(round_xz, local_xz)
    d_normed = d_normed + jnp.dot(round_bcdt, local_bcdt, preferred_element_type=jnp.float32)
    inner_sum = feature_sum(d_normed * values)[:, None]
    d_norm_in = scales * d_normed - values * (scales * scales * scales) * inner_sum / D
    d_input = (cot_rows.astype(jnp.float32) + d_norm_in).astype(jnp.bfloat16)
    prev_grad = send_along(d_input, -1)
    return (next_act[None], prev_grad[None], grad_xz[None], grad_bcdt[None], grad_out[None])


def solution(mesh):
    return jax.shard_map(
        per_device,
        mesh=mesh,
        in_specs=(
            P("section", None, "dp"),
            P("section", None, "dp"),
            P("section", None, "dp"),
            P("section", "dp", None),
            P("section", None, "dp"),
            P("section", None, "dp"),
            P("section", None, "dp"),
            P("section", None, None),
            P("section", "dp"),
            P("section", "dp"),
            P("section", "dp"),
            P("section", "dp"),
        ),
        out_specs=(
            P("section", None, "dp"),
            P("section", None, "dp"),
            P("section", "dp", None),
            P("section", None, "dp"),
            P("section", None, "dp"),
        ),
        check_vma=False,
    )
```

profile of v0, /device:TPU:0, one launch (start us, length us, event | category | flops | bytes accessed | tf_op | source)
XLA Modules:
  0.0 311.2 jit_solution(6612498661934579519)
XLA Ops:
  8.3 8.4 %psum.66 = f32[128]{0:T(128)S(1)} all-reduce(f32[128]{0:T(128)S(1)} %fusion.86), channel_id=1, replica_groups=mesh['section'=8,'dp'=4] {'dp'}, use_global_device_ids=true, to_apply=%region_8.9 | all-reduce | flops 128 | bytes 1024 | tf_op jit(solution)/shard_map/psum | solution.py:79
  17.2 1.9 fusion.80
  19.2 6.8 %fusion.2 = f32[128,8192]{1,0:T(8,128)} fusion(bf16[1,512,8192]{2,1,0:T(8,128)(2,1)} %param.15, bf16[1,128,512]{2,1,0:T(8,128)(2,1)} %param.13, f32[128]{0:T(128)S(1)} %get-tuple-element.49), kind=kOutput, calls=%fused_computation.3 | convolution fusion | flops 1073938432 | bytes 12714496 | tf_op jit(solution)/shard_map/dot_general | solution.py:129
  26.9 5.0 %fusion.6 = f32[128,4096]{1,0:T(8,128)} fusion(bf16[1,4096,512]{2,1,0:T(8,128)(2,1)} %param.17, bf16[1,128,512]{2,1,0:T(8,128)(2,1)S(1)} %copy-done.5), kind=kOutput, calls=%fused_computation.8 | convolution fusion | flops 536870912 | bytes 6422528 | tf_op jit(solution)/shard_map/dot_general | solution.py:67
  32.2 19.0 %all-reduce.18.cloned.1.call-done = f32[128,320]{0,1:T(8,128)} async-done(((f32[128,320]{0,1:T(8,128)}), f32[128,320]{0,1:T(8,128)}) %all-reduce.18.cloned.1.call-update) | async-done | bytes 163856 | tf_op jit(solution)/shard_map/psum | solution.py:132
  53.3 1.9 multiply_convert_fusion.2
  55.4 43.6 %reduce-scatter.6.cloned.1.call-done = f32[128,2048]{1,0:T(8,128)} async-done(((f32[128,8192]{1,0:T(8,128)}), f32[128,2048]{1,0:T(8,128)}) %reduce-scatter.6.cloned.1.call-update) | async-done | bytes 1048592 | tf_op jit(solution)/shard_map/reduce_scatter | solution.py:131
  99.0 1.5 copy.55
  101.8 3.0 multiply_reduce_fusion.3
  104.8 1.2 copy.60
  106.1 27.5 %reduce-scatter.8.cloned.1.call-done = f32[128,1024]{1,0:T(8,128)} async-done(((f32[128,4096]{1,0:T(8,128)}), f32[128,1024]{1,0:T(8,128)}) %reduce-scatter.8.cloned.1.call-update) | async-done | bytes 524304 | tf_op jit(solution)/shard_map/reduce_scatter | solution.py:174
  134.7 5.8 %all-reduce.13 = (f32[128]{0:T(128)S(1)}, f32[128]{0:T(128)S(1)}, f32[128]{0:T(128)S(1)}) all-reduce(f32[128]{0:T(128)S(1)} %fusion.84, f32[128]{0:T(128)S(1)} %multiply_reduce_fusion.2, f32[128]{0:T(128)S(1)} %get-tuple-element.20), channel_id=1, replica_groups=mesh['section'=8,'dp'=4] {'dp'}, use_global_device_ids=true, to_apply=%region_1.0 | all-reduce | flops 384 | bytes 3072 | tf_op jit(solution)/shard_map/psum | solution.py:79
  140.5 6.7 %fusion.4 = f32[128,8192]{1,0:T(8,128)} fusion(bf16[1,512,8192]{2,1,0:T(8,128)(2,1)} %param.15, bf16[1,128,512]{2,1,0:T(8,128)(2,1)S(1)} %copy-done.3, f32[128]{0:T(128)S(1)} %add_rsqrt_fusion.3), kind=kOutput, calls=%fused_computation.5 | convolution fusion | flops 1073938432 | bytes 12714496 | tf_op jit(solution)/shard_map/dot_general | solution.py:129
  147.5 2.0 multiply_convert_fusion
  149.7 4.2 %fusion.32 = (f32[16,128]{1,0:T(8,128)S(1)}, f32[16,128]{1,0:T(8,128)S(1)}, f32[16,128]{1,0:T(8,128)}, f32[128,128]{1,0:T(8,128)S(1)}) fusion(f32[16,128]{1,0:T(8,128)S(1)} %get-tuple-element.37, f32[128,128]{1,0:T(8,128)S(1)} %fusion.125, f32[16,128]{1,0:T(8,128)S(1)} %copy.57, pred[128,128]{1,0:T(8,128)(4,1)S(1)} %iota_compare_fusion, ...), kind=kOutput, calls=%fused_computation.47 | convolution fusion | flops 205891584 | bytes 1769472 | tf_op jit(solution)/shard_map/transpose(jvp(bhts,bshp->bthp))/dot_general | solution.py:60
  157.2 1.7 fusion.82
  159.1 2.3 fusion.10
  161.7 31.3 %reduce-scatter.4.cloned.1.call-done = f32[128,2048]{1,0:T(8,128)} async-done(((f32[128,8192]{1,0:T(8,128)}), f32[128,2048]{1,0:T(8,128)}) %reduce-scatter.4.cloned.1.call-update) | async-done | bytes 1048592 | tf_op jit(solution)/shard_map/reduce_scatter | solution.py:131
  193.0 1.5 copy.49
  194.6 1.9 broadcast_multiply_fusion.1
  198.9 28.8 %all-reduce.20.cloned.1.call-done = (f32[128,320]{0,1:T(8,128)}, f32[128,320]{0,1:T(8,128)}) async-done(((f32[128,320]{0,1:T(8,128)}, f32[128,320]{0,1:T(8,128)}), (f32[128,320]{0,1:T(8,128)}, f32[128,320]{0,1:T(8,128)})) %all-reduce.20.cloned.1.call-update) | async-done | bytes 327696 | tf_op jit(solution)/shard_map/psum | solution.py:132
  233.2 3.3 %multiply_reduce_fusion.4 = (f32[128]{0:T(128)S(1)}, f32[1,128,16,64]{1,3,2,0:T(8,128)S(1)}) fusion(f32[1,128,16,2,64]{1,4,3,2,0:T(8,128)S(1)} %bitcast.276, f32[1,128,16,64]{1,3,2,0:T(8,128)} %bitcast.288, f32[16]{0:T(128)S(1)} %bitcast.320, f32[128,16,64]{0,2,1:T(8,128)} %bitcast.289, f32[16,128]{1,0:T(8,128)S(1)} %get-tuple-element.35, ...), kind=kOutput, calls=%fused_computation.94 | convolution fusion | flops 203816832 | bytes 2204672 | tf_op jit(solution)/shard_map/jvp(bhts,bshp->bthp)/dot_general | solution.py:60
  236.8 15.6 %all-gather.6.cloned.1.call-done = bf16[128,8192]{0,1:T(8,128)(2,1)} async-done(((bf16[128,2048]{0,1:T(8,128)(2,1)}), bf16[128,8192]{0,1:T(8,128)(2,1)}) %all-gather.6.cloned.1.call-update) | async-done | bytes 2097168 | tf_op jit(solution)/shard_map/all_gather | solution.py:206
  252.3 6.9 %fusion = f32[128,512]{1,0:T(8,128)S(1)} fusion(bf16[128,8192]{0,1:T(8,128)(2,1)} %all-gather.6.cloned.1.call-done, bf16[1,512,8192]{2,1,0:T(8,128)(2,1)} %param.15), kind=kOutput, calls=%fused_computation.1 | convolution fusion | flops 1073741824 | bytes 10747904 | tf_op jit(solution)/shard_map/dot_general | solution.py:67
  259.6 6.3 %all-reduce.12 = (f32[128]{0:T(128)S(1)}, f32[128]{0:T(128)S(1)}) all-reduce(f32[128]{0:T(128)S(1)} %get-tuple-element.53, f32[128]{0:T(128)S(1)} %get-tuple-element.55), channel_id=1, replica_groups=mesh['section'=8,'dp'=4] {'dp'}, use_global_device_ids=true, to_apply=%region_6.7 | all-reduce | flops 256 | bytes 2048 | tf_op jit(solution)/shard_map/psum | solution.py:83
  267.9 3.4 %all-gather.8.cloned.1.call-done = bf16[128,4096]{1,0:T(8,128)(2,1)} async-done(((bf16[128,1024]{1,0:T(8,128)(2,1)}), bf16[128,4096]{1,0:T(8,128)(2,1)}) %all-gather.8.cloned.1.call-update) | async-done | bytes 1048592 | tf_op jit(solution)/shard_map/all_gather | solution.py:173
  271.3 5.9 %convolution_bitcast_fusion.1 = f32[1,4096,512]{2,1,0:T(8,128)} fusion(bf16[128,4096]{1,0:T(8,128)(2,1)} %all-gather.8.cloned.1.call-done, bf16[1,128,512]{2,1,0:T(8,128)(2,1)S(1)} %copy-done.5), kind=kOutput, calls=%fused_computation.7 | convolution fusion | flops 536870912 | bytes 9568256 | tf_op jit(solution)/shard_map/dot_general | solution.py:73
  277.4 4.3 %collective-permute-start.1 = (bf16[128,512]{1,0:T(8,128)(2,1)S(1)}, bf16[128,512]{1,0:T(8,128)(2,1)S(1)}, u32[]{:S(2)}, u32[]{:S(2)}) collective-permute-start(bf16[128,512]{1,0:T(8,128)(2,1)S(1)} %fusion.91), channel_id=1, source_target_pairs={{0,28},{4,0},{8,4},{12,8},{16,12},{20,16},{24,20},{28,24},{1,29},{... | collective-permute-start | bytes 393224 | tf_op jit(solution)/shard_map/ppermute | solution.py:16
  281.7 8.0 %all-gather.4.cloned.1.call-done = bf16[128,4096]{1,0:T(8,128)(2,1)} async-done(((bf16[128,1024]{1,0:T(8,128)(2,1)}), bf16[128,4096]{1,0:T(8,128)(2,1)}) %all-gather.4.cloned.1.call-update) | async-done | bytes 1048592 | tf_op jit(solution)/shard_map/all_gather | solution.py:164
  289.7 3.2 %fusion.17 = bf16[128,512]{1,0:T(8,128)(2,1)S(1)} fusion(bf16[128,4096]{1,0:T(8,128)(2,1)} %all-gather.4.cloned.1.call-done, bf16[1,4096,512]{2,1,0:T(8,128)(2,1)} %param.17, bf16[1,128,512]{2,1,0:T(8,128)(2,1)S(1)} %copy-done.4), kind=kOutput, calls=%fused_computation.28 | convolution fusion | flops 537067520 | bytes 5505024 | tf_op jit(solution)/shard_map/dot_general | solution.py:163
  292.9 1.5 collective-permute-start
  294.4 8.6 %convolution_bitcast_fusion = f32[1,512,8192]{2,1,0:T(8,128)} fusion(bf16[128,8192]{0,1:T(8,128)(2,1)S(1)} %copy-done.1, bf16[1,128,512]{2,1,0:T(8,128)(2,1)S(1)} %copy-done.2, f32[128]{0:T(128)S(1)} %get-tuple-element.49), kind=kOutput, calls=%fused_computation | convolution fusion | flops 1073938432 | bytes 19005952 | tf_op jit(solution)/shard_map/dot_general | solution.py:73
  (131 shorter events, 23.6 us)
Async XLA Ops:
  7.2 10.1 %copy-start = (bf16[1,320,512]{2,1,0:T(8,128)(2,1)S(1)}, bf16[1,320,512]{2,1,0:T(8,128)(2,1)}, u32[]{:S(2)}) copy-start(bf16[1,320,512]{2,1,0:T(8,128)(2,1)} %param.16) | copy-start | bytes 983044
  7.2 44.0 %all-reduce.18.cloned.1.call-start = ((), (), s32[]{:S(2)}) async-start(), calls=%async_computation.6 | async-start | bytes 327680 | tf_op jit(solution)/shard_map/psum | solution.py:132
  19.2 79.8 %reduce-scatter.6.cloned.1.call-start = ((), (), s32[]{:S(2)}) async-start(), calls=%async_computation.5 | async-start | bytes 5242880 | tf_op jit(solution)/shard_map/reduce_scatter | solution.py:131
  26.1 25.9 %copy-start.19 = (f32[1,16]{1,0:T(1,128)S(1)}, f32[1,16]{1,0:T(1,128)}, u32[]{:S(2)}) copy-start(f32[1,16]{1,0:T(1,128)} %param.20) | copy-start | bytes 196
  26.1 107.5 %reduce-scatter.8.cloned.1.call-start = ((), (), s32[]{:S(2)}) async-start(), calls=%async_computation.7 | async-start | bytes 2621440 | tf_op jit(solution)/shard_map/reduce_scatter | solution.py:174
  31.9 69.9 %copy-start.27 = (f32[1,16]{1,0:T(1,128)S(1)}, f32[1,16]{1,0:T(1,128)}, u32[]{:S(2)}) copy-start(f32[1,16]{1,0:T(1,128)} %param.22) | copy-start | bytes 196
  31.9 161.1 %reduce-scatter.4.cloned.1.call-start = ((), (), s32[]{:S(2)}) async-start(), calls=%async_computation.3 | async-start | bytes 5242880 | tf_op jit(solution)/shard_map/reduce_scatter | solution.py:131
  32.1 21.2 %copy-start.21 = (f32[16]{0:T(128)}, f32[16]{0:T(128)S(1)}, u32[]{:S(2)}) copy-start(f32[16]{0:T(128)S(1)} %negate_bitcast_fusion) | copy-start | bytes 196
  32.2 68.4 %copy-start.13 = (f32[1,1,256]{2,1,0:T(1,128)}, f32[1,1,256]{2,1,0:T(1,128)S(1)}, u32[]{:S(2)}) copy-start(f32[1,1,256]{2,1,0:T(1,128)S(1)} %get-tuple-element.44) | copy-start | bytes 3076
  32.2 72.6 %copy-start.15 = (f32[1,1,256]{2,1,0:T(1,128)}, f32[1,1,256]{2,1,0:T(1,128)S(1)}, u32[]{:S(2)}) copy-start(f32[1,1,256]{2,1,0:T(1,128)S(1)} %get-tuple-element.46) | copy-start | bytes 3076
  52.0 97.6 %copy-start.17 = (f32[16,128]{1,0:T(8,128)}, f32[16,128]{1,0:T(8,128)S(1)}, u32[]{:S(2)}) copy-start(f32[16,128]{1,0:T(8,128)S(1)} %get-tuple-element.37) | copy-start | bytes 24580
  52.4 97.3 %copy-start.18 = (f32[16,128]{1,0:T(8,128)}, f32[16,128]{1,0:T(8,128)S(1)}, u32[]{:S(2)}) copy-start(f32[16,128]{1,0:T(8,128)S(1)} %copy.57) | copy-start | bytes 24580
  55.4 94.3 %copy-start.10 = (f32[128,128]{1,0:T(8,128)}, f32[128,128]{1,0:T(8,128)S(1)}, u32[]{:S(2)}) copy-start(f32[128,128]{1,0:T(8,128)S(1)} %fusion.125) | copy-start | bytes 196612
  100.6 33.0 %copy-start.11 = (f32[1,1024]{1,0:T(1,128)S(1)}, f32[1,1024]{1,0:T(1,128)}, u32[]{:S(2)}) copy-start(f32[1,1024]{1,0:T(1,128)} %param.23) | copy-start | bytes 12292
  101.8 45.4 %copy-start.8 = (f32[1,128,1024]{1,2,0:T(8,128)}, f32[1,128,1024]{1,2,0:T(8,128)S(1)}, u32[]{:S(2)}) copy-start(f32[1,128,1024]{1,2,0:T(8,128)S(1)} %get-tuple-element.24) | copy-start | bytes 1572868
  147.3 80.4 %all-reduce.20.cloned.1.call-start = ((), (), s32[]{:S(2)}) async-start(), calls=%async_computation.10 | async-start | bytes 655360 | tf_op jit(solution)/shard_map/psum | solution.py:132
  161.7 90.6 %all-gather.6.cloned.1.call-start = ((), (), s32[]{:S(2)}) async-start(), calls=%async_computation.8 | async-start | bytes 2621440 | tf_op jit(solution)/shard_map/all_gather | solution.py:206
  194.6 35.5 %copy-start.9 = (f32[1,128,256]{1,2,0:T(8,128)S(1)}, f32[1,128,256]{1,2,0:T(8,128)}, u32[]{:S(2)}) copy-start(f32[1,128,256]{1,2,0:T(8,128)} %get-tuple-element.23) | copy-start | bytes 393220
  194.6 36.5 %copy-start.14 = (f32[1,1,256]{2,1,0:T(1,128)S(1)}, f32[1,1,256]{2,1,0:T(1,128)}, u32[]{:S(2)}) copy-start(f32[1,1,256]{2,1,0:T(1,128)} %copy-done.13) | copy-start | bytes 3076
  194.6 36.5 %copy-start.16 = (f32[1,1,256]{2,1,0:T(1,128)S(1)}, f32[1,1,256]{2,1,0:T(1,128)}, u32[]{:S(2)}) copy-start(f32[1,1,256]{2,1,0:T(1,128)} %copy-done.15) | copy-start | bytes 3076
  196.5 36.1 %copy-start.20 = (f32[1,16]{1,0:T(1,128)S(1)}, f32[1,16]{1,0:T(1,128)}, u32[]{:S(2)}) copy-start(f32[1,16]{1,0:T(1,128)} %param.20) | copy-start | bytes 196
  196.5 36.1 %copy-start.22 = (f32[16]{0:T(128)S(1)}, f32[16]{0:T(128)}, u32[]{:S(2)}) copy-start(f32[16]{0:T(128)} %copy-done.21) | copy-start | bytes 196
  196.5 36.7 %copy-start.28 = (f32[1,16]{1,0:T(1,128)S(1)}, f32[1,16]{1,0:T(1,128)}, u32[]{:S(2)}) copy-start(f32[1,16]{1,0:T(1,128)} %param.22) | copy-start | bytes 196
  197.9 73.4 %all-gather.8.cloned.1.call-start = ((), (), s32[]{:S(2)}) async-start(), calls=%async_computation.9 | async-start | bytes 1310720 | tf_op jit(solution)/shard_map/all_gather | solution.py:173
  198.6 91.0 %all-gather.4.cloned.1.call-start = ((), (), s32[]{:S(2)}) async-start(), calls=%async_computation.4 | async-start | bytes 1310720 | tf_op jit(solution)/shard_map/all_gather | solution.py:164
  236.7 22.5 %copy-start.2 = (bf16[1,128,512]{2,1,0:T(8,128)(2,1)S(1)}, bf16[1,128,512]{2,1,0:T(8,128)(2,1)}, u32[]{:S(2)}) copy-start(bf16[1,128,512]{2,1,0:T(8,128)(2,1)} %param.13) | copy-start | bytes 393220
  267.9 9.3 %copy-start.6 = (bf16[1,128,512]{2,1,0:T(8,128)(2,1)S(1)}, bf16[1,128,512]{2,1,0:T(8,128)(2,1)}, u32[]{:S(2)}) copy-start(bf16[1,128,512]{2,1,0:T(8,128)(2,1)} %param.14) | copy-start | bytes 393220
  267.9 9.3 %copy-start.25 = (f32[128]{0:T(128)S(1)}, f32[128]{0:T(128)}, u32[]{:S(2)}) copy-start(f32[128]{0:T(128)} %get-tuple-element.48) | copy-start | bytes 1540
  267.9 21.8 %copy-start.4 = (bf16[1,128,512]{2,1,0:T(8,128)(2,1)S(1)}, bf16[1,128,512]{2,1,0:T(8,128)(2,1)}, u32[]{:S(2)}) copy-start(bf16[1,128,512]{2,1,0:T(8,128)(2,1)} %param.12) | copy-start | bytes 393220
  277.2 17.2 %copy-start.1 = (bf16[128,8192]{0,1:T(8,128)(2,1)S(1)}, bf16[128,8192]{0,1:T(8,128)(2,1)}, u32[]{:S(2)}) copy-start(bf16[128,8192]{0,1:T(8,128)(2,1)} %all-gather.6.cloned.1.call-done) | copy-start | bytes 6291460
  277.4 25.7 %collective-permute-start.1 = (bf16[128,512]{1,0:T(8,128)(2,1)S(1)}, bf16[128,512]{1,0:T(8,128)(2,1)S(1)}, u32[]{:S(2)}, u32[]{:S(2)}) collective-permute-start(bf16[128,512]{1,0:T(8,128)(2,1)S(1)} %fusion.91), channel_id=1, source_target_pairs={{0,28},{4,0},{8,4},{12,8},{16,12},{20,16},{24,20},{28,24},{1,29},{... | collective-permute-start | bytes 393224 | tf_op jit(solution)/shard_map/ppermute | solution.py:16
  292.9 10.1 %collective-permute-start = (bf16[128,512]{1,0:T(8,128)(2,1)S(1)}, bf16[128,512]{1,0:T(8,128)(2,1)S(1)}, u32[]{:S(2)}, u32[]{:S(2)}) collective-permute-start(bf16[128,512]{1,0:T(8,128)(2,1)S(1)} %fusion.17), channel_id=1, source_target_pairs={{0,4},{4,8},{8,12},{12,16},{16,20},{20,24},{24,28},{28,0},{1,5},{5... | collective-permute-start | bytes 393224 | tf_op jit(solution)/shard_map/ppermute | solution.py:16
  (7 other events, 41.0 us)
Sparse Core Ops, SparseCore 0:
  19.3 31.8 all-reduce.17
  54.4 44.5 reduce-scatter.5
  102.1 31.4 reduce-scatter.7
  147.4 45.5 reduce-scatter.3
  195.2 32.4 all-reduce.19
  229.7 22.5 all-gather.5
  254.4 16.8 all-gather.7
  272.9 16.7 all-gather.3
where the time goes:
time: 312 us; the launch traced here: 311 us
  waiting for transfers between devices  178 us (57%)
  matrix products  61.8 us (20%)
  blocking collectives  20.4 us (7%)
  other arithmetic  17.4 us (6%)
  between operations  14.7 us (5%)
  local copies, waits for them, and re-layouts  12.5 us (4%)
  starting transfers between devices  6.58 us (2%)
    reduce_scatter x2, waiting for transfers between devices, project(): own_xz = lax.psum_scatter(part_xz, 'dp', scatter_dimension=1, tiled=True)  74.9 us
    psum x2, waiting for transfers between devices, project(): whole_cols = lax.psum(part_bcdt, 'dp')  47.7 us
    reduce_scatter x1, waiting for transfers between devices, per_device(): lax.psum_scatter(times_transposed(cot_rows, local_out), 'dp', scatter_dim...  27.5 us
    dot_general x3, matrix products, transposed_times(): lax.dot_general(left, right, (((0,), (0,)), ((), ())), preferred_element_...  15.6 us
    all_gather x1, waiting for transfers between devices, per_device(): round_xz = lax.all_gather(own_round, 'dp', axis=1, tiled=True)  15.6 us
    dot_general x4, matrix products, times_transposed(): lax.dot_general(left, right, (((1,), (1,)), ((), ())), preferred_element_...  15.5 us
    psum x2, blocking collectives, feature_sum(): return lax.psum(jnp.sum(values, axis=1), 'dp')  14.1 us
    dot_general x2, matrix products, project(): part_xz = jnp.dot(normed, local_xz, preferred_element_type=jnp.float32)  13.5 us
  transfers between devices with their start and end apart: 10, of which 8 were waited for; matrix products, arithmetic and copies ran while one was open for 25% of the time, Pallas kernels for 0%

commit v1 on v0

v1 whole, which is shorter than its diff:
```python
import jax
import jax.numpy as jnp
from jax import lax
from jax.sharding import PartitionSpec as P

D = 2048
HEAD_DIM = 64
NSTATE = 128
HEADS = 64
SEQ = 128
INNER = 4096
MAPS = 2 * NSTATE


def from_behind(x, axis, by):
    length = lax.axis_size(axis)
    return lax.ppermute(x, axis, [(i, (i + by) % length) for i in range(length)])


def swap(x, mask):
    length = lax.axis_size("dp")
    return lax.ppermute(x, "dp", [(i, i ^ mask) for i in range(length)])


def masks():
    length = lax.axis_size("dp")
    out = []
    bit = 1
    while bit < length:
        out.append(bit)
        bit *= 2
    return out


def sum_all(x):
    for bit in masks():
        x = x + swap(x, bit)
    return x


def sum_scatter(part):
    length = lax.axis_size("dp")
    held = None
    for bit in masks():
        live = [j for j in range(0, length, bit)]
        away = [j for j in live if j & bit]
        home = [j for j in live if not j & bit]
        if held is None:
            sent = [part(j).astype(jnp.bfloat16) for j in away]
        else:
            sent = [held[j].astype(jnp.bfloat16) for j in away]
        came = [swap(s, bit) for s in sent]
        if held is None:
            held = {j: part(j) for j in home}
        held = {j: held[j] + c.astype(jnp.float32) for j, c in zip(home, came)}
    return held[0]


def gather_cols(block):
    me = lax.axis_index("dp")
    rows, width = block.shape
    length = lax.axis_size("dp")
    held = [block]
    for bit in reversed(masks()):
        held = held + [swap(b, bit) for b in held]
    order = [0]
    for bit in reversed(masks()):
        order = order + [j ^ bit for j in order]
    by_mask = {j: b for j, b in zip(order, held)}
    level = [by_mask[j] for j in range(length)]
    for bit in masks():
        flip = (me & bit) != 0
        level = [jnp.where(flip, level[j ^ bit], level[j]) for j in range(length)]
    return jnp.concatenate(level, axis=1)


def causal_conv(values, kernel_taps):
    kernel = kernel_taps.shape[0]
    length = values.shape[0]
    padded = jnp.pad(values, ((kernel - 1, 0), (0, 0)))
    running = jnp.zeros_like(values)
    for offset in range(kernel):
        running = running + kernel_taps[offset] * padded[offset : offset + length]
    return running


def mixer(proj_x, proj_z, proj_dt, scores, conv_taps, dt_offset, log_rate, skip_gain):
    length, width = proj_x.shape
    nheads = dt_offset.shape[0]
    head_width = width // nheads
    xconv = jax.nn.silu(causal_conv(proj_x, conv_taps))
    steps = jax.nn.softplus(proj_dt + dt_offset)
    position = jnp.arange(length)
    causal = position[:, None] >= position[None, :]
    cumul = jnp.dot(
        causal.astype(jnp.float32), steps * -jnp.exp(log_rate), precision=lax.Precision.HIGHEST
    )
    heads_cum = cumul.T
    spread = heads_cum[:, :, None] - heads_cum[:, None, :]
    decay = jnp.where(causal[None], jnp.exp(jnp.where(causal[None], spread, 0.0)), 0.0)
    weights = decay * scores[None] * steps.T[:, None, :]
    heads_in = xconv.reshape(length, nheads, head_width)
    result = jnp.einsum("hts,shp->thp", weights, heads_in, precision=lax.Precision.HIGH)
    result = result + skip_gain[None, :, None] * heads_in
    gate_in = jax.nn.silu(proj_z.reshape(length, nheads, head_width))
    return (result * gate_in).reshape(length, width)


def times_transposed(left, right):
    return lax.dot_general(
        left, right, (((1,), (1,)), ((), ())), preferred_element_type=jnp.float32
    )


def transposed_times(left, right):
    return lax.dot_general(
        left, right, (((0,), (0,)), ((), ())), preferred_element_type=jnp.float32
    )


def per_device(
    act_in,
    saved_act,
    cotangent,
    weight_xz,
    weight_bcdt,
    weight_out,
    conv_x,
    conv_bc,
    dt_bias,
    a_log,
    d_skip,
    norm_gain,
):
    input_rows = act_in[0]
    saved_rows = saved_act[0]
    cot_rows = cotangent[0]
    local_xz = weight_xz[0]
    local_bcdt = weight_bcdt[0]
    local_out = weight_out[0]
    taps_x = conv_x[0]
    taps_bc = conv_bc[0]
    dt_offset = dt_bias[0]
    log_rate = a_log[0]
    skip_gain = d_skip[0]
    gain_local = norm_gain[0]
    own_heads = dt_offset.shape[0]
    me = lax.axis_index("dp")
    head_first = me * own_heads
    width = own_heads * HEAD_DIM

    def whole_act(pre_part):
        return jax.nn.silu(causal_conv(pre_part, taps_bc))

    def project(rows):
        values = rows.astype(jnp.float32)
        squares = jnp.sum(values * values, axis=1, keepdims=True)

        def part(j):
            cols = lax.dynamic_slice_in_dim(local_xz, (me ^ j) * 2 * width, 2 * width, 1)
            return jnp.dot(rows, cols, preferred_element_type=jnp.float32)

        raw_xz = sum_scatter(part)
        small = sum_all(jnp.concatenate([times_transposed(rows, local_bcdt), squares], axis=1))
        raw_cols = small[:, : MAPS + HEADS]
        scales = lax.rsqrt(small[:, MAPS + HEADS :] / D + 1e-05)
        return (values, scales, raw_xz, raw_cols)

    def gate_parts(projected):
        values, scales, raw_xz, raw_cols = projected
        own_xz = raw_xz * scales
        whole_cols = raw_cols * scales
        pre_part = whole_cols[:, :MAPS]
        maps = whole_act(pre_part).astype(jnp.bfloat16)
        own_dt = lax.dynamic_slice_in_dim(whole_cols[:, MAPS:], head_first, own_heads, 1)
        split_xz = own_xz.reshape(SEQ, own_heads, 2, HEAD_DIM)
        mix_x = split_xz[:, :, 0].reshape(SEQ, width)
        mix_z = split_xz[:, :, 1].reshape(SEQ, width)
        scores = times_transposed(maps[:, NSTATE:], maps[:, :NSTATE])

        def local_mix(in_x, in_z, in_dt, in_scores):
            return mixer(in_x, in_z, in_dt, in_scores, taps_x, dt_offset, log_rate, skip_gain)

        gated, mix_back = jax.vjp(local_mix, mix_x, mix_z, own_dt, scores)
        return (gated, mix_back, maps, pre_part)

    back_proj = project(saved_rows)

    def mixed_part(j):
        taken = lax.dynamic_slice_in_dim(local_out, (me ^ j) * width, width, 0)
        return times_transposed(cot_rows, taken)

    d_mixed = sum_scatter(mixed_part)
    forward_proj = project(input_rows)

    values, scales, raw_xz, raw_cols = back_proj
    gated, mix_back, maps, pre_part = gate_parts(back_proj)
    gained = gated * gain_local
    row_sums = sum_all(
        jnp.stack([jnp.sum(gated * gated, axis=1), jnp.sum(d_mixed * gained, axis=1)])
    )
    inverse = lax.rsqrt(row_sums[0] / INNER + 1e-05)[:, None]
    dots = row_sums[1][:, None]
    mixed_in = (gained * inverse).astype(jnp.bfloat16)
    d_gated = inverse * gain_local * d_mixed - gated * (inverse * inverse * inverse) * dots / INNER
    d_px, d_pz, d_pdt, d_scores = mix_back(d_gated)
    own_round = (
        jnp.stack(
            [
                d_px.reshape(SEQ, own_heads, HEAD_DIM),
                d_pz.reshape(SEQ, own_heads, HEAD_DIM),
            ],
            axis=2,
        )
        .reshape(SEQ, own_heads * 2 * HEAD_DIM)
        .astype(jnp.bfloat16)
    )
    round_xz = gather_cols(own_round)
    inner_own = jnp.sum(own_round.astype(jnp.float32) * raw_xz, axis=1, keepdims=True)
    wide_maps = maps.astype(jnp.float32)
    d_maps = jnp.concatenate(
        [
            jnp.dot(d_scores.T, wide_maps[:, NSTATE:], precision=lax.Precision.HIGH),
            jnp.dot(d_scores, wide_maps[:, :NSTATE], precision=lax.Precision.HIGH),
        ],
        axis=1,
    )
    d_dt_full = lax.dynamic_update_slice_in_dim(
        jnp.zeros((SEQ, HEADS), jnp.float32), d_pdt, head_first, 1
    )
    summed = sum_all(jnp.concatenate([d_maps, d_dt_full, inner_own], axis=1))
    conv_out, conv_back = jax.vjp(whole_act, pre_part)
    d_pre = conv_back(summed[:, :MAPS])[0]
    round_bcdt = jnp.concatenate([d_pre, summed[:, MAPS : MAPS + HEADS]], axis=1).astype(
        jnp.bfloat16
    )
    inner_sum = summed[:, MAPS + HEADS :] + jnp.sum(
        round_bcdt.astype(jnp.float32) * raw_cols, axis=1, keepdims=True
    )

    fwd_gated = gate_parts(forward_proj)[0]
    fwd_all = gather_cols((fwd_gated * gain_local).astype(jnp.bfloat16))
    fwd_sum = sum_all(jnp.sum(fwd_gated * fwd_gated, axis=1)[None])
    fwd_inverse = lax.rsqrt(fwd_sum[0] / INNER + 1e-05)[:, None]
    mixed = jnp.dot(fwd_all, local_out, preferred_element_type=jnp.float32) * fwd_inverse
    section_out = (input_rows.astype(jnp.float32) + mixed).astype(jnp.bfloat16)
    next_act = from_behind(section_out, "section", 1)

    normed = (values * scales).astype(jnp.bfloat16)
    d_normed = times_transposed(round_xz, local_xz)
    d_normed = d_normed + jnp.dot(round_bcdt, local_bcdt, preferred_element_type=jnp.float32)
    d_norm_in = scales * d_normed - values * (scales * scales * scales) * inner_sum / D
    d_input = (cot_rows.astype(jnp.float32) + d_norm_in).astype(jnp.bfloat16)
    prev_grad = from_behind(d_input, "section", -1)

    grad_out = transposed_times(gather_cols(mixed_in), cot_rows)
    grad_xz = transposed_times(normed, round_xz)
    grad_bcdt = transposed_times(round_bcdt, normed)
    return (next_act[None], prev_grad[None], grad_xz[None], grad_bcdt[None], grad_out[None])


def solution(mesh):
    return jax.shard_map(
        per_device,
        mesh=mesh,
        in_specs=(
            P("section", None, "dp"),
            P("section", None, "dp"),
            P("section", None, "dp"),
            P("section", "dp", None),
            P("section", None, "dp"),
            P("section", None, "dp"),
            P("section", None, "dp"),
            P("section", None, None),
            P("section", "dp"),
            P("section", "dp"),
            P("section", "dp"),
            P("section", "dp"),
        ),
        out_specs=(
            P("section", None, "dp"),
            P("section", None, "dp"),
            P("section", "dp", None),
            P("section", None, "dp"),
            P("section", None, "dp"),
        ),
        check_vma=False,
    )
```

time: 312 us -> 143 us (0.46)
  waiting for transfers between devices: 178 us -> 51.7 us
  blocking collectives: 20.4 us -> 0 us
  starting transfers between devices: 6.58 us -> 23.3 us
  between operations: 14.7 us -> 1.29 us
  local copies, waits for them, and re-layouts: 12.5 us -> 1.56 us
  matrix products: 61.8 us -> 54.2 us
  other arithmetic: 17.4 us -> 10.2 us
    reduce_scatter x3 -> x0, waiting for transfers between devices: 102 us -> none  [the longest x2 74.9 us: project(): own_xz = lax.psum_scatter(part_xz, 'dp', scatter_dimension=1, tiled=True)]
    ppermute x0 -> x28, waiting for transfers between devices: none -> 50.5 us  [swap(): return lax.ppermute(x, 'dp', [(i, i ^ mask) for i in range(length)])]
    psum x2 -> x0, waiting for transfers between devices: 47.7 us -> none  [project(): whole_cols = lax.psum(part_bcdt, 'dp')]
    all_gather x3 -> x0, waiting for transfers between devices: 26.9 us -> none  [the longest x1 15.6 us: per_device(): round_xz = lax.all_gather(own_round, 'dp', axis=1, tiled=True)]
    psum x3 -> x0, blocking collectives: 20.4 us -> none  [the longest x2 14.1 us: feature_sum(): return lax.psum(jnp.sum(values, axis=1), 'dp')]
    ppermute x0 -> x28, starting transfers between devices: none -> 19 us  [swap(): return lax.ppermute(x, 'dp', [(i, i ^ mask) for i in range(length)])]
    dot_general x4 -> x9, matrix products: 15.5 us -> 10.9 us  [times_transposed(): lax.dot_general(left, right, (((1,), (1,)), ((), ())), preferred_element_...]
    convert_element_type x4 -> x2, other arithmetic: 4.82 us -> 0.72 us  [the longest x1 0.42 us: gate_parts(): maps = whole_act(pre_part).astype(jnp.bfloat16)]
  transfers between devices with their start and end apart: 10 -> 30, of which waited for: 8 -> 11; matrix products, arithmetic and copies ran while one was open for 25% -> 41% of each run, Pallas kernels for 0% -> 0%
where the time goes in v1:
time: 143 us; the launch traced here: 142 us
  matrix products  54.2 us (38%)
  waiting for transfers between devices  51.7 us (36%)
  starting transfers between devices  23.3 us (16%)
  other arithmetic  10.2 us (7%)
  local copies, waits for them, and re-layouts  1.56 us (1%)
    ppermute x28, waiting for transfers between devices, swap(): return lax.ppermute(x, 'dp', [(i, i ^ mask) for i in range(length)])  50.5 us
    dot_general x8, matrix products, part(): return jnp.dot(rows, cols, preferred_element_type=jnp.float32)  21.4 us
    ppermute x28, starting transfers between devices, swap(): return lax.ppermute(x, 'dp', [(i, i ^ mask) for i in range(length)])  19 us
    dot_general x3, matrix products, transposed_times(): lax.dot_general(left, right, (((0,), (0,)), ((), ())), preferred_element_...  15.1 us
    dot_general x9, matrix products, times_transposed(): lax.dot_general(left, right, (((1,), (1,)), ((), ())), preferred_element_...  10.9 us
    dot_general x4, matrix products, mixer(): jnp.einsum('hts,shp->thp', weights, heads_in, precision=lax.Precision.HIGH)  5.05 us
    ppermute x2, starting transfers between devices, from_behind(): lax.ppermute(x, axis, [(i, (i + by) % length) for i in range(length)])  4.28 us
  transfers between devices with their start and end apart: 30, of which 11 were waited for; matrix products, arithmetic and copies ran while one was open for 41% of the time, Pallas kernels for 0%

profile of v1, /device:TPU:0, one launch (start us, length us, event | category | flops | bytes accessed | tf_op | source)
XLA Modules:
  0.0 142.3 jit_solution(11219333034733726009)
XLA Ops:
  4.0 3.2 %fusion.7 = bf16[128,2048]{0,1:T(8,128)(2,1)} fusion(bf16[1,512,8192]{2,1,0:T(8,128)(2,1)} %param.15, s32[]{:T(128)S(6)} %select_n.183, bf16[1,128,512]{2,1,0:T(8,128)(2,1)} %param.13), kind=kOutput, calls=%fused_computation.17 | convolution fusion | flops 268697600 | bytes 2752516 | tf_op jit(solution)/shard_map/dot_general | solution.py:161
  7.2 2.4 %fusion.6 = bf16[128,2048]{0,1:T(8,128)(2,1)S(1)} fusion(bf16[1,512,8192]{2,1,0:T(8,128)(2,1)} %param.15, s32[]{:T(128)S(6)} %select_n.181, bf16[1,128,512]{2,1,0:T(8,128)(2,1)} %param.13), kind=kOutput, calls=%fused_computation.16 | convolution fusion | flops 268697600 | bytes 2752516 | tf_op jit(solution)/shard_map/dot_general | solution.py:161
  10.1 3.1 %fusion.5 = bf16[128,2048]{0,1:T(8,128)(2,1)} fusion(bf16[1,512,8192]{2,1,0:T(8,128)(2,1)} %param.15, s32[]{:T(128)S(6)} %select_n.183, bf16[1,128,512]{2,1,0:T(8,128)(2,1)S(1)} %copy-done.2), kind=kOutput, calls=%fused_computation.15 | convolution fusion | flops 268697600 | bytes 2752516 | tf_op jit(solution)/shard_map/dot_general | solution.py:161
  14.8 3.2 %fusion.4 = bf16[128,2048]{0,1:T(8,128)(2,1)} fusion(bf16[1,512,8192]{2,1,0:T(8,128)(2,1)} %param.15, s32[]{:T(128)S(6)} %select_n.181, bf16[1,128,512]{2,1,0:T(8,128)(2,1)S(1)} %copy-done.2), kind=kOutput, calls=%fused_computation.14 | convolution fusion | flops 268697600 | bytes 2752516 | tf_op jit(solution)/shard_map/dot_general | solution.py:161
  18.0 2.3 %convolution_bitcast_fusion.5 = f32[128,2048]{0,1:T(8,128)S(1)} fusion(bf16[1,512,8192]{2,1,0:T(8,128)(2,1)} %param.15, s32[]{:T(128)S(6)} %select_n.180, bf16[1,128,512]{2,1,0:T(8,128)(2,1)S(1)} %copy-done.2), kind=kOutput, calls=%fused_computation.9 | convolution fusion | flops 268435456 | bytes 3276804 | tf_op jit(solution)/shard_map/dot_general | solution.py:161
  20.4 2.4 %fusion.29 = bf16[128,1024]{0,1:T(8,128)(2,1)} fusion(bf16[1,4096,512]{2,1,0:T(8,128)(2,1)} %param.17, s32[]{:T(128)S(6)} %select_n.204, bf16[1,128,512]{2,1,0:T(8,128)(2,1)S(1)} %copy-done.4), kind=kOutput, calls=%fused_computation.54 | convolution fusion | flops 134348800 | bytes 1441796 | tf_op jit(solution)/shard_map/dot_general | solution.py:110
  22.8 1.7 %fusion.28 = bf16[128,1024]{0,1:T(8,128)(2,1)S(1)} fusion(bf16[1,4096,512]{2,1,0:T(8,128)(2,1)} %param.17, s32[]{:T(128)S(6)} %select_n.202, bf16[1,128,512]{2,1,0:T(8,128)(2,1)S(1)} %copy-done.4), kind=kOutput, calls=%fused_computation.53 | convolution fusion | flops 134348800 | bytes 1441796 | tf_op jit(solution)/shard_map/dot_general | solution.py:110
  27.1 2.6 %collective-permute-start.12 = (f32[128,321]{0,1:T(8,128)S(1)}, f32[128,321]{0,1:T(8,128)S(1)}, u32[]{:S(2)}, u32[]{:S(2)}) collective-permute-start(f32[128,321]{0,1:T(8,128)S(1)} %fusion.248), channel_id=1, source_target_pairs={{0,2},{1,3},{2,0},{3,1},{4,6},{5,7},{6,4},{7,5},{8,10},{9,11},{10,... | collective-permute-start | bytes 493064 | tf_op jit(solution)/shard_map/ppermute | solution.py:22
  29.7 1.6 %add_convert_fusion.2 = bf16[128,1024]{0,1:T(8,128)(2,1)S(1)} fusion(bf16[128,1024]{0,1:T(8,128)(2,1)S(1)} %collective-permute-done.17, bf16[1,128,512]{2,1,0:T(8,128)(2,1)S(1)} %copy-done.4, bf16[1,4096,512]{2,1,0:T(8,128)(2,1)} %param.17, s32[]{:T(128)S(6)} %select_n.203), kind=kOutput, calls=%fused_computation.150 | convolution fusion | flops 134610944 | bytes 1703940 | tf_op jit(solution)/shard_map/dot_general | solution.py:110
  31.3 3.3 %collective-permute-done.12 = f32[128,321]{0,1:T(8,128)S(1)} collective-permute-done((f32[128,321]{0,1:T(8,128)S(1)}, f32[128,321]{0,1:T(8,128)S(1)}, u32[]{:S(2)}, u32[]{:S(2)}) %collective-permute-start.12) | collective-permute-done | bytes 164384 | tf_op jit(solution)/shard_map/ppermute | solution.py:22
  34.6 1.7 %collective-permute-start.4 = (f32[128,321]{0,1:T(8,128)S(1)}, f32[128,321]{0,1:T(8,128)S(1)}, u32[]{:S(2)}, u32[]{:S(2)}) collective-permute-start(f32[128,321]{0,1:T(8,128)S(1)} %fusion.249), channel_id=1, source_target_pairs={{0,2},{1,3},{2,0},{3,1},{4,6},{5,7},{6,4},{7,5},{8,10},{9,11},{10,... | collective-permute-start | bytes 493064 | tf_op jit(solution)/shard_map/ppermute | solution.py:22
  36.4 4.3 %collective-permute-done.4 = f32[128,321]{0,1:T(8,128)S(1)} collective-permute-done((f32[128,321]{0,1:T(8,128)S(1)}, f32[128,321]{0,1:T(8,128)S(1)}, u32[]{:S(2)}, u32[]{:S(2)}) %collective-permute-start.4) | collective-permute-done | bytes 164384 | tf_op jit(solution)/shard_map/ppermute | solution.py:22
  41.7 2.4 %add_convert_fusion = bf16[128,2048]{0,1:T(8,128)(2,1)S(1)} fusion(bf16[128,2048]{0,1:T(8,128)(2,1)} %collective-permute-done.14, bf16[1,128,512]{2,1,0:T(8,128)(2,1)S(1)} %copy-done.1, bf16[1,512,8192]{2,1,0:T(8,128)(2,1)} %param.15, s32[]{:T(128)S(6)} %select_n.182), kind=kOutput, calls=%fused_computation.98 | convolution fusion | flops 269221888 | bytes 3276804 | tf_op jit(solution)/shard_map/dot_general | solution.py:161
  44.2 1.6 %collective-permute-start.15 = (bf16[128,2048]{0,1:T(8,128)(2,1)S(1)}, bf16[128,2048]{0,1:T(8,128)(2,1)S(1)}, u32[]{:S(2)}, u32[]{:S(2)}) collective-permute-start(bf16[128,2048]{0,1:T(8,128)(2,1)S(1)} %add_convert_fusion), channel_id=1, source_target_pairs={{0,2},{1,3},{2,0},{3,1},{4,6},{5,7},{6,4},{7,5},{8,10},{9,11},{10,... | collective-permute-start | bytes 1572872 | tf_op jit(solution)/shard_map/ppermute | solution.py:22
  45.9 2.4 %add_convert_fusion.1 = bf16[128,2048]{0,1:T(8,128)(2,1)S(1)} fusion(bf16[128,2048]{0,1:T(8,128)(2,1)} %collective-permute-done.1, bf16[1,128,512]{2,1,0:T(8,128)(2,1)S(1)} %copy-done.2, bf16[1,512,8192]{2,1,0:T(8,128)(2,1)} %param.15, s32[]{:T(128)S(6)} %select_n.182), kind=kOutput, calls=%fused_computation.106 | convolution fusion | flops 269221888 | bytes 3276804 | tf_op jit(solution)/shard_map/dot_general | solution.py:161
  50.6 8.3 %collective-permute-done.15 = bf16[128,2048]{0,1:T(8,128)(2,1)S(1)} collective-permute-done((bf16[128,2048]{0,1:T(8,128)(2,1)S(1)}, bf16[128,2048]{0,1:T(8,128)(2,1)S(1)}, u32[]{:S(2)}, u32[]{:S(2)}) %collective-permute-start.15) | collective-permute-done | bytes 524320 | tf_op jit(solution)/shard_map/ppermute | solution.py:22
  58.9 2.3 %broadcast_multiply_fusion = (f32[128,2048]{0,1:T(8,128)S(1)}, f32[128,2048]{0,1:T(8,128)S(1)}) fusion(f32[128]{0:T(128)S(1)} %get-tuple-element.39, bf16[128,2048]{0,1:T(8,128)(2,1)S(1)} %collective-permute-done.15, bf16[128,2048]{0,1:T(8,128)(2,1)S(1)} %collective-permute-done.13, bf16[1,128,512]{2,1,0:T(8,128)(2,1)S(1)} %copy-done.1, ...), kind=kOutput, calls=%fused_computation.164 | convolution fusion | flops 269746176 | bytes 5374468 | tf_op jit(solution)/shard_map/dot_general | solution.py:161
  61.3 8.8 %collective-permute-done.2 = bf16[128,2048]{0,1:T(8,128)(2,1)S(1)} collective-permute-done((bf16[128,2048]{0,1:T(8,128)(2,1)S(1)}, bf16[128,2048]{0,1:T(8,128)(2,1)S(1)}, u32[]{:S(2)}, u32[]{:S(2)}) %collective-permute-start.2) | collective-permute-done | bytes 524320 | tf_op jit(solution)/shard_map/ppermute | solution.py:22
  70.5 1.8 %fusion.126 = (f32[128,1024]{0,1:T(8,128)S(1)}, f32[128,1024]{0,1:T(8,128)S(1)}, f32[128,1024]{0,1:T(8,128)S(1)}) fusion(f32[128,1024]{0,1:T(8,128)S(1)} %bitcast.314, f32[1024]{0:T(1024)S(1)} %bitcast.328, f32[1024]{0:T(1024)S(1)} %bitcast.326, f32[1024]{0:T(1024)S(1)} %bitcast.324, f32[1024]{0:T(1024)S(1)} %bitcast.322, f32[128,1024]{0,1:T(8,128)S(1)} %bitcast.315), kind=kLoop, calls=%fused_computation.163 | loop fusion | flops 2883584 | bytes 2637824 | tf_op jit(solution)/shard_map/jvp(jit(silu))/mul | solution.py:91
  73.4 2.0 %collective-permute-done.18 = bf16[128,1024]{0,1:T(8,128)(2,1)S(1)} collective-permute-done((bf16[128,1024]{0,1:T(8,128)(2,1)S(1)}, bf16[128,1024]{0,1:T(8,128)(2,1)S(1)}, u32[]{:S(2)}, u32[]{:S(2)}) %collective-permute-start.18) | collective-permute-done | bytes 262176 | tf_op jit(solution)/shard_map/ppermute | solution.py:22
  77.1 1.6 %collective-permute-start.20 = (f32[2,128]{1,0:T(2,128)S(1)}, f32[2,128]{1,0:T(2,128)S(1)}, u32[]{:S(2)}, u32[]{:S(2)}) collective-permute-start(f32[2,128]{1,0:T(2,128)S(1)} %fusion.246), channel_id=1, source_target_pairs={{0,2},{1,3},{2,0},{3,1},{4,6},{5,7},{6,4},{7,5},{8,10},{9,11},{10,... | collective-permute-start | bytes 3080 | tf_op jit(solution)/shard_map/ppermute | solution.py:22
  82.0 1.8 %fusion.91 = (f32[16,128]{1,0:T(8,128)S(1)}, f32[16,128]{1,0:T(8,128)S(1)}, f32[16,128]{1,0:T(8,128)S(1)}, f32[128,128]{1,0:T(8,128)S(1)}) fusion(f32[16,128]{1,0:T(8,128)S(1)} %get-tuple-element.54, f32[128,128]{1,0:T(8,128)S(1)} %fusion.202, f32[16,128]{1,0:T(8,128)S(1)} %fusion.195, pred[128,128]{1,0:T(8,128)(4,1)S(1)} %iota_compare_fusion, ...), kind=kOutput, calls=%fused_computation.110 | convolution fusion | flops 105228288 | bytes 1769472 | tf_op jit(solution)/shard_map/transpose(jvp(hts,shp->thp))/dot_general | solution.py:103
  86.3 1.6 %collective-permute-start.9 = (f32[1,128]{1,0:T(1,128)S(1)}, f32[1,128]{1,0:T(1,128)S(1)}, u32[]{:S(2)}, u32[]{:S(2)}) collective-permute-start(f32[1,128]{1,0:T(1,128)S(1)} %bitcast_add_fusion), channel_id=1, source_target_pairs={{0,2},{1,3},{2,0},{3,1},{4,6},{5,7},{6,4},{7,5},{8,10},{9,11},{10,... | collective-permute-start | bytes 1544 | tf_op jit(solution)/shard_map/ppermute | solution.py:22
  88.5 1.6 %collective-permute-start.25 = (f32[128,321]{0,1:T(8,128)S(1)}, f32[128,321]{0,1:T(8,128)S(1)}, u32[]{:S(2)}, u32[]{:S(2)}) collective-permute-start(f32[128,321]{0,1:T(8,128)S(1)} %fusion.250), channel_id=1, source_target_pairs={{0,2},{1,3},{2,0},{3,1},{4,6},{5,7},{6,4},{7,5},{8,10},{9,11},{10,... | collective-permute-start | bytes 493064 | tf_op jit(solution)/shard_map/ppermute | solution.py:22
  91.7 5.4 %collective-permute-done.5 = bf16[128,1024]{0,1:T(8,128)(2,1)S(1)} collective-permute-done((bf16[128,1024]{0,1:T(8,128)(2,1)S(1)}, bf16[128,1024]{0,1:T(8,128)(2,1)S(1)}, u32[]{:S(2)}, u32[]{:S(2)}) %collective-permute-start.5) | collective-permute-done | bytes 262176 | tf_op jit(solution)/shard_map/ppermute | solution.py:22
  97.6 3.1 %collective-permute-done.25 = f32[128,321]{0,1:T(8,128)S(1)} collective-permute-done((f32[128,321]{0,1:T(8,128)S(1)}, f32[128,321]{0,1:T(8,128)S(1)}, u32[]{:S(2)}, u32[]{:S(2)}) %collective-permute-start.25) | collective-permute-done | bytes 164384 | tf_op jit(solution)/shard_map/ppermute | solution.py:22
  103.2 13.5 %collective-permute-done.27 = bf16[128,1024]{0,1:T(8,128)(2,1)S(1)} collective-permute-done((bf16[128,1024]{0,1:T(8,128)(2,1)S(1)}, bf16[128,1024]{0,1:T(8,128)(2,1)S(1)}, u32[]{:S(2)}, u32[]{:S(2)}) %collective-permute-start.27) | collective-permute-done | bytes 262176 | tf_op jit(solution)/shard_map/ppermute | solution.py:22
  118.1 1.8 %collective-permute-start.10 = (bf16[128,512]{1,0:T(8,128)(2,1)S(1)}, bf16[128,512]{1,0:T(8,128)(2,1)S(1)}, u32[]{:S(2)}, u32[]{:S(2)}) collective-permute-start(bf16[128,512]{1,0:T(8,128)(2,1)S(1)} %fusion.51), channel_id=1, source_target_pairs={{0,4},{4,8},{8,12},{12,16},{16,20},{20,24},{24,28},{28,0},{1,5},{5... | collective-permute-start | bytes 393224 | tf_op jit(solution)/shard_map/ppermute | solution.py:17
  120.0 5.3 %convolution_bitcast_fusion.1 = f32[1,4096,512]{2,1,0:T(8,128)} fusion(bf16[128,1024]{0,1:T(8,128)(2,1)S(1)} %get-tuple-element.28, bf16[128,1024]{0,1:T(8,128)(2,1)S(1)} %get-tuple-element.27, bf16[128,1024]{0,1:T(8,128)(2,1)S(1)} %get-tuple-element.26, bf16[128,1024]{0,1:T(8,128)(2,1)S(1)} %get-tuple-element.25, bf16[1,128,512]{2,1,0:T(8,128)(2,1)S(1)} %copy-done.4), kind=kOutput, calls=%fused_computation.3 | convolution fusion | flops 541065216 | bytes 9568256 | tf_op jit(solution)/shard_map/dot_general | solution.py:116
  126.9 2.9 %fusion.48 = bf16[128,512]{1,0:T(8,128)(2,1)S(1)} fusion(f32[128,512]{1,0:T(8,128)S(1)} %fusion.137, bf16[1,512,8192]{2,1,0:T(8,128)(2,1)S(1)} %bitcast.302, bf16[128,2048]{0,1:T(8,128)(2,1)S(1)} %get-tuple-element.24, bf16[128,2048]{0,1:T(8,128)(2,1)S(1)} %get-tuple-element.23, bf16[128,2048]{0,1:T(8,128)(2,1)S(1)} %get-tuple-element.22, ...), kind=kOutput, calls=%fused_computation.61 | convolution fusion | flops 1082785792 | bytes 11142656 | tf_op jit(solution)/shard_map/dot_general | solution.py:110
  129.8 2.5 %collective-permute-start.26 = (bf16[128,512]{1,0:T(8,128)(2,1)S(1)}, bf16[128,512]{1,0:T(8,128)(2,1)S(1)}, u32[]{:S(2)}, u32[]{:S(2)}) collective-permute-start(bf16[128,512]{1,0:T(8,128)(2,1)S(1)} %fusion.48), channel_id=1, source_target_pairs={{0,28},{4,0},{8,4},{12,8},{16,12},{20,16},{24,20},{28,24},{1,29},{... | collective-permute-start | bytes 393224 | tf_op jit(solution)/shard_map/ppermute | solution.py:17
  132.3 8.6 %convolution_bitcast_fusion = f32[1,512,8192]{2,1,0:T(8,128)} fusion(bf16[128,2048]{0,1:T(8,128)(2,1)S(1)} %get-tuple-element.24, bf16[128,2048]{0,1:T(8,128)(2,1)S(1)} %get-tuple-element.23, bf16[128,2048]{0,1:T(8,128)(2,1)S(1)} %get-tuple-element.22, bf16[128,2048]{0,1:T(8,128)(2,1)S(1)} %get-tuple-element.21, bf16[1,128,512]{2,1,0:T(8,128)(2,1)S(1)} %copy-done.1, ...), kind=kOutput, calls=%fused_computation | convolution fusion | flops 1082327040 | bytes 19005952 | tf_op jit(solution)/shard_map/dot_general | solution.py:116
  (142 shorter events, 29.7 us)
Async XLA Ops:
  3.6 21.0 %collective-permute-start.11 = (f32[128,321]{0,1:T(8,128)}, f32[128,321]{0,1:T(8,128)}, u32[]{:S(2)}, u32[]{:S(2)}) collective-permute-start(f32[128,321]{0,1:T(8,128)} %pad_maximum_fusion.5), channel_id=1, source_target_pairs={{0,1},{1,0},{2,3},{3,2},{4,5},{5,4},{6,7},{7,6},{8,9},{9,8},{10,11... | collective-permute-start | bytes 493064 | tf_op jit(solution)/shard_map/ppermute | solution.py:22
  7.2 34.5 %collective-permute-start.14 = (bf16[128,2048]{0,1:T(8,128)(2,1)}, bf16[128,2048]{0,1:T(8,128)(2,1)}, u32[]{:S(2)}, u32[]{:S(2)}) collective-permute-start(bf16[128,2048]{0,1:T(8,128)(2,1)} %fusion.7), channel_id=1, source_target_pairs={{0,1},{1,0},{2,3},{3,2},{4,5},{5,4},{6,7},{7,6},{8,9},{9,8},{10,11... | collective-permute-start | bytes 1572872 | tf_op jit(solution)/shard_map/ppermute | solution.py:22
  9.6 39.5 %collective-permute-start.13 = (bf16[128,2048]{0,1:T(8,128)(2,1)S(1)}, bf16[128,2048]{0,1:T(8,128)(2,1)S(1)}, u32[]{:S(2)}, u32[]{:S(2)}) collective-permute-start(bf16[128,2048]{0,1:T(8,128)(2,1)S(1)} %fusion.6), channel_id=1, source_target_pairs={{0,1},{1,0},{2,3},{3,2},{4,5},{5,4},{6,7},{7,6},{8,9},{9,8},{10,11... | collective-permute-start | bytes 1572872 | tf_op jit(solution)/shard_map/ppermute | solution.py:22
  13.3 32.6 %collective-permute-start.1 = (bf16[128,2048]{0,1:T(8,128)(2,1)}, bf16[128,2048]{0,1:T(8,128)(2,1)}, u32[]{:S(2)}, u32[]{:S(2)}) collective-permute-start(bf16[128,2048]{0,1:T(8,128)(2,1)} %fusion.5), channel_id=1, source_target_pairs={{0,1},{1,0},{2,3},{3,2},{4,5},{5,4},{6,7},{7,6},{8,9},{9,8},{10,11... | collective-permute-start | bytes 1572872 | tf_op jit(solution)/shard_map/ppermute | solution.py:22
  14.4 11.2 %collective-permute-start.3 = (f32[128,321]{0,1:T(8,128)}, f32[128,321]{0,1:T(8,128)}, u32[]{:S(2)}, u32[]{:S(2)}) collective-permute-start(f32[128,321]{0,1:T(8,128)} %pad_maximum_fusion.4), channel_id=1, source_target_pairs={{0,1},{1,0},{2,3},{3,2},{4,5},{5,4},{6,7},{7,6},{8,9},{9,8},{10,11... | collective-permute-start | bytes 493064 | tf_op jit(solution)/shard_map/ppermute | solution.py:22
  20.4 21.3 %copy-start.1 = (bf16[1,128,512]{2,1,0:T(8,128)(2,1)S(1)}, bf16[1,128,512]{2,1,0:T(8,128)(2,1)}, u32[]{:S(2)}) copy-start(bf16[1,128,512]{2,1,0:T(8,128)(2,1)} %param.13) | copy-start | bytes 393220
  24.6 2.5 %collective-permute-start.17 = (bf16[128,1024]{0,1:T(8,128)(2,1)}, bf16[128,1024]{0,1:T(8,128)(2,1)S(1)}, u32[]{:S(2)}, u32[]{:S(2)}) collective-permute-start(bf16[128,1024]{0,1:T(8,128)(2,1)} %fusion.29), channel_id=1, source_target_pairs={{0,1},{1,0},{2,3},{3,2},{4,5},{5,4},{6,7},{7,6},{8,9},{9,8},{10,11... | collective-permute-start | bytes 786440 | tf_op jit(solution)/shard_map/ppermute | solution.py:22
  25.6 20.2 %copy-start.8 = (f32[1,16]{1,0:T(1,128)S(1)}, f32[1,16]{1,0:T(1,128)}, u32[]{:S(2)}) copy-start(f32[1,16]{1,0:T(1,128)} %param.20) | copy-start | bytes 196
  25.6 35.7 %collective-permute-start = (bf16[128,2048]{0,1:T(8,128)(2,1)}, bf16[128,2048]{0,1:T(8,128)(2,1)S(1)}, u32[]{:S(2)}, u32[]{:S(2)}) collective-permute-start(bf16[128,2048]{0,1:T(8,128)(2,1)} %fusion.4), channel_id=1, source_target_pairs={{0,1},{1,0},{2,3},{3,2},{4,5},{5,4},{6,7},{7,6},{8,9},{9,8},{10,11... | collective-permute-start | bytes 1572872 | tf_op jit(solution)/shard_map/ppermute | solution.py:22
  27.1 7.5 %collective-permute-start.12 = (f32[128,321]{0,1:T(8,128)S(1)}, f32[128,321]{0,1:T(8,128)S(1)}, u32[]{:S(2)}, u32[]{:S(2)}) collective-permute-start(f32[128,321]{0,1:T(8,128)S(1)} %fusion.248), channel_id=1, source_target_pairs={{0,2},{1,3},{2,0},{3,1},{4,6},{5,7},{6,4},{7,5},{8,10},{9,11},{10,... | collective-permute-start | bytes 493064 | tf_op jit(solution)/shard_map/ppermute | solution.py:22
  34.6 6.1 %collective-permute-start.4 = (f32[128,321]{0,1:T(8,128)S(1)}, f32[128,321]{0,1:T(8,128)S(1)}, u32[]{:S(2)}, u32[]{:S(2)}) collective-permute-start(f32[128,321]{0,1:T(8,128)S(1)} %fusion.249), channel_id=1, source_target_pairs={{0,2},{1,3},{2,0},{3,1},{4,6},{5,7},{6,4},{7,5},{8,10},{9,11},{10,... | collective-permute-start | bytes 493064 | tf_op jit(solution)/shard_map/ppermute | solution.py:22
  40.7 32.7 %collective-permute-start.16 = (bf16[128,1024]{0,1:T(8,128)(2,1)S(1)}, bf16[128,1024]{0,1:T(8,128)(2,1)S(1)}, u32[]{:S(2)}, u32[]{:S(2)}) collective-permute-start(bf16[128,1024]{0,1:T(8,128)(2,1)S(1)} %fusion.28), channel_id=1, source_target_pairs={{0,1},{1,0},{2,3},{3,2},{4,5},{5,4},{6,7},{7,6},{8,9},{9,8},{10,11... | collective-permute-start | bytes 786440 | tf_op jit(solution)/shard_map/ppermute | solution.py:22
  44.2 14.8 %collective-permute-start.15 = (bf16[128,2048]{0,1:T(8,128)(2,1)S(1)}, bf16[128,2048]{0,1:T(8,128)(2,1)S(1)}, u32[]{:S(2)}, u32[]{:S(2)}) collective-permute-start(bf16[128,2048]{0,1:T(8,128)(2,1)S(1)} %add_convert_fusion), channel_id=1, source_target_pairs={{0,2},{1,3},{2,0},{3,1},{4,6},{5,7},{6,4},{7,5},{8,10},{9,11},{10,... | collective-permute-start | bytes 1572872 | tf_op jit(solution)/shard_map/ppermute | solution.py:22
  48.3 21.9 %collective-permute-start.2 = (bf16[128,2048]{0,1:T(8,128)(2,1)S(1)}, bf16[128,2048]{0,1:T(8,128)(2,1)S(1)}, u32[]{:S(2)}, u32[]{:S(2)}) collective-permute-start(bf16[128,2048]{0,1:T(8,128)(2,1)S(1)} %add_convert_fusion.1), channel_id=1, source_target_pairs={{0,2},{1,3},{2,0},{3,1},{4,6},{5,7},{6,4},{7,5},{8,10},{9,11},{10,... | collective-permute-start | bytes 1572872 | tf_op jit(solution)/shard_map/ppermute | solution.py:22
  49.0 26.4 %collective-permute-start.18 = (bf16[128,1024]{0,1:T(8,128)(2,1)S(1)}, bf16[128,1024]{0,1:T(8,128)(2,1)S(1)}, u32[]{:S(2)}, u32[]{:S(2)}) collective-permute-start(bf16[128,1024]{0,1:T(8,128)(2,1)S(1)} %add_convert_fusion.2), channel_id=1, source_target_pairs={{0,2},{1,3},{2,0},{3,1},{4,6},{5,7},{6,4},{7,5},{8,10},{9,11},{10,... | collective-permute-start | bytes 786440 | tf_op jit(solution)/shard_map/ppermute | solution.py:22
  75.9 1.2 collective-permute-start.19
  77.1 3.6 %collective-permute-start.20 = (f32[2,128]{1,0:T(2,128)S(1)}, f32[2,128]{1,0:T(2,128)S(1)}, u32[]{:S(2)}, u32[]{:S(2)}) collective-permute-start(f32[2,128]{1,0:T(2,128)S(1)} %fusion.246), channel_id=1, source_target_pairs={{0,2},{1,3},{2,0},{3,1},{4,6},{5,7},{6,4},{7,5},{8,10},{9,11},{10,... | collective-permute-start | bytes 3080 | tf_op jit(solution)/shard_map/ppermute | solution.py:22
  79.9 6.4 %collective-permute-start.8 = (f32[1,128]{1,0:T(1,128)S(1)}, f32[1,128]{1,0:T(1,128)S(1)}, u32[]{:S(2)}, u32[]{:S(2)}) collective-permute-start(f32[1,128]{1,0:T(1,128)S(1)} %bitcast.359), channel_id=1, source_target_pairs={{0,1},{1,0},{2,3},{3,2},{4,5},{5,4},{6,7},{7,6},{8,9},{9,8},{10,11... | collective-permute-start | bytes 1544 | tf_op jit(solution)/shard_map/ppermute | solution.py:22
  86.2 2.2 %collective-permute-start.24 = (f32[128,321]{0,1:T(8,128)S(1)}, f32[128,321]{0,1:T(8,128)S(1)}, u32[]{:S(2)}, u32[]{:S(2)}) collective-permute-start(f32[128,321]{0,1:T(8,128)S(1)} %pad_maximum_fusion.6), channel_id=1, source_target_pairs={{0,1},{1,0},{2,3},{3,2},{4,5},{5,4},{6,7},{7,6},{8,9},{9,8},{10,11... | collective-permute-start | bytes 493064 | tf_op jit(solution)/shard_map/ppermute | solution.py:22
  86.3 3.7 %collective-permute-start.9 = (f32[1,128]{1,0:T(1,128)S(1)}, f32[1,128]{1,0:T(1,128)S(1)}, u32[]{:S(2)}, u32[]{:S(2)}) collective-permute-start(f32[1,128]{1,0:T(1,128)S(1)} %bitcast_add_fusion), channel_id=1, source_target_pairs={{0,2},{1,3},{2,0},{3,1},{4,6},{5,7},{6,4},{7,5},{8,10},{9,11},{10,... | collective-permute-start | bytes 1544 | tf_op jit(solution)/shard_map/ppermute | solution.py:22
  87.9 9.2 %collective-permute-start.5 = (bf16[128,1024]{0,1:T(8,128)(2,1)S(1)}, bf16[128,1024]{0,1:T(8,128)(2,1)S(1)}, u32[]{:S(2)}, u32[]{:S(2)}) collective-permute-start(bf16[128,1024]{0,1:T(8,128)(2,1)S(1)} %get-tuple-element.48), channel_id=1, source_target_pairs={{0,2},{1,3},{2,0},{3,1},{4,6},{5,7},{6,4},{7,5},{8,10},{9,11},{10,... | collective-permute-start | bytes 786440 | tf_op jit(solution)/shard_map/ppermute | solution.py:22
  88.5 12.2 %collective-permute-start.25 = (f32[128,321]{0,1:T(8,128)S(1)}, f32[128,321]{0,1:T(8,128)S(1)}, u32[]{:S(2)}, u32[]{:S(2)}) collective-permute-start(f32[128,321]{0,1:T(8,128)S(1)} %fusion.250), channel_id=1, source_target_pairs={{0,2},{1,3},{2,0},{3,1},{4,6},{5,7},{6,4},{7,5},{8,10},{9,11},{10,... | collective-permute-start | bytes 493064 | tf_op jit(solution)/shard_map/ppermute | solution.py:22
  90.1 12.6 %collective-permute-start.7 = (bf16[128,1024]{0,1:T(8,128)(2,1)S(1)}, bf16[128,1024]{0,1:T(8,128)(2,1)S(1)}, u32[]{:S(2)}, u32[]{:S(2)}) collective-permute-start(bf16[128,1024]{0,1:T(8,128)(2,1)S(1)} %get-tuple-element.48), channel_id=1, source_target_pairs={{0,1},{1,0},{2,3},{3,2},{4,5},{5,4},{6,7},{7,6},{8,9},{9,8},{10,11... | collective-permute-start | bytes 786440 | tf_op jit(solution)/shard_map/ppermute | solution.py:22
  90.2 26.6 %collective-permute-start.21 = (bf16[128,2048]{0,1:T(8,128)(2,1)S(1)}, bf16[128,2048]{0,1:T(8,128)(2,1)S(1)}, u32[]{:S(2)}, u32[]{:S(2)}) collective-permute-start(bf16[128,2048]{0,1:T(8,128)(2,1)S(1)} %bitcast.303), channel_id=1, source_target_pairs={{0,2},{1,3},{2,0},{3,1},{4,6},{5,7},{6,4},{7,5},{8,10},{9,11},{10,... | collective-permute-start | bytes 1572872 | tf_op jit(solution)/shard_map/ppermute | solution.py:22
  91.6 35.1 %collective-permute-start.23 = (bf16[128,2048]{0,1:T(8,128)(2,1)S(1)}, bf16[128,2048]{0,1:T(8,128)(2,1)S(1)}, u32[]{:S(2)}, u32[]{:S(2)}) collective-permute-start(bf16[128,2048]{0,1:T(8,128)(2,1)S(1)} %bitcast.304), channel_id=1, source_target_pairs={{0,1},{1,0},{2,3},{3,2},{4,5},{5,4},{6,7},{7,6},{8,9},{9,8},{10,11... | collective-permute-start | bytes 1572872 | tf_op jit(solution)/shard_map/ppermute | solution.py:22
  97.1 19.7 %collective-permute-start.27 = (bf16[128,1024]{0,1:T(8,128)(2,1)S(1)}, bf16[128,1024]{0,1:T(8,128)(2,1)S(1)}, u32[]{:S(2)}, u32[]{:S(2)}) collective-permute-start(bf16[128,1024]{0,1:T(8,128)(2,1)S(1)} %get-tuple-element.33), channel_id=1, source_target_pairs={{0,2},{1,3},{2,0},{3,1},{4,6},{5,7},{6,4},{7,5},{8,10},{9,11},{10,... | collective-permute-start | bytes 786440 | tf_op jit(solution)/shard_map/ppermute | solution.py:22
  100.7 16.6 %collective-permute-start.6 = (bf16[128,1024]{0,1:T(8,128)(2,1)S(1)}, bf16[128,1024]{0,1:T(8,128)(2,1)S(1)}, u32[]{:S(2)}, u32[]{:S(2)}) collective-permute-start(bf16[128,1024]{0,1:T(8,128)(2,1)S(1)} %collective-permute-done.5), channel_id=1, source_target_pairs={{0,1},{1,0},{2,3},{3,2},{4,5},{5,4},{6,7},{7,6},{8,9},{9,8},{10,11... | collective-permute-start | bytes 786440 | tf_op jit(solution)/shard_map/ppermute | solution.py:22
  102.7 17.2 %collective-permute-start.29 = (bf16[128,1024]{0,1:T(8,128)(2,1)S(1)}, bf16[128,1024]{0,1:T(8,128)(2,1)S(1)}, u32[]{:S(2)}, u32[]{:S(2)}) collective-permute-start(bf16[128,1024]{0,1:T(8,128)(2,1)S(1)} %get-tuple-element.33), channel_id=1, source_target_pairs={{0,1},{1,0},{2,3},{3,2},{4,5},{5,4},{6,7},{7,6},{8,9},{9,8},{10,11... | collective-permute-start | bytes 786440 | tf_op jit(solution)/shard_map/ppermute | solution.py:22
  116.8 3.2 %collective-permute-start.28 = (bf16[128,1024]{0,1:T(8,128)(2,1)S(1)}, bf16[128,1024]{0,1:T(8,128)(2,1)S(1)}, u32[]{:S(2)}, u32[]{:S(2)}) collective-permute-start(bf16[128,1024]{0,1:T(8,128)(2,1)S(1)} %collective-permute-done.27), channel_id=1, source_target_pairs={{0,1},{1,0},{2,3},{3,2},{4,5},{5,4},{6,7},{7,6},{8,9},{9,8},{10,11... | collective-permute-start | bytes 786440 | tf_op jit(solution)/shard_map/ppermute | solution.py:22
  116.8 9.9 %collective-permute-start.22 = (bf16[128,2048]{0,1:T(8,128)(2,1)S(1)}, bf16[128,2048]{0,1:T(8,128)(2,1)S(1)}, u32[]{:S(2)}, u32[]{:S(2)}) collective-permute-start(bf16[128,2048]{0,1:T(8,128)(2,1)S(1)} %collective-permute-done.21), channel_id=1, source_target_pairs={{0,1},{1,0},{2,3},{3,2},{4,5},{5,4},{6,7},{7,6},{8,9},{9,8},{10,11... | collective-permute-start | bytes 1572872 | tf_op jit(solution)/shard_map/ppermute | solution.py:22
  118.1 8.5 %collective-permute-start.10 = (bf16[128,512]{1,0:T(8,128)(2,1)S(1)}, bf16[128,512]{1,0:T(8,128)(2,1)S(1)}, u32[]{:S(2)}, u32[]{:S(2)}) collective-permute-start(bf16[128,512]{1,0:T(8,128)(2,1)S(1)} %fusion.51), channel_id=1, source_target_pairs={{0,4},{4,8},{8,12},{12,16},{16,20},{20,24},{24,28},{28,0},{1,5},{5... | collective-permute-start | bytes 393224 | tf_op jit(solution)/shard_map/ppermute | solution.py:17
  129.8 11.1 %collective-permute-start.26 = (bf16[128,512]{1,0:T(8,128)(2,1)S(1)}, bf16[128,512]{1,0:T(8,128)(2,1)S(1)}, u32[]{:S(2)}, u32[]{:S(2)}) collective-permute-start(bf16[128,512]{1,0:T(8,128)(2,1)S(1)} %fusion.48), channel_id=1, source_target_pairs={{0,28},{4,0},{8,4},{12,8},{16,12},{20,16},{24,20},{28,24},{1,29},{... | collective-permute-start | bytes 393224 | tf_op jit(solution)/shard_map/ppermute | solution.py:17
  (11 other events, 80.0 us)

commit v2 on v1

--- a/solution.py
+++ b/solution.py
@@ -1,6 +1,10 @@
+import functools
+
 import jax
 import jax.numpy as jnp
 from jax import lax
+from jax.experimental import pallas as pl
+from jax.experimental.pallas import tpu as pltpu
 from jax.sharding import PartitionSpec as P
 
 D = 2048
@@ -38,22 +42,109 @@
     return x
 
 
-def sum_scatter(part):
+def parts_body(counts, transposed, me_ref, *refs):
+    streams, addends = counts
+    rows = refs[0][...]
+    weights = refs[1][...]
+    contract = 1 if transposed else 0
+    product = lax.dot_general(
+        rows, weights, (((1,), (contract,)), ((), ())), preferred_element_type=jnp.float32
+    )
+    outs = refs[2 + addends :]
+    for at in range(streams):
+        term = product[at * SEQ : (at + 1) * SEQ]
+        if addends:
+            term = term + refs[2 + at][0].astype(jnp.float32)
+        outs[at][0] = term.astype(outs[at].dtype)
+
+
+def parts(me, rows, weights, first, step, added, kind, transposed, name):
     length = lax.axis_size("dp")
-    held = None
-    for bit in masks():
-        live = [j for j in range(0, length, bit)]
-        away = [j for j in live if j & bit]
-        home = [j for j in live if not j & bit]
-        if held is None:
-            sent = [part(j).astype(jnp.bfloat16) for j in away]
-        else:
-            sent = [held[j].astype(jnp.bfloat16) for j in away]
-        came = [swap(s, bit) for s in sent]
-        if held is None:
-            held = {j: part(j) for j in home}
-        held = {j: held[j] + c.astype(jnp.float32) for j, c in zip(home, came)}
-    return held[0]
+    count = (length - first + step - 1) // step
+    streams = rows.shape[0] // SEQ
+    depth = rows.shape[1]
+    total = weights.shape[0] if transposed else weights.shape[1]
+    chunk = total // length
+    tile = min(1024, chunk)
+    tiles = chunk // tile
+
+    def block_at(g, t, me_ref):
+        return (me_ref[0] ^ (first + step * g)) * tiles + t
+
+    if transposed:
+        weight_spec = pl.BlockSpec((tile, depth), lambda g, t, me_ref: (block_at(g, t, me_ref), 0))
+    else:
+        weight_spec = pl.BlockSpec((depth, tile), lambda g, t, me_ref: (0, block_at(g, t, me_ref)))
+    stack_spec = pl.BlockSpec((1, SEQ, tile), lambda g, t, me_ref: (g, 0, t))
+    size = jnp.dtype(kind).itemsize
+    return pl.pallas_call(
+        functools.partial(parts_body, (streams, len(added)), transposed),
+        grid_spec=pltpu.PrefetchScalarGridSpec(
+            num_scalar_prefetch=1,
+            grid=(count, tiles),
+            in_specs=[pl.BlockSpec(rows.shape, lambda g, t, me_ref: (0, 0)), weight_spec]
+            + [stack_spec] * len(added),
+            out_specs=[stack_spec] * streams,
+        ),
+        out_shape=[jax.ShapeDtypeStruct((count, SEQ, chunk), kind)] * streams,
+        cost_estimate=pl.CostEstimate(
+            flops=2 * rows.shape[0] * depth * chunk * count,
+            bytes_accessed=count * chunk * (2 * depth + streams * SEQ * size),
+            transcendentals=0,
+        ),
+        name=name,
+    )(me, rows, weights, *added)
+
+
+def grad_body(left_ref, right_ref, out_ref):
+    out_ref[0] = lax.dot_general(
+        left_ref[...],
+        right_ref[...],
+        (((0,), (0,)), ((), ())),
+        preferred_element_type=jnp.float32,
+    )
+
+
+def weight_grad(left, right, by_rows, name):
+    length, high = left.shape
+    wide = right.shape[1]
+    if by_rows:
+        tile = min(1024, high)
+        grid = (high // tile,)
+        specs = [
+            pl.BlockSpec((length, tile), lambda t: (0, t)),
+            pl.BlockSpec((length, wide), lambda t: (0, 0)),
+        ]
+        out_spec = pl.BlockSpec((1, tile, wide), lambda t: (0, t, 0))
+    else:
+        tile = min(1024, wide)
+        grid = (wide // tile,)
+        specs = [
+            pl.BlockSpec((length, high), lambda t: (0, 0)),
+            pl.BlockSpec((length, tile), lambda t: (0, t)),
+        ]
+        out_spec = pl.BlockSpec((1, high, tile), lambda t: (0, 0, t))
+    return pl.pallas_call(
+        grad_body,
+        grid=grid,
+        in_specs=specs,
+        out_specs=out_spec,
+        out_shape=jax.ShapeDtypeStruct((1, high, wide), jnp.float32),
+        cost_estimate=pl.CostEstimate(
+            flops=2 * length * high * wide,
+            bytes_accessed=4 * high * wide,
+            transcendentals=0,
+        ),
+        name=name,
+    )(left, right)
+
+
+def tied(x, other):
+    return lax.optimization_barrier((x, other))[0]
+
+
+def first_swaps(stacks):
+    return [swap(s, 1) for s in stacks]
 
 
 def gather_cols(block):
@@ -152,19 +243,60 @@
     def whole_act(pre_part):
         return jax.nn.silu(causal_conv(pre_part, taps_bc))
 
-    def project(rows):
-        values = rows.astype(jnp.float32)
-        squares = jnp.sum(values * values, axis=1, keepdims=True)
-
-        def part(j):
-            cols = lax.dynamic_slice_in_dim(local_xz, (me ^ j) * 2 * width, 2 * width, 1)
-            return jnp.dot(rows, cols, preferred_element_type=jnp.float32)
-
-        raw_xz = sum_scatter(part)
-        small = sum_all(jnp.concatenate([times_transposed(rows, local_bcdt), squares], axis=1))
-        raw_cols = small[:, : MAPS + HEADS]
-        scales = lax.rsqrt(small[:, MAPS + HEADS :] / D + 1e-05)
-        return (values, scales, raw_xz, raw_cols)
+    me_one = jnp.full((1,), me, jnp.int32)
+    length = lax.axis_size("dp")
+    both = jnp.concatenate([saved_rows, input_rows], axis=0)
+    xz_away = parts(me_one, both, local_xz, 1, 2, [], jnp.bfloat16, False, "xz_away")
+    xz_came = first_swaps(xz_away)
+    out_away = parts(me_one, cot_rows, local_out, 1, 2, [], jnp.bfloat16, True, "out_away")
+    out_came = first_swaps(out_away)
+    both_values = both.astype(jnp.float32)
+    squares = jnp.sum(both_values * both_values, axis=1, keepdims=True)
+    small = sum_all(jnp.concatenate([times_transposed(both, local_bcdt), squares], axis=1))
+
+    def later(stack_came, rows, weights, transposed, name):
+        sent = None
+        if length > 2:
+            sent = parts(
+                me_one, rows, weights, 2, 4, [c[1::2] for c in stack_came], jnp.bfloat16, transposed, name + "_send"
+            )
+        kept = parts(
+            me_one, rows, weights, 0, 4, [c[0::2] for c in stack_came], jnp.float32,
+            transposed, name + "_keep"
+        )
+        return sent, kept
+
+    def finish(kept, came):
+        held = kept if came is None else kept + came.astype(jnp.float32)
+        bit = 4
+        held = {4 * k: held[k] for k in range(held.shape[0])}
+        while bit < length:
+            held = {
+                j: held[j] + swap(held[j ^ bit].astype(jnp.bfloat16), bit).astype(jnp.float32)
+                for j in held
+                if not j & bit
+            }
+            bit *= 2
+        return held[0]
+
+    xz_sent, xz_kept = later(xz_came, both, local_xz, False, "xz")
+    out_sent, out_kept = later(out_came, cot_rows, local_out, True, "out")
+    back_came = forward_came = mixed_came = None
+    if xz_sent is not None:
+        back_came = swap(xz_sent[0], 2)
+        mixed_came = swap(out_sent[0], 2)
+        forward_came = swap(tied(xz_sent[1], back_came), 2)
+    back_raw = finish(xz_kept[0], back_came)
+    d_mixed = finish(out_kept[0], mixed_came)
+    forward_raw = finish(xz_kept[1], forward_came)
+
+    def project(rows, own_small, raw_xz):
+        raw_cols = own_small[:, : MAPS + HEADS]
+        scales = lax.rsqrt(own_small[:, MAPS + HEADS :] / D + 1e-05)
+        return (rows.astype(jnp.float32), scales, raw_xz, raw_cols)
+
+    back_proj = project(saved_rows, small[:SEQ], back_raw)
+    forward_proj = project(input_rows, small[SEQ:], forward_raw)
 
     def gate_parts(projected):
         values, scales, raw_xz, raw_cols = projected
@@ -183,15 +315,6 @@
 
         gated, mix_back = jax.vjp(local_mix, mix_x, mix_z, own_dt, scores)
         return (gated, mix_back, maps, pre_part)
-
-    back_proj = project(saved_rows)
-
-    def mixed_part(j):
-        taken = lax.dynamic_slice_in_dim(local_out, (me ^ j) * width, width, 0)
-        return times_transposed(cot_rows, taken)
-
-    d_mixed = sum_scatter(mixed_part)
-    forward_proj = project(input_rows)
 
     values, scales, raw_xz, raw_cols = back_proj
     gated, mix_back, maps, pre_part = gate_parts(back_proj)
@@ -253,10 +376,10 @@
     d_input = (cot_rows.astype(jnp.float32) + d_norm_in).astype(jnp.bfloat16)
     prev_grad = from_behind(d_input, "section", -1)
 
-    grad_out = transposed_times(gather_cols(mixed_in), cot_rows)
-    grad_xz = transposed_times(normed, round_xz)
+    grad_out = weight_grad(gather_cols(mixed_in), cot_rows, True, "grad_out")
+    grad_xz = weight_grad(normed, round_xz, False, "grad_xz")
     grad_bcdt = transposed_times(round_bcdt, normed)
-    return (next_act[None], prev_grad[None], grad_xz[None], grad_bcdt[None], grad_out[None])
+    return (next_act[None], prev_grad[None], grad_xz, grad_bcdt[None], grad_out)
 
 
 def solution(mesh):

time: 143 us -> 158 us (1.10)
  Pallas kernels: 0 us -> 34.6 us
  matrix products: 54.2 us -> 22.6 us
  waiting for transfers between devices: 51.7 us -> 35.4 us
  local copies, waits for them, and re-layouts: 1.56 us -> 17.2 us
  other arithmetic: 10.2 us -> 24.6 us
  starting transfers between devices: 23.3 us -> 20.7 us
    pallas_call x0 -> x8, Pallas kernels: none -> 34.6 us  [the longest x6 19.7 us: parts(): pl.pallas_call(functools.partial(parts_body, (streams, len(added)), trans...]
    dot_general x8 -> x0, matrix products: 21.4 us -> none  [part(): return jnp.dot(rows, cols, preferred_element_type=jnp.float32)]
    ppermute x28 -> x23, waiting for transfers between devices: 50.5 us -> 35.4 us  [swap(): return lax.ppermute(x, 'dp', [(i, i ^ mask) for i in range(length)])]
    dot_general x3 -> x1, matrix products: 15.1 us -> 1.07 us  [transposed_times(): lax.dot_general(left, right, (((0,), (0,)), ((), ())), preferred_element_...]
    add x0 -> x3, local copies, waits for them, and re-layouts: none -> 4.65 us  [finish(): held = kept if came is None else kept + came.astype(jnp.float32)]
    dot_general x4, matrix products: 5.05 us -> 9.54 us  [mixer(): jnp.einsum('hts,shp->thp', weights, heads_in, precision=lax.Precision.HIGH)]
    slice x0 -> x3, local copies, waits for them, and re-layouts: none -> 4.07 us  [later(): c[1::2]]
    ppermute x28 -> x23, starting transfers between devices: 19 us -> 15.2 us  [swap(): return lax.ppermute(x, 'dp', [(i, i ^ mask) for i in range(length)])]
  transfers between devices with their start and end apart: 30 -> 25, of which waited for: 11 -> 10; matrix products, arithmetic and copies ran while one was open for 41% -> 24% of each run, Pallas kernels for 0% -> 19%
where the time goes in v2:
time: 158 us; the launch traced here: 157 us
  waiting for transfers between devices  35.4 us (22%)
  Pallas kernels  34.6 us (22%)
  other arithmetic  24.6 us (16%)
  matrix products  22.6 us (14%)
  starting transfers between devices  20.7 us (13%)
  local copies, waits for them, and re-layouts  17.2 us (11%)
  between operations  1.7 us (1%)
    ppermute x23, waiting for transfers between devices, swap(): return lax.ppermute(x, 'dp', [(i, i ^ mask) for i in range(length)])  35.4 us
    pallas_call x6, Pallas kernels, parts(): pl.pallas_call(functools.partial(parts_body, (streams, len(added)), trans...  19.7 us
    ppermute x23, starting transfers between devices, swap(): return lax.ppermute(x, 'dp', [(i, i ^ mask) for i in range(length)])  15.2 us
    pallas_call x2, Pallas kernels, weight_grad(): pl.pallas_call(grad_body, grid=grid, in_specs=specs, out_specs=out_spec,...  15 us
    dot_general x4, matrix products, mixer(): jnp.einsum('hts,shp->thp', weights, heads_in, precision=lax.Precision.HIGH)  9.54 us
    dot_general x4, matrix products, times_transposed(): lax.dot_general(left, right, (((1,), (1,)), ((), ())), preferred_element_...  7.6 us
    ppermute x2, starting transfers between devices, from_behind(): lax.ppermute(x, axis, [(i, (i + by) % length) for i in range(length)])  5.53 us
    add x3, local copies, waits for them, and re-layouts, finish(): held = kept if came is None else kept + came.astype(jnp.float32)  4.65 us
  transfers between devices with their start and end apart: 25, of which 10 were waited for; matrix products, arithmetic and copies ran while one was open for 24% of the time, Pallas kernels for 19%

profile of v2, /device:TPU:0, one launch (start us, length us, event | category | flops | bytes accessed | tf_op | source)
XLA Modules:
  0.0 156.8 jit_solution(10668332430684152303)
XLA Ops:
  0.7 1.7 %pad_maximum_fusion.4.refs_0_ = bf16[256,512]{1,0:T(8,128)(2,1)} fusion(bf16[128,512]{1,0:T(8,128)(2,1)} %bitcast.169, bf16[128,512]{1,0:T(8,128)(2,1)} %bitcast.166), kind=kLoop, calls=%fused_computation.143 | loop fusion | flops 524288 | bytes 524288 | tf_op jit(solution)/shard_map/concatenate | solution.py:248
  2.4 5.0 %xz_away.1 = (bf16[2,128,2048]{2,1,0:T(8,128)(2,1)}, bf16[2,128,2048]{2,1,0:T(8,128)(2,1)}) custom-call(s32[1]{0:T(128)} %bitcast.2.me_ref, bf16[256,512]{1,0:T(8,128)(2,1)} %pad_maximum_fusion.4.refs_0_, bf16[512,8192]{1,0:T(8,128)(2,1)} %bitcast.147), custom_call_target="tpu_custom_call" | custom-call | flops 1073741824 | bytes 6291456 | tf_op jit(solution)/shard_map/xz_away/pallas_call | solution.py:80
  8.9 3.0 %out_away.1 = bf16[2,128,1024]{2,1,0:T(8,128)(2,1)} custom-call(s32[1]{0:T(128)} %bitcast.2.me_ref, bf16[128,512]{1,0:T(8,128)(2,1)} %bitcast.155, bf16[4096,512]{1,0:T(8,128)(2,1)} %bitcast.150), custom_call_target="tpu_custom_call" | custom-call | flops 268435456 | bytes 2621440 | tf_op jit(solution)/shard_map/out_away/pallas_call | solution.py:80
  12.6 3.0 %collective-permute-start.5 = (f32[256,321]{0,1:T(8,128)S(1)}, f32[256,321]{0,1:T(8,128)S(1)}, u32[]{:S(2)}, u32[]{:S(2)}) collective-permute-start(f32[256,321]{0,1:T(8,128)S(1)} %fusion.144), channel_id=1, source_target_pairs={{0,2},{1,3},{2,0},{3,1},{4,6},{5,7},{6,4},{7,5},{8,10},{9,11},{10,... | collective-permute-start | bytes 986120 | tf_op jit(solution)/shard_map/ppermute | solution.py:26
  16.3 1.9 %fusion.156 = (bf16[1,128,1024]{2,1,0:T(8,128)(2,1)}, bf16[1,128,1024]{2,1,0:T(8,128)(2,1)}) fusion(bf16[2,128,1024]{2,1,0:T(8,128)(2,1)} %collective-permute-done.12), kind=kLoop, calls=%fused_computation.264 | loop fusion | bytes 1048576 | tf_op jit(solution)/shard_map/slice | solution.py:261
  18.1 2.5 %out_send.1 = bf16[1,128,1024]{2,1,0:T(8,128)(2,1)} custom-call(s32[1]{0:T(128)} %bitcast.2.me_ref, bf16[128,512]{1,0:T(8,128)(2,1)} %bitcast.156, bf16[4096,512]{1,0:T(8,128)(2,1)} %bitcast.151, bf16[1,128,1024]{2,1,0:T(8,128)(2,1)} %get-tuple-element.56.refs_2_), custom_call_target="tpu_custom_call" | custom-call | flops 134217728 | bytes 1310720 | tf_op jit(solution)/shard_map/out_send/pallas_call | solution.py:80
  21.1 2.6 %out_keep.1 = f32[1,128,1024]{2,1,0:T(8,128)} custom-call(s32[1]{0:T(128)} %bitcast.2.me_ref, bf16[128,512]{1,0:T(8,128)(2,1)} %bitcast.157, bf16[4096,512]{1,0:T(8,128)(2,1)} %bitcast.152, bf16[1,128,1024]{2,1,0:T(8,128)(2,1)} %get-tuple-element.57.refs_2_), custom_call_target="tpu_custom_call" | custom-call | flops 134217728 | bytes 1572864 | tf_op jit(solution)/shard_map/out_keep/pallas_call | solution.py:80
  26.6 3.3 %xz_send.1 = (bf16[1,128,2048]{2,1,0:T(8,128)(2,1)}, bf16[1,128,2048]{2,1,0:T(8,128)(2,1)}) custom-call(s32[1]{0:T(128)} %bitcast.2.me_ref, bf16[256,512]{1,0:T(8,128)(2,1)} %pad_maximum_fusion.4.refs_0_, bf16[512,8192]{1,0:T(8,128)(2,1)} %bitcast.148, bf16[1,128,2048]{2,1,0:T(8,128)(2,1)} %get-tuple-element.51.refs_2_, ...), custom_call_target="tpu_custom_call" | custom-call | flops 536870912 | bytes 3145728 | tf_op jit(solution)/shard_map/xz_send/pallas_call | solution.py:80
  29.8 2.2 %collective-permute-start.2 = (bf16[1,128,2048]{2,1,0:T(8,128)(2,1)}, bf16[1,128,2048]{2,1,0:T(8,128)(2,1)S(1)}, u32[]{:S(2)}, u32[]{:S(2)}) collective-permute-start(bf16[1,128,2048]{2,1,0:T(8,128)(2,1)} %get-tuple-element.16), channel_id=1, source_target_pairs={{0,2},{1,3},{2,0},{3,1},{4,6},{5,7},{6,4},{7,5},{8,10},{9,11},{10,... | collective-permute-start | bytes 1572872 | tf_op jit(solution)/shard_map/ppermute | solution.py:26
  33.5 9.9 %collective-permute-done.2 = bf16[1,128,2048]{2,1,0:T(8,128)(2,1)S(1)} collective-permute-done((bf16[1,128,2048]{2,1,0:T(8,128)(2,1)}, bf16[1,128,2048]{2,1,0:T(8,128)(2,1)S(1)}, u32[]{:S(2)}, u32[]{:S(2)}) %collective-permute-start.2) | collective-permute-done | bytes 524320 | tf_op jit(solution)/shard_map/ppermute | solution.py:26
  46.8 3.4 %xz_keep.1 = (f32[1,128,2048]{2,1,0:T(8,128)}, f32[1,128,2048]{2,1,0:T(8,128)}) custom-call(s32[1]{0:T(128)} %bitcast.2.me_ref, bf16[256,512]{1,0:T(8,128)(2,1)} %pad_maximum_fusion.4.refs_0_, bf16[512,8192]{1,0:T(8,128)(2,1)} %bitcast.149, bf16[1,128,2048]{2,1,0:T(8,128)(2,1)} %get-tuple-element.52.refs_2_, bf16[1,128,2048]{2,1,0:T(8,128)(2,1)} %get-tuple-element.50.refs_3_), custom_call_target="tpu_custom_call" | custom-call | flops 536870912 | bytes 4194304 | tf_op jit(solution)/shard_map/xz_keep/pallas_call | solution.py:80
  50.2 5.7 %collective-permute-done.3 = bf16[1,128,2048]{2,1,0:T(8,128)(2,1)S(1)} collective-permute-done((bf16[1,128,2048]{2,1,0:T(8,128)(2,1)}, bf16[1,128,2048]{2,1,0:T(8,128)(2,1)S(1)}, u32[]{:S(2)}, u32[]{:S(2)}) %collective-permute-start.3) | collective-permute-done | bytes 524320 | tf_op jit(solution)/shard_map/ppermute | solution.py:26
  55.9 1.8 %convert_add_fusion = (f32[1,128,2048]{2,1,0:T(8,128)S(1)}, f32[1,128,2048]{2,1,0:T(8,128)S(1)}) fusion(f32[1,128,2048]{2,1,0:T(8,128)} %get-tuple-element.18, bf16[1,128,2048]{2,1,0:T(8,128)(2,1)S(1)} %collective-permute-done.2, f32[1,128,2048]{2,1,0:T(8,128)} %get-tuple-element.14, bf16[1,128,2048]{2,1,0:T(8,128)(2,1)S(1)} %collective-permute-done.3), kind=kLoop, calls=%fused_computation.46 | loop fusion | flops 1048576 | bytes 5242880 | tf_op jit(solution)/shard_map/add | solution.py:270
  62.4 1.4 copy_multiply_fusion.1
  64.9 2.4 %fusion.65 = (f32[128,1024]{0,1:T(8,128)S(1)}, f32[128,1024]{0,1:T(8,128)}, f32[128,1024]{0,1:T(8,128)}) fusion(f32[128,1024]{0,1:T(8,128)S(1)} %bitcast.163, f32[1024]{0:T(1024)S(1)} %bitcast.187, f32[1024]{0:T(1024)S(1)} %bitcast.185, f32[1024]{0:T(1024)S(1)} %bitcast.183, f32[1024]{0:T(1024)S(1)} %bitcast.181, f32[128,1024]{0,1:T(8,128)S(1)} %bitcast.164), kind=kLoop, calls=%fused_computation.104 | loop fusion | flops 2883584 | bytes 2637824 | tf_op jit(solution)/shard_map/jvp(jit(silu))/mul | solution.py:182
  67.3 2.4 %multiply_reduce_fusion.2 = (f32[128]{0:T(128)}, f32[128,16,64]{0,2,1:T(8,128)S(1)}, f32[128,16,64]{0,2,1:T(8,128)}) fusion(f32[128,16,2,64]{0,3,1,2:T(8,128)S(1)} %copy_multiply_fusion, f32[128,16,64]{0,2,1:T(8,128)S(1)} %bitcast.174, f32[16]{0:T(128)S(1)} %bitcast.217, f32[16,128]{1,0:T(8,128)S(1)} %copy-done.44, f32[128,128]{1,0:T(8,128)S(1)} %copy-done.23, ...), kind=kOutput, calls=%fused_computation.92 | convolution fusion | flops 103153536 | bytes 2728960 | tf_op jit(solution)/shard_map/jvp(hts,shp->thp)/dot_general | solution.py:194
  70.0 2.0 %fusion.55 = (f32[128]{0:T(128)S(1)}, f32[1,128,1024]{2,1,0:T(8,128)}) fusion(f32[128,1024]{1,0:T(8,128)S(1)} %copy.28, f32[1024]{0:T(1024)S(1)} %bitcast.179, f32[1,128,1024]{2,1,0:T(8,128)} %out_keep.1, bf16[1,128,1024]{2,1,0:T(8,128)(2,1)} %collective-permute-done.13), kind=kLoop, calls=%fused_computation.88 | loop fusion | flops 655232 | bytes 1839616 | tf_op jit(solution)/shard_map/reduce_sum | solution.py:323
  78.2 2.0 %copy.29 = f32[1,128,1024]{1,2,0:T(8,128)} copy(f32[1,128,1024]{2,1,0:T(8,128)} %get-tuple-element.32) | data formatting | bytes 1048576 | tf_op jit(solution)/shard_map/add | solution.py:270
  81.0 2.5 %fusion = f32[128,16,64]{0,2,1:T(8,128)S(1)} fusion(f32[16,128]{1,0:T(8,128)} %fusion.143, f32[128,128]{1,0:T(8,128)} %fusion.108, f32[16,128]{1,0:T(8,128)} %fusion.101, pred[128,128]{1,0:T(8,128)(4,1)} %iota_compare_fusion, f32[16]{0:T(128)} %bitcast.216, f32[128]{0:T(128)S(1)} %slice_bitcast_fusion.2, f32[128,16,64]{0,2,1:T(8,128)S(1)} %get-tuple-element.30, ...), kind=kOutput, calls=%fused_computation.9 | convolution fusion | flops 105119744 | bytes 3796480 | tf_op jit(solution)/shard_map/transpose(jvp(hts,shp->thp))/dot_general | solution.py:194
  83.6 2.7 %fusion.33 = (f32[16,128]{1,0:T(8,128)}, f32[16,128]{1,0:T(8,128)}, f32[16,128]{1,0:T(8,128)}, f32[128,128]{1,0:T(8,128)S(1)}) fusion(f32[16,128]{1,0:T(8,128)S(1)} %copy-done.45, f32[128,128]{1,0:T(8,128)S(1)} %copy-done.24, f32[16,128]{1,0:T(8,128)S(1)} %copy-done.64, pred[128,128]{1,0:T(8,128)(4,1)S(1)} %copy-done.32, f32[128,16,64]{0,2,1:T(8,128)S(1)} %bitcast.175, ...), kind=kOutput, calls=%fused_computation.57 | convolution fusion | flops 106014720 | bytes 2303488 | tf_op jit(solution)/shard_map/transpose(jvp(hts,shp->thp))/dot_general | solution.py:194
  92.6 1.8 %collective-permute-start.20 = (f32[128,321]{0,1:T(8,128)S(1)}, f32[128,321]{0,1:T(8,128)S(1)}, u32[]{:S(2)}, u32[]{:S(2)}) collective-permute-start(f32[128,321]{0,1:T(8,128)S(1)} %fusion.145), channel_id=1, source_target_pairs={{0,2},{1,3},{2,0},{3,1},{4,6},{5,7},{6,4},{7,5},{8,10},{9,11},{10,... | collective-permute-start | bytes 493064 | tf_op jit(solution)/shard_map/ppermute | solution.py:26
  94.9 4.9 %collective-permute-done.20 = f32[128,321]{0,1:T(8,128)S(1)} collective-permute-done((f32[128,321]{0,1:T(8,128)S(1)}, f32[128,321]{0,1:T(8,128)S(1)}, u32[]{:S(2)}, u32[]{:S(2)}) %collective-permute-start.20) | collective-permute-done | bytes 164384 | tf_op jit(solution)/shard_map/ppermute | solution.py:26
  101.4 2.0 %multiply_reduce_fusion.3 = (f32[128]{0:T(128)S(1)}, f32[128,16,64]{0,2,1:T(8,128)}) fusion(f32[128,16,2,64]{0,3,1,2:T(8,128)S(1)} %copy-done.3, f32[128,16,64]{0,2,1:T(8,128)S(1)} %bitcast.173, f32[16]{0:T(128)S(1)} %bitcast.218, f32[16,128]{1,0:T(8,128)S(1)} %fusion.121, f32[128,128]{1,0:T(8,128)S(1)} %fusion.103, f32[16,128]{1,0:T(8,128)S(1)} %fusion.102, ...), kind=kOutput, calls=%fused_computation.105 | convolution fusion | flops 103153536 | bytes 2204672 | tf_op jit(solution)/shard_map/jvp(hts,shp->thp)/dot_general | solution.py:194
  104.7 1.8 %collective-permute-start.6 = (bf16[128,1024]{1,0:T(8,128)(2,1)S(1)}, bf16[128,1024]{1,0:T(8,128)(2,1)S(1)}, u32[]{:S(2)}, u32[]{:S(2)}) collective-permute-start(bf16[128,1024]{1,0:T(8,128)(2,1)S(1)} %get-tuple-element.72), channel_id=1, source_target_pairs={{0,2},{1,3},{2,0},{3,1},{4,6},{5,7},{6,4},{7,5},{8,10},{9,11},{10,... | collective-permute-start | bytes 786440 | tf_op jit(solution)/shard_map/ppermute | solution.py:26
  109.4 7.3 %collective-permute-done.6 = bf16[128,1024]{1,0:T(8,128)(2,1)S(1)} collective-permute-done((bf16[128,1024]{1,0:T(8,128)(2,1)S(1)}, bf16[128,1024]{1,0:T(8,128)(2,1)S(1)}, u32[]{:S(2)}, u32[]{:S(2)}) %collective-permute-start.6) | collective-permute-done | bytes 262176 | tf_op jit(solution)/shard_map/ppermute | solution.py:26
  117.7 3.8 %collective-permute-done.10 = f32[1,128]{1,0:T(1,128)S(1)} collective-permute-done((f32[1,128]{1,0:T(1,128)S(1)}, f32[1,128]{1,0:T(1,128)S(1)}, u32[]{:S(2)}, u32[]{:S(2)}) %collective-permute-start.10) | collective-permute-done | bytes 544 | tf_op jit(solution)/shard_map/ppermute | solution.py:26
  126.1 5.7 %grad_out.1 = f32[1,4096,512]{2,1,0:T(8,128)} custom-call(bf16[128,4096]{1,0:T(8,128)(2,1)} %pad_maximum_fusion.1.left_ref, bf16[128,512]{1,0:T(8,128)(2,1)} %bitcast.158), custom_call_target="tpu_custom_call" | custom-call | flops 536870912 | bytes 8388608 | tf_op jit(solution)/shard_map/grad_out/pallas_call | solution.py:127
  132.6 1.5 broadcast_select_fusion.7
  134.2 6.3 %fusion.8 = bf16[128,512]{1,0:T(8,128)(2,1)S(1)} fusion(f32[128,512]{1,0:T(8,128)S(1)} %fusion.76, f32[128]{0:T(128)S(1)} %fusion.124, f32[128]{0:T(128)S(1)} %copy-done.54, f32[128]{0:T(128)S(1)} %copy-done.43, bf16[1,128,512]{2,1,0:T(8,128)(2,1)S(1)} %copy-done.4, bf16[1,512,8192]{2,1,0:T(8,128)(2,1)} %param.15, bf16[1,128,512]{2,1,0:T(8,128)(2,1)S(1)} %copy-done.9, ...), kind=kOutput, calls=%fused_computation.21 | convolution fusion | flops 1082785792 | bytes 11142656 | tf_op jit(solution)/shard_map/dot_general | solution.py:201
  140.5 4.3 %collective-permute-start.21 = (bf16[128,512]{1,0:T(8,128)(2,1)S(1)}, bf16[128,512]{1,0:T(8,128)(2,1)S(1)}, u32[]{:S(2)}, u32[]{:S(2)}) collective-permute-start(bf16[128,512]{1,0:T(8,128)(2,1)S(1)} %fusion.8), channel_id=1, source_target_pairs={{0,28},{4,0},{8,4},{12,8},{16,12},{20,16},{24,20},{28,24},{1,29},{... | collective-permute-start | bytes 393224 | tf_op jit(solution)/shard_map/ppermute | solution.py:21
  144.8 1.4 pad_maximum_fusion.right_ref
  146.2 9.3 %grad_xz.1 = f32[1,512,8192]{2,1,0:T(8,128)} custom-call(bf16[128,512]{1,0:T(8,128)(2,1)} %copy-done.12, bf16[128,8192]{1,0:T(8,128)(2,1)} %pad_maximum_fusion.right_ref), custom_call_target="tpu_custom_call" | custom-call | flops 1073741824 | bytes 16777216 | tf_op jit(solution)/shard_map/grad_xz/pallas_call | solution.py:127
  (243 shorter events, 43.8 us)
Async XLA Ops:
  7.4 16.9 %collective-permute-start = (bf16[2,128,2048]{2,1,0:T(8,128)(2,1)}, bf16[2,128,2048]{2,1,0:T(8,128)(2,1)S(1)}, u32[]{:S(2)}, u32[]{:S(2)}) collective-permute-start(bf16[2,128,2048]{2,1,0:T(8,128)(2,1)} %get-tuple-element.12), channel_id=1, source_target_pairs={{0,1},{1,0},{2,3},{3,2},{4,5},{5,4},{6,7},{7,6},{8,9},{9,8},{10,11... | collective-permute-start | bytes 3145736 | tf_op jit(solution)/shard_map/ppermute | solution.py:26
  7.9 17.6 %collective-permute-start.1 = (bf16[2,128,2048]{2,1,0:T(8,128)(2,1)}, bf16[2,128,2048]{2,1,0:T(8,128)(2,1)S(1)}, u32[]{:S(2)}, u32[]{:S(2)}) collective-permute-start(bf16[2,128,2048]{2,1,0:T(8,128)(2,1)} %get-tuple-element.13), channel_id=1, source_target_pairs={{0,1},{1,0},{2,3},{3,2},{4,5},{5,4},{6,7},{7,6},{8,9},{9,8},{10,11... | collective-permute-start | bytes 3145736 | tf_op jit(solution)/shard_map/ppermute | solution.py:26
  8.4 4.2 %collective-permute-start.4 = (f32[256,321]{0,1:T(8,128)S(1)}, f32[256,321]{0,1:T(8,128)S(1)}, u32[]{:S(2)}, u32[]{:S(2)}) collective-permute-start(f32[256,321]{0,1:T(8,128)S(1)} %pad_maximum_fusion.3), channel_id=1, source_target_pairs={{0,1},{1,0},{2,3},{3,2},{4,5},{5,4},{6,7},{7,6},{8,9},{9,8},{10,11... | collective-permute-start | bytes 986120 | tf_op jit(solution)/shard_map/ppermute | solution.py:26
  11.9 4.4 %collective-permute-start.12 = (bf16[2,128,1024]{2,1,0:T(8,128)(2,1)}, bf16[2,128,1024]{2,1,0:T(8,128)(2,1)}, u32[]{:S(2)}, u32[]{:S(2)}) collective-permute-start(bf16[2,128,1024]{2,1,0:T(8,128)(2,1)} %out_away.1), channel_id=1, source_target_pairs={{0,1},{1,0},{2,3},{3,2},{4,5},{5,4},{6,7},{7,6},{8,9},{9,8},{10,11... | collective-permute-start | bytes 1572872 | tf_op jit(solution)/shard_map/ppermute | solution.py:26
  11.9 52.9 %copy-start.27 = (f32[1,1,1024]{2,1,0:T(1,128)}, f32[1,1,1024]{2,1,0:T(1,128)S(1)}, u32[]{:S(2)}) copy-start(f32[1,1,1024]{2,1,0:T(1,128)S(1)} %get-tuple-element.69) | copy-start | bytes 12292
  12.5 20.1 %copy-start.58 = (f32[16]{0:T(128)}, f32[16]{0:T(128)S(1)}, u32[]{:S(2)}) copy-start(f32[16]{0:T(128)S(1)} %negate_bitcast_fusion) | copy-start | bytes 196
  12.6 11.6 %collective-permute-start.5 = (f32[256,321]{0,1:T(8,128)S(1)}, f32[256,321]{0,1:T(8,128)S(1)}, u32[]{:S(2)}, u32[]{:S(2)}) collective-permute-start(f32[256,321]{0,1:T(8,128)S(1)} %fusion.144), channel_id=1, source_target_pairs={{0,2},{1,3},{2,0},{3,1},{4,6},{5,7},{6,4},{7,5},{8,10},{9,11},{10,... | collective-permute-start | bytes 986120 | tf_op jit(solution)/shard_map/ppermute | solution.py:26
  20.6 49.4 %collective-permute-start.13 = (bf16[1,128,1024]{2,1,0:T(8,128)(2,1)}, bf16[1,128,1024]{2,1,0:T(8,128)(2,1)}, u32[]{:S(2)}, u32[]{:S(2)}) collective-permute-start(bf16[1,128,1024]{2,1,0:T(8,128)(2,1)} %out_send.1), channel_id=1, source_target_pairs={{0,2},{1,3},{2,0},{3,1},{4,6},{5,7},{6,4},{7,5},{8,10},{9,11},{10,... | collective-permute-start | bytes 786440 | tf_op jit(solution)/shard_map/ppermute | solution.py:26
  26.5 18.5 %copy-start.34 = (f32[1,1,256]{2,1,0:T(1,128)S(1)}, f32[1,1,256]{2,1,0:T(1,128)}, u32[]{:S(2)}) copy-start(f32[1,1,256]{2,1,0:T(1,128)} %get-tuple-element.73) | copy-start | bytes 3076
  26.5 18.5 %copy-start.36 = (f32[1,1,256]{2,1,0:T(1,128)S(1)}, f32[1,1,256]{2,1,0:T(1,128)}, u32[]{:S(2)}) copy-start(f32[1,1,256]{2,1,0:T(1,128)} %get-tuple-element.74) | copy-start | bytes 3076
  26.5 18.5 %copy-start.38 = (f32[1,1,256]{2,1,0:T(1,128)S(1)}, f32[1,1,256]{2,1,0:T(1,128)}, u32[]{:S(2)}) copy-start(f32[1,1,256]{2,1,0:T(1,128)} %get-tuple-element.75) | copy-start | bytes 3076
  26.5 18.5 %copy-start.40 = (f32[1,1,256]{2,1,0:T(1,128)S(1)}, f32[1,1,256]{2,1,0:T(1,128)}, u32[]{:S(2)}) copy-start(f32[1,1,256]{2,1,0:T(1,128)} %get-tuple-element.76) | copy-start | bytes 3076
  29.8 13.6 %collective-permute-start.2 = (bf16[1,128,2048]{2,1,0:T(8,128)(2,1)}, bf16[1,128,2048]{2,1,0:T(8,128)(2,1)S(1)}, u32[]{:S(2)}, u32[]{:S(2)}) collective-permute-start(bf16[1,128,2048]{2,1,0:T(8,128)(2,1)} %get-tuple-element.16), channel_id=1, source_target_pairs={{0,2},{1,3},{2,0},{3,1},{4,6},{5,7},{6,4},{7,5},{8,10},{9,11},{10,... | collective-permute-start | bytes 1572872 | tf_op jit(solution)/shard_map/ppermute | solution.py:26
  43.4 12.5 %collective-permute-start.3 = (bf16[1,128,2048]{2,1,0:T(8,128)(2,1)}, bf16[1,128,2048]{2,1,0:T(8,128)(2,1)S(1)}, u32[]{:S(2)}, u32[]{:S(2)}) collective-permute-start(bf16[1,128,2048]{2,1,0:T(8,128)(2,1)} %get-tuple-element.17), channel_id=1, source_target_pairs={{0,2},{1,3},{2,0},{3,1},{4,6},{5,7},{6,4},{7,5},{8,10},{9,11},{10,... | collective-permute-start | bytes 1572872 | tf_op jit(solution)/shard_map/ppermute | solution.py:26
  72.6 1.1 collective-permute-start.14
  74.8 5.4 %collective-permute-start.15 = (f32[2,128]{1,0:T(2,128)}, f32[2,128]{1,0:T(2,128)}, u32[]{:S(2)}, u32[]{:S(2)}) collective-permute-start(f32[2,128]{1,0:T(2,128)} %fusion.142), channel_id=1, source_target_pairs={{0,2},{1,3},{2,0},{3,1},{4,6},{5,7},{6,4},{7,5},{8,10},{9,11},{10,... | collective-permute-start | bytes 3080 | tf_op jit(solution)/shard_map/ppermute | solution.py:26
  91.1 1.5 collective-permute-start.19
  92.6 7.2 %collective-permute-start.20 = (f32[128,321]{0,1:T(8,128)S(1)}, f32[128,321]{0,1:T(8,128)S(1)}, u32[]{:S(2)}, u32[]{:S(2)}) collective-permute-start(f32[128,321]{0,1:T(8,128)S(1)} %fusion.145), channel_id=1, source_target_pairs={{0,2},{1,3},{2,0},{3,1},{4,6},{5,7},{6,4},{7,5},{8,10},{9,11},{10,... | collective-permute-start | bytes 493064 | tf_op jit(solution)/shard_map/ppermute | solution.py:26
  94.5 22.2 %copy-start.12 = (bf16[128,512]{1,0:T(8,128)(2,1)}, bf16[128,512]{1,0:T(8,128)(2,1)S(1)}, u32[]{:S(2)}) copy-start(bf16[128,512]{1,0:T(8,128)(2,1)S(1)} %fusion.82.left_ref) | copy-start | bytes 393220
  94.5 27.0 %collective-permute-start.16 = (bf16[128,2048]{1,0:T(8,128)(2,1)S(1)}, bf16[128,2048]{1,0:T(8,128)(2,1)}, u32[]{:S(2)}, u32[]{:S(2)}) collective-permute-start(bf16[128,2048]{1,0:T(8,128)(2,1)S(1)} %copy.31), channel_id=1, source_target_pairs={{0,2},{1,3},{2,0},{3,1},{4,6},{5,7},{6,4},{7,5},{8,10},{9,11},{10,... | collective-permute-start | bytes 1572872 | tf_op jit(solution)/shard_map/ppermute | solution.py:26
  104.7 12.0 %collective-permute-start.6 = (bf16[128,1024]{1,0:T(8,128)(2,1)S(1)}, bf16[128,1024]{1,0:T(8,128)(2,1)S(1)}, u32[]{:S(2)}, u32[]{:S(2)}) collective-permute-start(bf16[128,1024]{1,0:T(8,128)(2,1)S(1)} %get-tuple-element.72), channel_id=1, source_target_pairs={{0,2},{1,3},{2,0},{3,1},{4,6},{5,7},{6,4},{7,5},{8,10},{9,11},{10,... | collective-permute-start | bytes 786440 | tf_op jit(solution)/shard_map/ppermute | solution.py:26
  106.5 15.6 %collective-permute-start.8 = (bf16[128,1024]{1,0:T(8,128)(2,1)S(1)}, bf16[128,1024]{1,0:T(8,128)(2,1)S(1)}, u32[]{:S(2)}, u32[]{:S(2)}) collective-permute-start(bf16[128,1024]{1,0:T(8,128)(2,1)S(1)} %get-tuple-element.72), channel_id=1, source_target_pairs={{0,1},{1,0},{2,3},{3,2},{4,5},{5,4},{6,7},{7,6},{8,9},{9,8},{10,11... | collective-permute-start | bytes 786440 | tf_op jit(solution)/shard_map/ppermute | solution.py:26
  106.8 1.4 collective-permute-start.9
  107.3 14.9 %collective-permute-start.22 = (bf16[128,1024]{1,0:T(8,128)(2,1)S(1)}, bf16[128,1024]{1,0:T(8,128)(2,1)S(1)}, u32[]{:S(2)}, u32[]{:S(2)}) collective-permute-start(bf16[128,1024]{1,0:T(8,128)(2,1)S(1)} %get-tuple-element.71), channel_id=1, source_target_pairs={{0,2},{1,3},{2,0},{3,1},{4,6},{5,7},{6,4},{7,5},{8,10},{9,11},{10,... | collective-permute-start | bytes 786440 | tf_op jit(solution)/shard_map/ppermute | solution.py:26
  108.2 13.4 %collective-permute-start.10 = (f32[1,128]{1,0:T(1,128)S(1)}, f32[1,128]{1,0:T(1,128)S(1)}, u32[]{:S(2)}, u32[]{:S(2)}) collective-permute-start(f32[1,128]{1,0:T(1,128)S(1)} %bitcast_add_fusion), channel_id=1, source_target_pairs={{0,2},{1,3},{2,0},{3,1},{4,6},{5,7},{6,4},{7,5},{8,10},{9,11},{10,... | collective-permute-start | bytes 1544 | tf_op jit(solution)/shard_map/ppermute | solution.py:26
  116.7 6.0 %collective-permute-start.7 = (bf16[128,1024]{1,0:T(8,128)(2,1)S(1)}, bf16[128,1024]{1,0:T(8,128)(2,1)S(1)}, u32[]{:S(2)}, u32[]{:S(2)}) collective-permute-start(bf16[128,1024]{1,0:T(8,128)(2,1)S(1)} %collective-permute-done.6), channel_id=1, source_target_pairs={{0,1},{1,0},{2,3},{3,2},{4,5},{5,4},{6,7},{7,6},{8,9},{9,8},{10,11... | collective-permute-start | bytes 786440 | tf_op jit(solution)/shard_map/ppermute | solution.py:26
  121.6 10.3 %collective-permute-start.18 = (bf16[128,2048]{1,0:T(8,128)(2,1)S(1)}, bf16[128,2048]{1,0:T(8,128)(2,1)S(1)}, u32[]{:S(2)}, u32[]{:S(2)}) collective-permute-start(bf16[128,2048]{1,0:T(8,128)(2,1)S(1)} %copy.31), channel_id=1, source_target_pairs={{0,1},{1,0},{2,3},{3,2},{4,5},{5,4},{6,7},{7,6},{8,9},{9,8},{10,11... | collective-permute-start | bytes 1572872 | tf_op jit(solution)/shard_map/ppermute | solution.py:26
  121.6 3.2 %collective-permute-start.24 = (bf16[128,1024]{1,0:T(8,128)(2,1)S(1)}, bf16[128,1024]{1,0:T(8,128)(2,1)S(1)}, u32[]{:S(2)}, u32[]{:S(2)}) collective-permute-start(bf16[128,1024]{1,0:T(8,128)(2,1)S(1)} %get-tuple-element.71), channel_id=1, source_target_pairs={{0,1},{1,0},{2,3},{3,2},{4,5},{5,4},{6,7},{7,6},{8,9},{9,8},{10,11... | collective-permute-start | bytes 786440 | tf_op jit(solution)/shard_map/ppermute | solution.py:26
  122.1 10.5 %collective-permute-start.17 = (bf16[128,2048]{1,0:T(8,128)(2,1)}, bf16[128,2048]{1,0:T(8,128)(2,1)}, u32[]{:S(2)}, u32[]{:S(2)}) collective-permute-start(bf16[128,2048]{1,0:T(8,128)(2,1)} %collective-permute-done.16), channel_id=1, source_target_pairs={{0,1},{1,0},{2,3},{3,2},{4,5},{5,4},{6,7},{7,6},{8,9},{9,8},{10,11... | collective-permute-start | bytes 1572872 | tf_op jit(solution)/shard_map/ppermute | solution.py:26
  122.2 2.7 %collective-permute-start.23 = (bf16[128,1024]{1,0:T(8,128)(2,1)S(1)}, bf16[128,1024]{1,0:T(8,128)(2,1)S(1)}, u32[]{:S(2)}, u32[]{:S(2)}) collective-permute-start(bf16[128,1024]{1,0:T(8,128)(2,1)S(1)} %collective-permute-done.22), channel_id=1, source_target_pairs={{0,1},{1,0},{2,3},{3,2},{4,5},{5,4},{6,7},{7,6},{8,9},{9,8},{10,11... | collective-permute-start | bytes 786440 | tf_op jit(solution)/shard_map/ppermute | solution.py:26
  123.5 8.3 %collective-permute-start.11 = (bf16[128,512]{1,0:T(8,128)(2,1)S(1)}, bf16[128,512]{1,0:T(8,128)(2,1)S(1)}, u32[]{:S(2)}, u32[]{:S(2)}) collective-permute-start(bf16[128,512]{1,0:T(8,128)(2,1)S(1)} %fusion.9), channel_id=1, source_target_pairs={{0,4},{4,8},{8,12},{12,16},{16,20},{20,24},{24,28},{28,0},{1,5},{5... | collective-permute-start | bytes 393224 | tf_op jit(solution)/shard_map/ppermute | solution.py:21
  140.5 15.0 %collective-permute-start.21 = (bf16[128,512]{1,0:T(8,128)(2,1)S(1)}, bf16[128,512]{1,0:T(8,128)(2,1)S(1)}, u32[]{:S(2)}, u32[]{:S(2)}) collective-permute-start(bf16[128,512]{1,0:T(8,128)(2,1)S(1)} %fusion.8), channel_id=1, source_target_pairs={{0,28},{4,0},{8,4},{12,8},{16,12},{20,16},{24,20},{28,24},{1,29},{... | collective-permute-start | bytes 393224 | tf_op jit(solution)/shard_map/ppermute | solution.py:21
  (58 other events, 295.5 us)

commit v3 on v1

--- a/solution.py
+++ b/solution.py
@@ -38,40 +38,59 @@
     return x
 
 
-def sum_scatter(part):
+def tied(x, other):
+    return lax.optimization_barrier((x, other))[0]
+
+
+def sum_first(part):
     length = lax.axis_size("dp")
-    held = None
-    for bit in masks():
-        live = [j for j in range(0, length, bit)]
-        away = [j for j in live if j & bit]
-        home = [j for j in live if not j & bit]
-        if held is None:
-            sent = [part(j).astype(jnp.bfloat16) for j in away]
-        else:
-            sent = [held[j].astype(jnp.bfloat16) for j in away]
-        came = [swap(s, bit) for s in sent]
-        if held is None:
-            held = {j: part(j) for j in home}
-        held = {j: held[j] + c.astype(jnp.float32) for j, c in zip(home, came)}
-    return held[0]
-
-
-def gather_cols(block):
+    came = {j - 1: swap(part(j).astype(jnp.bfloat16), 1) for j in range(1, length, 2)}
+    return {j: part(j) + came[j].astype(jnp.float32) for j in sorted(came, reverse=True)}
+
+
+def sum_rest(held, after=None):
+    first = None
+    for bit in masks()[1:]:
+        sent = {j: held[j].astype(jnp.bfloat16) for j in held if j & bit}
+        if after is not None and first is None:
+            sent = {j: tied(x, after) for j, x in sent.items()}
+        came = {j ^ bit: swap(x, bit) for j, x in sent.items()}
+        if first is None:
+            first = came[0]
+        held = {j: held[j] + came[j].astype(jnp.float32) for j in came}
+    return held[0], first
+
+
+def sum_both(x):
     me = lax.axis_index("dp")
-    rows, width = block.shape
+    odd = (me & 1) != 0
+    x = x + swap(x, 1)
+    mine = jnp.where(odd, x[SEQ:], x[:SEQ])
+    for bit in masks()[1:]:
+        mine = mine + swap(mine, bit)
+    other = swap(mine, 1)
+    return jnp.where(odd, other, mine), jnp.where(odd, mine, other)
+
+
+def gather_cols(block, after=None):
+    me = lax.axis_index("dp")
     length = lax.axis_size("dp")
+    if after is not None:
+        block = tied(block, after)
     held = [block]
+    order = [0]
+    first = None
     for bit in reversed(masks()):
         held = held + [swap(b, bit) for b in held]
-    order = [0]
-    for bit in reversed(masks()):
         order = order + [j ^ bit for j in order]
+        if first is None:
+            first = held[1]
     by_mask = {j: b for j, b in zip(order, held)}
     level = [by_mask[j] for j in range(length)]
     for bit in masks():
         flip = (me & bit) != 0
         level = [jnp.where(flip, level[j ^ bit], level[j]) for j in range(length)]
-    return jnp.concatenate(level, axis=1)
+    return jnp.concatenate(level, axis=1), first
 
 
 def causal_conv(values, kernel_taps):
@@ -152,19 +171,36 @@
     def whole_act(pre_part):
         return jax.nn.silu(causal_conv(pre_part, taps_bc))
 
-    def project(rows):
-        values = rows.astype(jnp.float32)
-        squares = jnp.sum(values * values, axis=1, keepdims=True)
-
-        def part(j):
-            cols = lax.dynamic_slice_in_dim(local_xz, (me ^ j) * 2 * width, 2 * width, 1)
-            return jnp.dot(rows, cols, preferred_element_type=jnp.float32)
-
-        raw_xz = sum_scatter(part)
-        small = sum_all(jnp.concatenate([times_transposed(rows, local_bcdt), squares], axis=1))
+    both = jnp.concatenate([saved_rows, input_rows], axis=0)
+    both_values = both.astype(jnp.float32)
+    squares = jnp.sum(both_values * both_values, axis=1, keepdims=True)
+    back_small, forward_small = sum_both(
+        jnp.concatenate([times_transposed(both, local_bcdt), squares], axis=1)
+    )
+
+    def xz_part(j):
+        cols = lax.dynamic_slice_in_dim(local_xz, (me ^ j) * 2 * width, 2 * width, 1)
+        return jnp.dot(both, cols, preferred_element_type=jnp.float32)
+
+    held_xz = sum_first(xz_part)
+    back_raw, back_first = sum_rest({j: x[:SEQ] for j, x in held_xz.items()})
+
+    def mixed_part(j):
+        taken = lax.dynamic_slice_in_dim(local_out, (me ^ j) * width, width, 0)
+        return times_transposed(cot_rows, taken)
+
+    d_mixed, mixed_first = sum_rest(sum_first(mixed_part), back_first)
+    forward_raw, forward_first = sum_rest(
+        {j: x[SEQ:] for j, x in held_xz.items()}, mixed_first
+    )
+
+    def project(rows, small, raw_xz):
         raw_cols = small[:, : MAPS + HEADS]
         scales = lax.rsqrt(small[:, MAPS + HEADS :] / D + 1e-05)
-        return (values, scales, raw_xz, raw_cols)
+        return (rows.astype(jnp.float32), scales, raw_xz, raw_cols)
+
+    back_proj = project(saved_rows, back_small, back_raw)
+    forward_proj = project(input_rows, forward_small, forward_raw)
 
     def gate_parts(projected):
         values, scales, raw_xz, raw_cols = projected
@@ -183,15 +219,6 @@
 
         gated, mix_back = jax.vjp(local_mix, mix_x, mix_z, own_dt, scores)
         return (gated, mix_back, maps, pre_part)
-
-    back_proj = project(saved_rows)
-
-    def mixed_part(j):
-        taken = lax.dynamic_slice_in_dim(local_out, (me ^ j) * width, width, 0)
-        return times_transposed(cot_rows, taken)
-
-    d_mixed = sum_scatter(mixed_part)
-    forward_proj = project(input_rows)
 
     values, scales, raw_xz, raw_cols = back_proj
     gated, mix_back, maps, pre_part = gate_parts(back_proj)
@@ -215,7 +242,7 @@
         .reshape(SEQ, own_heads * 2 * HEAD_DIM)
         .astype(jnp.bfloat16)
     )
-    round_xz = gather_cols(own_round)
+    round_xz, round_first = gather_cols(own_round)
     inner_own = jnp.sum(own_round.astype(jnp.float32) * raw_xz, axis=1, keepdims=True)
     wide_maps = maps.astype(jnp.float32)
     d_maps = jnp.concatenate(
@@ -239,7 +266,7 @@
     )
 
     fwd_gated = gate_parts(forward_proj)[0]
-    fwd_all = gather_cols((fwd_gated * gain_local).astype(jnp.bfloat16))
+    fwd_all, _ = gather_cols((fwd_gated * gain_local).astype(jnp.bfloat16), round_first)
     fwd_sum = sum_all(jnp.sum(fwd_gated * fwd_gated, axis=1)[None])
     fwd_inverse = lax.rsqrt(fwd_sum[0] / INNER + 1e-05)[:, None]
     mixed = jnp.dot(fwd_all, local_out, preferred_element_type=jnp.float32) * fwd_inverse
@@ -253,7 +280,7 @@
     d_input = (cot_rows.astype(jnp.float32) + d_norm_in).astype(jnp.bfloat16)
     prev_grad = from_behind(d_input, "section", -1)
 
-    grad_out = transposed_times(gather_cols(mixed_in), cot_rows)
+    grad_out = transposed_times(gather_cols(mixed_in, round_first)[0], cot_rows)
     grad_xz = transposed_times(normed, round_xz)
     grad_bcdt = transposed_times(round_bcdt, normed)
     return (next_act[None], prev_grad[None], grad_xz[None], grad_bcdt[None], grad_out[None])

time: 143 us -> 131 us (0.916)
  waiting for transfers between devices: 51.7 us -> 33.4 us
  local copies, waits for them, and re-layouts: 1.56 us -> 9.77 us
  matrix products: 54.2 us -> 49.2 us
  other arithmetic: 10.2 us -> 15.1 us
  starting transfers between devices: 23.3 us -> 21.1 us
    ppermute x28 -> x25, waiting for transfers between devices: 50.5 us -> 33.4 us  [swap(): return lax.ppermute(x, 'dp', [(i, i ^ mask) for i in range(length)])]
    dot_general x8 -> x4, matrix products: 21.4 us -> 11.7 us  [xz_part(): return jnp.dot(both, cols, preferred_element_type=jnp.float32)]
    mul x0 -> x2, local copies, waits for them, and re-layouts: none -> 4.16 us  [gate_parts(): own_xz = raw_xz * scales]
    ppermute x28 -> x25, starting transfers between devices: 19 us -> 15.9 us  [swap(): return lax.ppermute(x, 'dp', [(i, i ^ mask) for i in range(length)])]
    reduce_sum x1, other arithmetic: 0.38 us -> 2.82 us  [per_device(): jnp.sum(own_round.astype(jnp.float32) * raw_xz, axis=1, keepdims=True)]
    add x9 -> x5, other arithmetic: 1.99 us -> 0.06 us  [sum_all(): x = x + swap(x, bit)]
    convert_element_type x1, other arithmetic: 0.3 us -> 1.98 us  [per_device(): mixed_in = (gained * inverse).astype(jnp.bfloat16)]
    dot_general x9 -> x8, matrix products: 10.9 us -> 11.6 us  [times_transposed(): lax.dot_general(left, right, (((1,), (1,)), ((), ())), preferred_element_...]
  transfers between devices with their start and end apart: 30 -> 27, of which waited for: 11 -> 11; matrix products, arithmetic and copies ran while one was open for 41% -> 51% of each run, Pallas kernels for 0% -> 0%
where the time goes in v3:
time: 131 us; the launch traced here: 130 us
  matrix products  49.2 us (38%)
  waiting for transfers between devices  33.4 us (25%)
  starting transfers between devices  21.1 us (16%)
  other arithmetic  15.1 us (12%)
  local copies, waits for them, and re-layouts  9.77 us (7%)
  between operations  1.72 us (1%)
    ppermute x25, waiting for transfers between devices, swap(): return lax.ppermute(x, 'dp', [(i, i ^ mask) for i in range(length)])  33.4 us
    ppermute x25, starting transfers between devices, swap(): return lax.ppermute(x, 'dp', [(i, i ^ mask) for i in range(length)])  15.9 us
    dot_general x3, matrix products, transposed_times(): lax.dot_general(left, right, (((0,), (0,)), ((), ())), preferred_element_...  15 us
    dot_general x4, matrix products, xz_part(): return jnp.dot(both, cols, preferred_element_type=jnp.float32)  11.7 us
    dot_general x8, matrix products, times_transposed(): lax.dot_general(left, right, (((1,), (1,)), ((), ())), preferred_element_...  11.6 us
    dot_general x4, matrix products, mixer(): jnp.einsum('hts,shp->thp', weights, heads_in, precision=lax.Precision.HIGH)  6.37 us
    ppermute x2, starting transfers between devices, from_behind(): lax.ppermute(x, axis, [(i, (i + by) % length) for i in range(length)])  5.18 us
    mul x2, local copies, waits for them, and re-layouts, gate_parts(): own_xz = raw_xz * scales  4.16 us
  transfers between devices with their start and end apart: 27, of which 11 were waited for; matrix products, arithmetic and copies ran while one was open for 51% of the time, Pallas kernels for 0%

profile of v3, /device:TPU:0, one launch (start us, length us, event | category | flops | bytes accessed | tf_op | source)
XLA Modules:
  0.0 130.3 jit_solution(5187045410424552843)
XLA Ops:
  0.7 3.5 %convolution_convert_fusion = bf16[256,2048]{1,0:T(8,128)(2,1)} fusion(bf16[1,512,8192]{2,1,0:T(8,128)(2,1)} %param.15, s32[]{:T(128)S(6)} %select_n.195, bf16[128,512]{1,0:T(8,128)(2,1)} %bitcast.252, bf16[128,512]{1,0:T(8,128)(2,1)} %bitcast.244), kind=kOutput, calls=%fused_computation.6 | convolution fusion | flops 537919488 | bytes 3407876 | tf_op jit(solution)/shard_map/dot_general | solution.py:183
  4.6 3.3 %convolution_convert_fusion.1 = bf16[256,2048]{1,0:T(8,128)(2,1)} fusion(bf16[1,512,8192]{2,1,0:T(8,128)(2,1)} %param.15, s32[]{:T(128)S(6)} %select_n.193, bf16[128,512]{1,0:T(8,128)(2,1)S(1)} %bitcast.253, bf16[128,512]{1,0:T(8,128)(2,1)S(1)} %bitcast.245), kind=kOutput, calls=%fused_computation.7 | convolution fusion | flops 537919488 | bytes 3407876 | tf_op jit(solution)/shard_map/dot_general | solution.py:183
  9.0 1.7 %fusion.22 = bf16[128,1024]{0,1:T(8,128)(2,1)S(1)} fusion(bf16[1,4096,512]{2,1,0:T(8,128)(2,1)} %param.17, s32[]{:T(128)S(6)} %select_n.197, bf16[1,128,512]{2,1,0:T(8,128)(2,1)S(1)} %copy-done.5), kind=kOutput, calls=%fused_computation.39 | convolution fusion | flops 134348800 | bytes 1441796 | tf_op jit(solution)/shard_map/dot_general | solution.py:129
  10.8 2.4 %fusion.23 = bf16[128,1024]{0,1:T(8,128)(2,1)} fusion(bf16[1,4096,512]{2,1,0:T(8,128)(2,1)} %param.17, s32[]{:T(128)S(6)} %select_n.210, bf16[1,128,512]{2,1,0:T(8,128)(2,1)S(1)} %copy-done.5), kind=kOutput, calls=%fused_computation.40 | convolution fusion | flops 134348800 | bytes 1441796 | tf_op jit(solution)/shard_map/dot_general | solution.py:129
  13.8 2.6 %collective-permute-start.7 = (f32[128,321]{0,1:T(8,128)S(1)}, f32[128,321]{0,1:T(8,128)S(1)}, u32[]{:S(2)}, u32[]{:S(2)}) collective-permute-start(f32[128,321]{0,1:T(8,128)S(1)} %slice_select_fusion), channel_id=1, source_target_pairs={{0,2},{1,3},{2,0},{3,1},{4,6},{5,7},{6,4},{7,5},{8,10},{9,11},{10,... | collective-permute-start | bytes 493064 | tf_op jit(solution)/shard_map/ppermute | solution.py:22
  16.5 4.9 %collective-permute-done.7 = f32[128,321]{0,1:T(8,128)S(1)} collective-permute-done((f32[128,321]{0,1:T(8,128)S(1)}, f32[128,321]{0,1:T(8,128)S(1)}, u32[]{:S(2)}, u32[]{:S(2)}) %collective-permute-start.7) | collective-permute-done | bytes 164384 | tf_op jit(solution)/shard_map/ppermute | solution.py:22
  21.5 1.7 %add_convert_fusion.1 = bf16[128,1024]{0,1:T(8,128)(2,1)S(1)} fusion(bf16[128,1024]{0,1:T(8,128)(2,1)S(1)} %collective-permute-done.2, bf16[1,128,512]{2,1,0:T(8,128)(2,1)S(1)} %copy-done.5, bf16[1,4096,512]{2,1,0:T(8,128)(2,1)} %param.17, s32[]{:T(128)S(6)} %select_n.196), kind=kOutput, calls=%fused_computation.159 | convolution fusion | flops 134610944 | bytes 1703940 | tf_op jit(solution)/shard_map/dot_general | solution.py:129
  25.8 2.3 %add_convert_fusion = bf16[256,2048]{1,0:T(8,128)(2,1)S(1)} fusion(bf16[256,2048]{1,0:T(8,128)(2,1)S(1)} %collective-permute-done.1, bf16[1,512,8192]{2,1,0:T(8,128)(2,1)} %param.15, s32[]{:T(128)S(6)} %select_n.194, bf16[128,512]{1,0:T(8,128)(2,1)S(1)} %bitcast.256, bf16[128,512]{1,0:T(8,128)(2,1)S(1)} %bitcast.248), kind=kOutput, calls=%fused_computation.15 | convolution fusion | flops 538968064 | bytes 4456452 | tf_op jit(solution)/shard_map/dot_general | solution.py:183
  29.1 1.7 %collective-permute-start.3 = (bf16[128,2048]{1,0:T(8,128)(2,1)S(1)}, bf16[128,2048]{1,0:T(8,128)(2,1)S(1)}, u32[]{:S(2)}, u32[]{:S(2)}) collective-permute-start(bf16[128,2048]{1,0:T(8,128)(2,1)S(1)} %get-tuple-element.43), channel_id=1, source_target_pairs={{0,2},{1,3},{2,0},{3,1},{4,6},{5,7},{6,4},{7,5},{8,10},{9,11},{10,... | collective-permute-start | bytes 1572872 | tf_op jit(solution)/shard_map/ppermute | solution.py:22
  31.0 2.6 %convert_add_fusion = f32[256,2048]{1,0:T(8,128)S(1)} fusion(bf16[256,2048]{1,0:T(8,128)(2,1)} %collective-permute-done, bf16[1,512,8192]{2,1,0:T(8,128)(2,1)} %param.15, s32[]{:T(128)S(6)} %select_n.192, bf16[128,512]{1,0:T(8,128)(2,1)S(1)} %bitcast.257, bf16[128,512]{1,0:T(8,128)(2,1)S(1)} %bitcast.249), kind=kOutput, calls=%fused_computation.18 | convolution fusion | flops 538443776 | bytes 5505028 | tf_op jit(solution)/shard_map/dot_general | solution.py:183
  33.6 9.7 %collective-permute-done.3 = bf16[128,2048]{1,0:T(8,128)(2,1)S(1)} collective-permute-done((bf16[128,2048]{1,0:T(8,128)(2,1)S(1)}, bf16[128,2048]{1,0:T(8,128)(2,1)S(1)}, u32[]{:S(2)}, u32[]{:S(2)}) %collective-permute-start.3) | collective-permute-done | bytes 524320 | tf_op jit(solution)/shard_map/ppermute | solution.py:22
  45.3 2.5 %copy.26 = f32[128,2048]{0,1:T(8,128)} copy(f32[128,2048]{1,0:T(8,128)} %fusion.85) | data formatting | bytes 2097152 | tf_op jit(solution)/shard_map/mul | solution.py:207
  49.1 1.8 %collective-permute-start.4 = (bf16[128,1024]{0,1:T(8,128)(2,1)S(1)}, bf16[128,1024]{0,1:T(8,128)(2,1)S(1)}, u32[]{:S(2)}, u32[]{:S(2)}) collective-permute-start(bf16[128,1024]{0,1:T(8,128)(2,1)S(1)} %add_convert_fusion.1), channel_id=1, source_target_pairs={{0,2},{1,3},{2,0},{3,1},{4,6},{5,7},{6,4},{7,5},{8,10},{9,11},{10,... | collective-permute-start | bytes 786440 | tf_op jit(solution)/shard_map/ppermute | solution.py:22
  53.3 3.8 %collective-permute-done.4 = bf16[128,1024]{0,1:T(8,128)(2,1)S(1)} collective-permute-done((bf16[128,1024]{0,1:T(8,128)(2,1)S(1)}, bf16[128,1024]{0,1:T(8,128)(2,1)S(1)}, u32[]{:S(2)}, u32[]{:S(2)}) %collective-permute-start.4) | collective-permute-done | bytes 262176 | tf_op jit(solution)/shard_map/ppermute | solution.py:22
  57.1 1.7 %multiply_reduce_fusion.4 = (f32[128]{0:T(128)S(1)}, f32[128,1024]{0,1:T(8,128)S(1)}) fusion(f32[128,16,64]{0,2,1:T(8,128)S(1)} %get-tuple-element.24, f32[1024]{0:T(1024)S(1)} %bitcast.290, bf16[128,1024]{0,1:T(8,128)(2,1)S(1)} %collective-permute-done.4, bf16[128,1024]{0,1:T(8,128)(2,1)} %collective-permute-done.9, ...), kind=kOutput, calls=%fused_computation.135 | convolution fusion | flops 135135104 | bytes 2757124 | tf_op jit(solution)/shard_map/dot_general | solution.py:129
  60.0 1.8 %collective-permute-start.11 = (f32[2,128]{1,0:T(2,128)S(1)}, f32[2,128]{1,0:T(2,128)S(1)}, u32[]{:S(2)}, u32[]{:S(2)}) collective-permute-start(f32[2,128]{1,0:T(2,128)S(1)} %fusion.218), channel_id=1, source_target_pairs={{0,2},{1,3},{2,0},{3,1},{4,6},{5,7},{6,4},{7,5},{8,10},{9,11},{10,... | collective-permute-start | bytes 3080 | tf_op jit(solution)/shard_map/ppermute | solution.py:22
  63.7 2.0 %multiply_convert_fusion = (bf16[128,1024]{0,1:T(8,128)(2,1)}, f32[128,1024]{0,1:T(8,128)S(1)}) fusion(f32[128,16,64]{0,2,1:T(8,128)S(1)} %get-tuple-element.24, f32[128]{0:T(128)S(1)} %get-tuple-element.22, f32[1024]{0:T(1024)S(1)} %bitcast.291, f32[128]{0:T(128)S(1)} %slice_bitcast_fusion.2, f32[128]{0:T(128)S(1)} %get-tuple-element.21, ...), kind=kLoop, calls=%fused_computation.133 | loop fusion | flops 1703936 | bytes 2364928 | tf_op jit(solution)/shard_map/convert_element_type | solution.py:231
  69.3 1.8 %collective-permute-start.12 = (bf16[128,2048]{0,1:T(8,128)(2,1)S(1)}, bf16[128,2048]{0,1:T(8,128)(2,1)}, u32[]{:S(2)}, u32[]{:S(2)}) collective-permute-start(bf16[128,2048]{0,1:T(8,128)(2,1)S(1)} %bitcast.259), channel_id=1, source_target_pairs={{0,2},{1,3},{2,0},{3,1},{4,6},{5,7},{6,4},{7,5},{8,10},{9,11},{10,... | collective-permute-start | bytes 1572872 | tf_op jit(solution)/shard_map/ppermute | solution.py:22
  71.1 3.1 %fusion.87 = (f32[16,128]{1,0:T(8,128)S(1)}, f32[16,128]{1,0:T(8,128)S(1)}, f32[16,128]{1,0:T(8,128)S(1)}, f32[128,128]{1,0:T(8,128)S(1)}) fusion(f32[16,128]{1,0:T(8,128)S(1)} %copy-done.39, f32[128,128]{1,0:T(8,128)} %copy-done.19, f32[16,128]{1,0:T(8,128)S(1)} %copy-done.53, pred[128,128]{1,0:T(8,128)(4,1)S(1)} %iota_compare_fusion, ...), kind=kOutput, calls=%fused_computation.96 | convolution fusion | flops 105228288 | bytes 1769472 | tf_op jit(solution)/shard_map/transpose(jvp(hts,shp->thp))/dot_general | solution.py:122
  77.8 2.8 %multiply_reduce_fusion = (f32[128]{0:T(128)}, f32[128,2048]{1,0:T(8,128)}) fusion(bf16[128,2048]{1,0:T(8,128)(2,1)S(1)} %copy-done.7, bf16[128,2048]{1,0:T(8,128)(2,1)S(1)} %copy-done.9, f32[256,2048]{1,0:T(8,128)S(1)} %convert_add_fusion, f32[128]{0:T(128)S(1)} %copy-done.43, bf16[128,2048]{1,0:T(8,128)(2,1)} %collective-permute-done.5), kind=kLoop, calls=%fused_computation.74 | loop fusion | flops 2097024 | bytes 4719616 | tf_op jit(solution)/shard_map/reduce_sum | solution.py:246
  80.6 1.6 %copy.24 = f32[128,2048]{0,1:T(8,128)S(1)} copy(f32[128,2048]{1,0:T(8,128)} %get-tuple-element.34) | data formatting | bytes 2097152 | tf_op jit(solution)/shard_map/mul | solution.py:207
  82.3 1.4 %divide_multiply_fusion = f32[128,1024]{0,1:T(8,128)S(1)} fusion(f32[128,1024]{0,1:T(8,128)S(1)} %bitcast.271, f32[1024]{0:T(1024)S(1)} %bitcast.286, f32[1024]{0:T(1024)S(1)} %bitcast.289, f32[1024]{0:T(1024)S(1)} %bitcast.283, f32[1024]{0:T(1024)S(1)} %bitcast.280), kind=kLoop, calls=%fused_computation.157 | loop fusion | flops 1441792 | bytes 1064960 | tf_op jit(solution)/shard_map/jvp(jit(silu))/mul | solution.py:110
  86.5 1.4 %collective-permute-done.12 = bf16[128,2048]{0,1:T(8,128)(2,1)} collective-permute-done((bf16[128,2048]{0,1:T(8,128)(2,1)S(1)}, bf16[128,2048]{0,1:T(8,128)(2,1)}, u32[]{:S(2)}, u32[]{:S(2)}) %collective-permute-start.12) | collective-permute-done | bytes 524320 | tf_op jit(solution)/shard_map/ppermute | solution.py:22
  88.3 1.7 %collective-permute-start.22 = (f32[128,321]{0,1:T(8,128)S(1)}, f32[128,321]{0,1:T(8,128)S(1)}, u32[]{:S(2)}, u32[]{:S(2)}) collective-permute-start(f32[128,321]{0,1:T(8,128)S(1)} %fusion.221), channel_id=1, source_target_pairs={{0,2},{1,3},{2,0},{3,1},{4,6},{5,7},{6,4},{7,5},{8,10},{9,11},{10,... | collective-permute-start | bytes 493064 | tf_op jit(solution)/shard_map/ppermute | solution.py:22
  90.5 6.6 %collective-permute-done.13 = bf16[128,1024]{0,1:T(8,128)(2,1)S(1)} collective-permute-done((bf16[128,1024]{0,1:T(8,128)(2,1)S(1)}, bf16[128,1024]{0,1:T(8,128)(2,1)S(1)}, u32[]{:S(2)}, u32[]{:S(2)}) %collective-permute-start.13) | collective-permute-done | bytes 262176 | tf_op jit(solution)/shard_map/ppermute | solution.py:22
  97.2 3.6 %collective-permute-done.22 = f32[128,321]{0,1:T(8,128)S(1)} collective-permute-done((f32[128,321]{0,1:T(8,128)S(1)}, f32[128,321]{0,1:T(8,128)S(1)}, u32[]{:S(2)}, u32[]{:S(2)}) %collective-permute-start.22) | collective-permute-done | bytes 164384 | tf_op jit(solution)/shard_map/ppermute | solution.py:22
  105.3 1.6 %collective-permute-start.18 = (bf16[128,512]{1,0:T(8,128)(2,1)S(1)}, bf16[128,512]{1,0:T(8,128)(2,1)S(1)}, u32[]{:S(2)}, u32[]{:S(2)}) collective-permute-start(bf16[128,512]{1,0:T(8,128)(2,1)S(1)} %fusion.45), channel_id=1, source_target_pairs={{0,4},{4,8},{8,12},{12,16},{16,20},{20,24},{24,28},{28,0},{1,5},{5... | collective-permute-start | bytes 393224 | tf_op jit(solution)/shard_map/ppermute | solution.py:17
  107.0 5.3 %convolution_bitcast_fusion.1 = f32[1,4096,512]{2,1,0:T(8,128)} fusion(bf16[128,1024]{0,1:T(8,128)(2,1)S(1)} %get-tuple-element.38, bf16[128,1024]{0,1:T(8,128)(2,1)S(1)} %get-tuple-element.37, bf16[128,1024]{0,1:T(8,128)(2,1)S(1)} %get-tuple-element.36, bf16[128,1024]{0,1:T(8,128)(2,1)S(1)} %get-tuple-element.35, bf16[1,128,512]{2,1,0:T(8,128)(2,1)S(1)} %copy-done.5), kind=kOutput, calls=%fused_computation.3 | convolution fusion | flops 541065216 | bytes 9568256 | tf_op jit(solution)/shard_map/dot_general | solution.py:135
  112.4 1.4 %broadcast_select_fusion.7 = (bf16[128,2048]{0,1:T(8,128)(2,1)S(1)}, bf16[128,2048]{0,1:T(8,128)(2,1)S(1)}, bf16[128,2048]{0,1:T(8,128)(2,1)S(1)}, bf16[128,2048]{0,1:T(8,128)(2,1)S(1)}) fusion(pred[]{:T(512)S(6)} %ne.19, bf16[128,2048]{0,1:T(8,128)(2,1)S(1)} %collective-permute-done.19, bf16[128,2048]{0,1:T(8,128)(2,1)} %collective-permute-done.12, ...), kind=kLoop, calls=%fused_computation.167 | loop fusion | flops 2097152 | bytes 4194306 | tf_op jit(solution)/shard_map/jit(_where)/select_n | solution.py:92
  113.8 3.0 %fusion.42 = bf16[128,512]{1,0:T(8,128)(2,1)S(1)} fusion(f32[128,512]{1,0:T(8,128)S(1)} %fusion.133, bf16[1,512,8192]{2,1,0:T(8,128)(2,1)S(1)} %bitcast.251, bf16[128,2048]{0,1:T(8,128)(2,1)S(1)} %get-tuple-element.32, bf16[128,2048]{0,1:T(8,128)(2,1)S(1)} %get-tuple-element.31, bf16[128,2048]{0,1:T(8,128)(2,1)S(1)} %get-tuple-element.30, ...), kind=kOutput, calls=%fused_computation.47 | convolution fusion | flops 1082785792 | bytes 11142656 | tf_op jit(solution)/shard_map/dot_general | solution.py:129
  116.8 3.6 %collective-permute-start.23 = (bf16[128,512]{1,0:T(8,128)(2,1)S(1)}, bf16[128,512]{1,0:T(8,128)(2,1)S(1)}, u32[]{:S(2)}, u32[]{:S(2)}) collective-permute-start(bf16[128,512]{1,0:T(8,128)(2,1)S(1)} %fusion.42), channel_id=1, source_target_pairs={{0,28},{4,0},{8,4},{12,8},{16,12},{20,16},{24,20},{28,24},{1,29},{... | collective-permute-start | bytes 393224 | tf_op jit(solution)/shard_map/ppermute | solution.py:17
  120.4 8.6 %convolution_bitcast_fusion = f32[1,512,8192]{2,1,0:T(8,128)} fusion(bf16[128,2048]{0,1:T(8,128)(2,1)S(1)} %get-tuple-element.32, bf16[128,2048]{0,1:T(8,128)(2,1)S(1)} %get-tuple-element.31, bf16[128,2048]{0,1:T(8,128)(2,1)S(1)} %get-tuple-element.30, bf16[128,2048]{0,1:T(8,128)(2,1)S(1)} %get-tuple-element.29, f32[128]{0:T(128)S(1)} %copy-done.25, ...), kind=kOutput, calls=%fused_computation | convolution fusion | flops 1082327040 | bytes 19005952 | tf_op jit(solution)/shard_map/dot_general | solution.py:135
  (222 shorter events, 31.1 us)
Async XLA Ops:
  4.2 21.7 %collective-permute-start.1 = (bf16[256,2048]{1,0:T(8,128)(2,1)}, bf16[256,2048]{1,0:T(8,128)(2,1)S(1)}, u32[]{:S(2)}, u32[]{:S(2)}) collective-permute-start(bf16[256,2048]{1,0:T(8,128)(2,1)} %convolution_convert_fusion), channel_id=1, source_target_pairs={{0,1},{1,0},{2,3},{3,2},{4,5},{5,4},{6,7},{7,6},{8,9},{9,8},{10,11... | collective-permute-start | bytes 3145736 | tf_op jit(solution)/shard_map/ppermute | solution.py:22
  7.9 23.1 %collective-permute-start = (bf16[256,2048]{1,0:T(8,128)(2,1)}, bf16[256,2048]{1,0:T(8,128)(2,1)}, u32[]{:S(2)}, u32[]{:S(2)}) collective-permute-start(bf16[256,2048]{1,0:T(8,128)(2,1)} %convolution_convert_fusion.1), channel_id=1, source_target_pairs={{0,1},{1,0},{2,3},{3,2},{4,5},{5,4},{6,7},{7,6},{8,9},{9,8},{10,11... | collective-permute-start | bytes 3145736 | tf_op jit(solution)/shard_map/ppermute | solution.py:22
  8.5 5.2 %collective-permute-start.6 = (f32[256,321]{0,1:T(8,128)S(1)}, f32[256,321]{0,1:T(8,128)S(1)}, u32[]{:S(2)}, u32[]{:S(2)}) collective-permute-start(f32[256,321]{0,1:T(8,128)S(1)} %pad_maximum_fusion.4), channel_id=1, source_target_pairs={{0,1},{1,0},{2,3},{3,2},{4,5},{5,4},{6,7},{7,6},{8,9},{9,8},{10,11... | collective-permute-start | bytes 986120 | tf_op jit(solution)/shard_map/ppermute | solution.py:22
  10.6 10.8 %collective-permute-start.2 = (bf16[128,1024]{0,1:T(8,128)(2,1)S(1)}, bf16[128,1024]{0,1:T(8,128)(2,1)S(1)}, u32[]{:S(2)}, u32[]{:S(2)}) collective-permute-start(bf16[128,1024]{0,1:T(8,128)(2,1)S(1)} %fusion.22), channel_id=1, source_target_pairs={{0,1},{1,0},{2,3},{3,2},{4,5},{5,4},{6,7},{7,6},{8,9},{9,8},{10,11... | collective-permute-start | bytes 786440 | tf_op jit(solution)/shard_map/ppermute | solution.py:22
  13.1 40.1 %collective-permute-start.9 = (bf16[128,1024]{0,1:T(8,128)(2,1)}, bf16[128,1024]{0,1:T(8,128)(2,1)}, u32[]{:S(2)}, u32[]{:S(2)}) collective-permute-start(bf16[128,1024]{0,1:T(8,128)(2,1)} %fusion.23), channel_id=1, source_target_pairs={{0,1},{1,0},{2,3},{3,2},{4,5},{5,4},{6,7},{7,6},{8,9},{9,8},{10,11... | collective-permute-start | bytes 786440 | tf_op jit(solution)/shard_map/ppermute | solution.py:22
  13.7 53.5 %copy-start.17 = (f32[1,1,1024]{2,1,0:T(1,128)}, f32[1,1,1024]{2,1,0:T(1,128)S(1)}, u32[]{:S(2)}) copy-start(f32[1,1,1024]{2,1,0:T(1,128)S(1)} %get-tuple-element.60) | copy-start | bytes 12292
  13.8 7.5 %collective-permute-start.7 = (f32[128,321]{0,1:T(8,128)S(1)}, f32[128,321]{0,1:T(8,128)S(1)}, u32[]{:S(2)}, u32[]{:S(2)}) collective-permute-start(f32[128,321]{0,1:T(8,128)S(1)} %slice_select_fusion), channel_id=1, source_target_pairs={{0,2},{1,3},{2,0},{3,1},{4,6},{5,7},{6,4},{7,5},{8,10},{9,11},{10,... | collective-permute-start | bytes 493064 | tf_op jit(solution)/shard_map/ppermute | solution.py:22
  16.4 45.4 %copy-start.50 = (f32[16]{0:T(128)}, f32[16]{0:T(128)S(1)}, u32[]{:S(2)}) copy-start(f32[16]{0:T(128)S(1)} %negate_bitcast_fusion) | copy-start | bytes 196
  16.4 54.6 %copy-start.27 = (pred[128,128]{1,0:T(8,128)(4,1)}, pred[128,128]{1,0:T(8,128)(4,1)S(1)}, u32[]{:S(2)}) copy-start(pred[128,128]{1,0:T(8,128)(4,1)S(1)} %iota_compare_fusion) | copy-start | bytes 49156
  21.4 1.8 %collective-permute-start.8 = (f32[128,321]{0,1:T(8,128)S(1)}, f32[128,321]{0,1:T(8,128)S(1)}, u32[]{:S(2)}, u32[]{:S(2)}) collective-permute-start(f32[128,321]{0,1:T(8,128)S(1)} %fusion.239), channel_id=1, source_target_pairs={{0,1},{1,0},{2,3},{3,2},{4,5},{5,4},{6,7},{7,6},{8,9},{9,8},{10,11... | collective-permute-start | bytes 493064 | tf_op jit(solution)/shard_map/ppermute | solution.py:22
  25.1 40.8 %copy-start.19 = (f32[128,128]{1,0:T(8,128)}, f32[128,128]{1,0:T(8,128)S(1)}, u32[]{:S(2)}) copy-start(f32[128,128]{1,0:T(8,128)S(1)} %fusion.176) | copy-start | bytes 196612
  25.8 40.1 %copy-start.38 = (f32[16,128]{1,0:T(8,128)}, f32[16,128]{1,0:T(8,128)S(1)}, u32[]{:S(2)}) copy-start(f32[16,128]{1,0:T(8,128)S(1)} %get-tuple-element.66) | copy-start | bytes 24580
  29.1 14.3 %collective-permute-start.3 = (bf16[128,2048]{1,0:T(8,128)(2,1)S(1)}, bf16[128,2048]{1,0:T(8,128)(2,1)S(1)}, u32[]{:S(2)}, u32[]{:S(2)}) collective-permute-start(bf16[128,2048]{1,0:T(8,128)(2,1)S(1)} %get-tuple-element.43), channel_id=1, source_target_pairs={{0,2},{1,3},{2,0},{3,1},{4,6},{5,7},{6,4},{7,5},{8,10},{9,11},{10,... | collective-permute-start | bytes 1572872 | tf_op jit(solution)/shard_map/ppermute | solution.py:22
  49.1 8.0 %collective-permute-start.4 = (bf16[128,1024]{0,1:T(8,128)(2,1)S(1)}, bf16[128,1024]{0,1:T(8,128)(2,1)S(1)}, u32[]{:S(2)}, u32[]{:S(2)}) collective-permute-start(bf16[128,1024]{0,1:T(8,128)(2,1)S(1)} %add_convert_fusion.1), channel_id=1, source_target_pairs={{0,2},{1,3},{2,0},{3,1},{4,6},{5,7},{6,4},{7,5},{8,10},{9,11},{10,... | collective-permute-start | bytes 786440 | tf_op jit(solution)/shard_map/ppermute | solution.py:22
  58.8 1.2 collective-permute-start.10
  60.0 3.6 %collective-permute-start.11 = (f32[2,128]{1,0:T(2,128)S(1)}, f32[2,128]{1,0:T(2,128)S(1)}, u32[]{:S(2)}, u32[]{:S(2)}) collective-permute-start(f32[2,128]{1,0:T(2,128)S(1)} %fusion.218), channel_id=1, source_target_pairs={{0,2},{1,3},{2,0},{3,1},{4,6},{5,7},{6,4},{7,5},{8,10},{9,11},{10,... | collective-permute-start | bytes 3080 | tf_op jit(solution)/shard_map/ppermute | solution.py:22
  62.6 15.1 %collective-permute-start.5 = (bf16[128,2048]{1,0:T(8,128)(2,1)}, bf16[128,2048]{1,0:T(8,128)(2,1)}, u32[]{:S(2)}, u32[]{:S(2)}) collective-permute-start(bf16[128,2048]{1,0:T(8,128)(2,1)} %get-tuple-element.10), channel_id=1, source_target_pairs={{0,2},{1,3},{2,0},{3,1},{4,6},{5,7},{6,4},{7,5},{8,10},{9,11},{10,... | collective-permute-start | bytes 1572872 | tf_op jit(solution)/shard_map/ppermute | solution.py:22
  69.3 18.7 %collective-permute-start.12 = (bf16[128,2048]{0,1:T(8,128)(2,1)S(1)}, bf16[128,2048]{0,1:T(8,128)(2,1)}, u32[]{:S(2)}, u32[]{:S(2)}) collective-permute-start(bf16[128,2048]{0,1:T(8,128)(2,1)S(1)} %bitcast.259), channel_id=1, source_target_pairs={{0,2},{1,3},{2,0},{3,1},{4,6},{5,7},{6,4},{7,5},{8,10},{9,11},{10,... | collective-permute-start | bytes 1572872 | tf_op jit(solution)/shard_map/ppermute | solution.py:22
  74.1 38.2 %collective-permute-start.20 = (bf16[128,2048]{0,1:T(8,128)(2,1)S(1)}, bf16[128,2048]{0,1:T(8,128)(2,1)}, u32[]{:S(2)}, u32[]{:S(2)}) collective-permute-start(bf16[128,2048]{0,1:T(8,128)(2,1)S(1)} %bitcast.260), channel_id=1, source_target_pairs={{0,1},{1,0},{2,3},{3,2},{4,5},{5,4},{6,7},{7,6},{8,9},{9,8},{10,11... | collective-permute-start | bytes 1572872 | tf_op jit(solution)/shard_map/ppermute | solution.py:22
  85.0 1.2 collective-permute-start.16
  85.4 2.9 %collective-permute-start.21 = (f32[128,321]{0,1:T(8,128)S(1)}, f32[128,321]{0,1:T(8,128)S(1)}, u32[]{:S(2)}, u32[]{:S(2)}) collective-permute-start(f32[128,321]{0,1:T(8,128)S(1)} %pad_maximum_fusion.6), channel_id=1, source_target_pairs={{0,1},{1,0},{2,3},{3,2},{4,5},{5,4},{6,7},{7,6},{8,9},{9,8},{10,11... | collective-permute-start | bytes 493064 | tf_op jit(solution)/shard_map/ppermute | solution.py:22
  86.2 3.8 %collective-permute-start.17 = (f32[1,128]{1,0:T(1,128)S(1)}, f32[1,128]{1,0:T(1,128)S(1)}, u32[]{:S(2)}, u32[]{:S(2)}) collective-permute-start(f32[1,128]{1,0:T(1,128)S(1)} %bitcast_add_fusion), channel_id=1, source_target_pairs={{0,2},{1,3},{2,0},{3,1},{4,6},{5,7},{6,4},{7,5},{8,10},{9,11},{10,... | collective-permute-start | bytes 1544 | tf_op jit(solution)/shard_map/ppermute | solution.py:22
  87.9 9.2 %collective-permute-start.13 = (bf16[128,1024]{0,1:T(8,128)(2,1)S(1)}, bf16[128,1024]{0,1:T(8,128)(2,1)S(1)}, u32[]{:S(2)}, u32[]{:S(2)}) collective-permute-start(bf16[128,1024]{0,1:T(8,128)(2,1)S(1)} %fusion.112), channel_id=1, source_target_pairs={{0,2},{1,3},{2,0},{3,1},{4,6},{5,7},{6,4},{7,5},{8,10},{9,11},{10,... | collective-permute-start | bytes 786440 | tf_op jit(solution)/shard_map/ppermute | solution.py:22
  88.3 12.5 %collective-permute-start.22 = (f32[128,321]{0,1:T(8,128)S(1)}, f32[128,321]{0,1:T(8,128)S(1)}, u32[]{:S(2)}, u32[]{:S(2)}) collective-permute-start(f32[128,321]{0,1:T(8,128)S(1)} %fusion.221), channel_id=1, source_target_pairs={{0,2},{1,3},{2,0},{3,1},{4,6},{5,7},{6,4},{7,5},{8,10},{9,11},{10,... | collective-permute-start | bytes 493064 | tf_op jit(solution)/shard_map/ppermute | solution.py:22
  90.1 12.7 %collective-permute-start.15 = (bf16[128,1024]{0,1:T(8,128)(2,1)S(1)}, bf16[128,1024]{0,1:T(8,128)(2,1)S(1)}, u32[]{:S(2)}, u32[]{:S(2)}) collective-permute-start(bf16[128,1024]{0,1:T(8,128)(2,1)S(1)} %fusion.112), channel_id=1, source_target_pairs={{0,1},{1,0},{2,3},{3,2},{4,5},{5,4},{6,7},{7,6},{8,9},{9,8},{10,11... | collective-permute-start | bytes 786440 | tf_op jit(solution)/shard_map/ppermute | solution.py:22
  90.1 14.3 %collective-permute-start.24 = (bf16[128,1024]{0,1:T(8,128)(2,1)S(1)}, bf16[128,1024]{0,1:T(8,128)(2,1)S(1)}, u32[]{:S(2)}, u32[]{:S(2)}) collective-permute-start(bf16[128,1024]{0,1:T(8,128)(2,1)S(1)} %copy-done.10), channel_id=1, source_target_pairs={{0,2},{1,3},{2,0},{3,1},{4,6},{5,7},{6,4},{7,5},{8,10},{9,11},{10,... | collective-permute-start | bytes 786440 | tf_op jit(solution)/shard_map/ppermute | solution.py:22
  97.2 9.7 %collective-permute-start.26 = (bf16[128,1024]{0,1:T(8,128)(2,1)S(1)}, bf16[128,1024]{0,1:T(8,128)(2,1)S(1)}, u32[]{:S(2)}, u32[]{:S(2)}) collective-permute-start(bf16[128,1024]{0,1:T(8,128)(2,1)S(1)} %copy-done.10), channel_id=1, source_target_pairs={{0,1},{1,0},{2,3},{3,2},{4,5},{5,4},{6,7},{7,6},{8,9},{9,8},{10,11... | collective-permute-start | bytes 786440 | tf_op jit(solution)/shard_map/ppermute | solution.py:22
  100.8 3.6 %collective-permute-start.14 = (bf16[128,1024]{0,1:T(8,128)(2,1)S(1)}, bf16[128,1024]{0,1:T(8,128)(2,1)S(1)}, u32[]{:S(2)}, u32[]{:S(2)}) collective-permute-start(bf16[128,1024]{0,1:T(8,128)(2,1)S(1)} %collective-permute-done.13), channel_id=1, source_target_pairs={{0,1},{1,0},{2,3},{3,2},{4,5},{5,4},{6,7},{7,6},{8,9},{9,8},{10,11... | collective-permute-start | bytes 786440 | tf_op jit(solution)/shard_map/ppermute | solution.py:22
  102.8 9.6 %collective-permute-start.19 = (bf16[128,2048]{0,1:T(8,128)(2,1)}, bf16[128,2048]{0,1:T(8,128)(2,1)S(1)}, u32[]{:S(2)}, u32[]{:S(2)}) collective-permute-start(bf16[128,2048]{0,1:T(8,128)(2,1)} %collective-permute-done.12), channel_id=1, source_target_pairs={{0,1},{1,0},{2,3},{3,2},{4,5},{5,4},{6,7},{7,6},{8,9},{9,8},{10,11... | collective-permute-start | bytes 1572872 | tf_op jit(solution)/shard_map/ppermute | solution.py:22
  104.4 2.5 %collective-permute-start.25 = (bf16[128,1024]{0,1:T(8,128)(2,1)S(1)}, bf16[128,1024]{0,1:T(8,128)(2,1)S(1)}, u32[]{:S(2)}, u32[]{:S(2)}) collective-permute-start(bf16[128,1024]{0,1:T(8,128)(2,1)S(1)} %collective-permute-done.24), channel_id=1, source_target_pairs={{0,1},{1,0},{2,3},{3,2},{4,5},{5,4},{6,7},{7,6},{8,9},{9,8},{10,11... | collective-permute-start | bytes 786440 | tf_op jit(solution)/shard_map/ppermute | solution.py:22
  105.3 23.7 %collective-permute-start.18 = (bf16[128,512]{1,0:T(8,128)(2,1)S(1)}, bf16[128,512]{1,0:T(8,128)(2,1)S(1)}, u32[]{:S(2)}, u32[]{:S(2)}) collective-permute-start(bf16[128,512]{1,0:T(8,128)(2,1)S(1)} %fusion.45), channel_id=1, source_target_pairs={{0,4},{4,8},{8,12},{12,16},{16,20},{20,24},{24,28},{28,0},{1,5},{5... | collective-permute-start | bytes 393224 | tf_op jit(solution)/shard_map/ppermute | solution.py:17
  116.8 12.2 %collective-permute-start.23 = (bf16[128,512]{1,0:T(8,128)(2,1)S(1)}, bf16[128,512]{1,0:T(8,128)(2,1)S(1)}, u32[]{:S(2)}, u32[]{:S(2)}) collective-permute-start(bf16[128,512]{1,0:T(8,128)(2,1)S(1)} %fusion.42), channel_id=1, source_target_pairs={{0,28},{4,0},{8,4},{12,8},{16,12},{20,16},{24,20},{28,24},{1,29},{... | collective-permute-start | bytes 393224 | tf_op jit(solution)/shard_map/ppermute | solution.py:17
  (52 other events, 362.7 us)

commit v4 on v3

--- a/solution.py
+++ b/solution.py
@@ -49,7 +49,7 @@
 
 
 def sum_rest(held, after=None):
-    first = None
+    first = begun = None
     for bit in masks()[1:]:
         sent = {j: held[j].astype(jnp.bfloat16) for j in held if j & bit}
         if after is not None and first is None:
@@ -57,15 +57,16 @@
         came = {j ^ bit: swap(x, bit) for j, x in sent.items()}
         if first is None:
             first = came[0]
+            begun = sent[bit]
         held = {j: held[j] + came[j].astype(jnp.float32) for j in came}
-    return held[0], first
-
-
-def sum_both(x):
+    return held[0], first, begun
+
+
+def sum_both(x, after):
     me = lax.axis_index("dp")
     odd = (me & 1) != 0
     x = x + swap(x, 1)
-    mine = jnp.where(odd, x[SEQ:], x[:SEQ])
+    mine = tied(jnp.where(odd, x[SEQ:], x[:SEQ]), after)
     for bit in masks()[1:]:
         mine = mine + swap(mine, bit)
     other = swap(mine, 1)
@@ -79,18 +80,15 @@
         block = tied(block, after)
     held = [block]
     order = [0]
-    first = None
     for bit in reversed(masks()):
         held = held + [swap(b, bit) for b in held]
         order = order + [j ^ bit for j in order]
-        if first is None:
-            first = held[1]
     by_mask = {j: b for j, b in zip(order, held)}
     level = [by_mask[j] for j in range(length)]
     for bit in masks():
         flip = (me & bit) != 0
         level = [jnp.where(flip, level[j ^ bit], level[j]) for j in range(length)]
-    return jnp.concatenate(level, axis=1), first
+    return jnp.concatenate(level, axis=1), held[-1]
 
 
 def causal_conv(values, kernel_taps):
@@ -174,25 +172,22 @@
     both = jnp.concatenate([saved_rows, input_rows], axis=0)
     both_values = both.astype(jnp.float32)
     squares = jnp.sum(both_values * both_values, axis=1, keepdims=True)
-    back_small, forward_small = sum_both(
-        jnp.concatenate([times_transposed(both, local_bcdt), squares], axis=1)
-    )
-
     def xz_part(j):
         cols = lax.dynamic_slice_in_dim(local_xz, (me ^ j) * 2 * width, 2 * width, 1)
         return jnp.dot(both, cols, preferred_element_type=jnp.float32)
 
     held_xz = sum_first(xz_part)
-    back_raw, back_first = sum_rest({j: x[:SEQ] for j, x in held_xz.items()})
+    back_raw, back_first, back_begun = sum_rest({j: x[:SEQ] for j, x in held_xz.items()})
+    back_small, forward_small = sum_both(
+        jnp.concatenate([times_transposed(both, local_bcdt), squares], axis=1), back_begun
+    )
 
     def mixed_part(j):
         taken = lax.dynamic_slice_in_dim(local_out, (me ^ j) * width, width, 0)
         return times_transposed(cot_rows, taken)
 
-    d_mixed, mixed_first = sum_rest(sum_first(mixed_part), back_first)
-    forward_raw, forward_first = sum_rest(
-        {j: x[SEQ:] for j, x in held_xz.items()}, mixed_first
-    )
+    d_mixed = sum_rest(sum_first(mixed_part), back_begun)[0]
+    forward_raw = sum_rest({j: x[SEQ:] for j, x in held_xz.items()}, back_first)[0]
 
     def project(rows, small, raw_xz):
         raw_cols = small[:, : MAPS + HEADS]
@@ -242,7 +237,7 @@
         .reshape(SEQ, own_heads * 2 * HEAD_DIM)
         .astype(jnp.bfloat16)
     )
-    round_xz, round_first = gather_cols(own_round)
+    round_xz, round_last = gather_cols(own_round)
     inner_own = jnp.sum(own_round.astype(jnp.float32) * raw_xz, axis=1, keepdims=True)
     wide_maps = maps.astype(jnp.float32)
     d_maps = jnp.concatenate(
@@ -266,7 +261,7 @@
     )
 
     fwd_gated = gate_parts(forward_proj)[0]
-    fwd_all, _ = gather_cols((fwd_gated * gain_local).astype(jnp.bfloat16), round_first)
+    fwd_all, _ = gather_cols((fwd_gated * gain_local).astype(jnp.bfloat16), round_last)
     fwd_sum = sum_all(jnp.sum(fwd_gated * fwd_gated, axis=1)[None])
     fwd_inverse = lax.rsqrt(fwd_sum[0] / INNER + 1e-05)[:, None]
     mixed = jnp.dot(fwd_all, local_out, preferred_element_type=jnp.float32) * fwd_inverse
@@ -280,7 +275,7 @@
     d_input = (cot_rows.astype(jnp.float32) + d_norm_in).astype(jnp.bfloat16)
     prev_grad = from_behind(d_input, "section", -1)
 
-    grad_out = transposed_times(gather_cols(mixed_in, round_first)[0], cot_rows)
+    grad_out = transposed_times(gather_cols(mixed_in, round_last)[0], cot_rows)
     grad_xz = transposed_times(normed, round_xz)
     grad_bcdt = transposed_times(round_bcdt, normed)
     return (next_act[None], prev_grad[None], grad_xz[None], grad_bcdt[None], grad_out[None])

time: 131 us -> 116 us (0.89)
  waiting for transfers between devices: 33.4 us -> 16.4 us
  matrix products: 49.2 us -> 51.3 us
  other arithmetic: 15.1 us -> 16.6 us
    ppermute x25, waiting for transfers between devices: 33.4 us -> 13.2 us  [swap(): return lax.ppermute(x, 'dp', [(i, i ^ mask) for i in range(length)])]
    ppermute x2, waiting for transfers between devices: 0.01 us -> 3.27 us  [from_behind(): lax.ppermute(x, axis, [(i, (i + by) % length) for i in range(length)])]
    dot_general x8, matrix products: 11.6 us -> 13.1 us  [times_transposed(): lax.dot_general(left, right, (((1,), (1,)), ((), ())), preferred_element_...]
    dot_general x3, matrix products: 1.84 us -> 3.2 us  [mixer(): jnp.dot(causal.astype(jnp.float32), steps * -jnp.exp(log_rate), precision...]
  transfers between devices with their start and end apart: 27 -> 27, of which waited for: 11 -> 10; matrix products, arithmetic and copies ran while one was open for 51% -> 61% of each run, Pallas kernels for 0% -> 0%
where the time goes in v4:
time: 116 us; the launch traced here: 115 us
  matrix products  51.3 us (44%)
  starting transfers between devices  19.8 us (17%)
  other arithmetic  16.6 us (14%)
  waiting for transfers between devices  16.4 us (14%)
  local copies, waits for them, and re-layouts  9.6 us (8%)
  between operations  1.75 us (2%)
    ppermute x25, starting transfers between devices, swap(): return lax.ppermute(x, 'dp', [(i, i ^ mask) for i in range(length)])  15.2 us
    dot_general x3, matrix products, transposed_times(): lax.dot_general(left, right, (((0,), (0,)), ((), ())), preferred_element_...  14.4 us
    ppermute x25, waiting for transfers between devices, swap(): return lax.ppermute(x, 'dp', [(i, i ^ mask) for i in range(length)])  13.2 us
    dot_general x8, matrix products, times_transposed(): lax.dot_general(left, right, (((1,), (1,)), ((), ())), preferred_element_...  13.1 us
    dot_general x4, matrix products, xz_part(): return jnp.dot(both, cols, preferred_element_type=jnp.float32)  11.7 us
    dot_general x4, matrix products, mixer(): jnp.einsum('hts,shp->thp', weights, heads_in, precision=lax.Precision.HIGH)  6.38 us
    ppermute x2, starting transfers between devices, from_behind(): lax.ppermute(x, axis, [(i, (i + by) % length) for i in range(length)])  4.63 us
    mul x2, local copies, waits for them, and re-layouts, gate_parts(): own_xz = raw_xz * scales  4.17 us
  transfers between devices with their start and end apart: 27, of which 10 were waited for; matrix products, arithmetic and copies ran while one was open for 61% of the time, Pallas kernels for 0%

profile of v4, /device:TPU:0, one launch (start us, length us, event | category | flops | bytes accessed | tf_op | source)
XLA Modules:
  0.0 115.4 jit_solution(6685426655422182000)
XLA Ops:
  0.7 3.5 %convolution_convert_fusion = bf16[256,2048]{1,0:T(8,128)(2,1)} fusion(bf16[1,512,8192]{2,1,0:T(8,128)(2,1)} %param.15, s32[]{:T(128)S(6)} %select_n.195, bf16[128,512]{1,0:T(8,128)(2,1)} %bitcast.252, bf16[128,512]{1,0:T(8,128)(2,1)} %bitcast.244), kind=kOutput, calls=%fused_computation.6 | convolution fusion | flops 537919488 | bytes 3407876 | tf_op jit(solution)/shard_map/dot_general | solution.py:177
  4.6 3.3 %convolution_convert_fusion.1 = bf16[256,2048]{1,0:T(8,128)(2,1)} fusion(bf16[1,512,8192]{2,1,0:T(8,128)(2,1)} %param.15, s32[]{:T(128)S(6)} %select_n.193, bf16[128,512]{1,0:T(8,128)(2,1)S(1)} %bitcast.253, bf16[128,512]{1,0:T(8,128)(2,1)S(1)} %bitcast.245), kind=kOutput, calls=%fused_computation.7 | convolution fusion | flops 537919488 | bytes 3407876 | tf_op jit(solution)/shard_map/dot_general | solution.py:177
  9.0 1.7 %fusion.23 = bf16[128,1024]{0,1:T(8,128)(2,1)S(1)} fusion(bf16[1,4096,512]{2,1,0:T(8,128)(2,1)} %param.17, s32[]{:T(128)S(6)} %select_n.210, bf16[1,128,512]{2,1,0:T(8,128)(2,1)S(1)} %copy-done.5), kind=kOutput, calls=%fused_computation.40 | convolution fusion | flops 134348800 | bytes 1441796 | tf_op jit(solution)/shard_map/dot_general | solution.py:127
  10.8 2.4 %fusion.22 = bf16[128,1024]{0,1:T(8,128)(2,1)} fusion(bf16[1,4096,512]{2,1,0:T(8,128)(2,1)} %param.17, s32[]{:T(128)S(6)} %select_n.208, bf16[1,128,512]{2,1,0:T(8,128)(2,1)S(1)} %copy-done.5), kind=kOutput, calls=%fused_computation.39 | convolution fusion | flops 134348800 | bytes 1441796 | tf_op jit(solution)/shard_map/dot_general | solution.py:127
  15.0 2.3 %add_convert_fusion = bf16[256,2048]{1,0:T(8,128)(2,1)S(1)} fusion(bf16[256,2048]{1,0:T(8,128)(2,1)S(1)} %collective-permute-done.1, bf16[1,512,8192]{2,1,0:T(8,128)(2,1)} %param.15, s32[]{:T(128)S(6)} %select_n.194, bf16[128,512]{1,0:T(8,128)(2,1)S(1)} %bitcast.256, bf16[128,512]{1,0:T(8,128)(2,1)S(1)} %bitcast.248), kind=kOutput, calls=%fused_computation.15 | convolution fusion | flops 538968064 | bytes 4456452 | tf_op jit(solution)/shard_map/dot_general | solution.py:177
  18.2 2.5 %collective-permute-start.5 = (f32[128,321]{0,1:T(8,128)S(1)}, f32[128,321]{0,1:T(8,128)S(1)}, u32[]{:S(2)}, u32[]{:S(2)}) collective-permute-start(f32[128,321]{0,1:T(8,128)S(1)} %slice_select_fusion), channel_id=1, source_target_pairs={{0,2},{1,3},{2,0},{3,1},{4,6},{5,7},{6,4},{7,5},{8,10},{9,11},{10,... | collective-permute-start | bytes 493064 | tf_op jit(solution)/shard_map/ppermute | solution.py:22
  20.7 2.4 %add_convert_fusion.1 = bf16[128,1024]{0,1:T(8,128)(2,1)} fusion(bf16[128,1024]{0,1:T(8,128)(2,1)S(1)} %collective-permute-done.8, bf16[1,128,512]{2,1,0:T(8,128)(2,1)S(1)} %copy-done.5, bf16[1,4096,512]{2,1,0:T(8,128)(2,1)} %param.17, s32[]{:T(128)S(6)} %select_n.209), kind=kOutput, calls=%fused_computation.137 | convolution fusion | flops 134610944 | bytes 1703940 | tf_op jit(solution)/shard_map/dot_general | solution.py:127
  23.1 2.0 %collective-permute-start.9 = (bf16[128,1024]{0,1:T(8,128)(2,1)}, bf16[128,1024]{0,1:T(8,128)(2,1)}, u32[]{:S(2)}, u32[]{:S(2)}) collective-permute-start(bf16[128,1024]{0,1:T(8,128)(2,1)} %add_convert_fusion.1), channel_id=1, source_target_pairs={{0,2},{1,3},{2,0},{3,1},{4,6},{5,7},{6,4},{7,5},{8,10},{9,11},{10,... | collective-permute-start | bytes 786440 | tf_op jit(solution)/shard_map/ppermute | solution.py:22
  25.8 2.6 %convert_add_fusion = f32[256,2048]{1,0:T(8,128)S(1)} fusion(bf16[256,2048]{1,0:T(8,128)(2,1)} %collective-permute-done, bf16[1,512,8192]{2,1,0:T(8,128)(2,1)} %param.15, s32[]{:T(128)S(6)} %select_n.192, bf16[128,512]{1,0:T(8,128)(2,1)S(1)} %bitcast.257, bf16[128,512]{1,0:T(8,128)(2,1)S(1)} %bitcast.249), kind=kOutput, calls=%fused_computation.18 | convolution fusion | flops 538443776 | bytes 5505028 | tf_op jit(solution)/shard_map/dot_general | solution.py:177
  33.3 4.6 %collective-permute-done.2 = bf16[128,2048]{1,0:T(8,128)(2,1)S(1)} collective-permute-done((bf16[128,2048]{1,0:T(8,128)(2,1)S(1)}, bf16[128,2048]{1,0:T(8,128)(2,1)S(1)}, u32[]{:S(2)}, u32[]{:S(2)}) %collective-permute-start.2) | collective-permute-done | bytes 524320 | tf_op jit(solution)/shard_map/ppermute | solution.py:22
  39.0 2.6 %copy.26 = f32[128,2048]{0,1:T(8,128)} copy(f32[128,2048]{1,0:T(8,128)} %fusion.85) | data formatting | bytes 2097152 | tf_op jit(solution)/shard_map/mul | solution.py:202
  42.8 1.4 %fusion.122 = (f32[128,1024]{0,1:T(8,128)S(1)}, f32[128,1024]{0,1:T(8,128)S(1)}) fusion(f32[128,1024]{0,1:T(8,128)S(1)} %bitcast.270, f32[1024]{0:T(1024)S(1)} %bitcast.284, f32[1024]{0:T(1024)S(1)} %bitcast.287, f32[1024]{0:T(1024)S(1)} %bitcast.281, f32[1024]{0:T(1024)S(1)} %bitcast.278), kind=kLoop, calls=%fused_computation.150 | loop fusion | flops 1441792 | bytes 1589248 | tf_op jit(solution)/shard_map/jvp(jit(silu))/mul | solution.py:108
  44.2 1.2 %multiply_reduce_fusion.5 = (f32[128]{0:T(128)S(1)}, f32[128,16,64]{0,2,1:T(8,128)S(1)}, f32[128,16,64]{0,2,1:T(8,128)S(1)}) fusion(f32[128,16,2,64]{0,3,2,1:T(8,128)S(1)} %bitcast.263, f32[128,16,64]{0,2,1:T(8,128)S(1)} %bitcast.273, f32[16]{0:T(128)S(1)} %bitcast.315, f32[16,128]{1,0:T(8,128)S(1)} %copy-done.40, f32[128,128]{1,0:T(8,128)S(1)} %copy-done.21, ...), kind=kOutput, calls=%fused_computation.138 | convolution fusion | flops 103153536 | bytes 2728960 | tf_op jit(solution)/shard_map/jvp(hts,shp->thp)/dot_general | solution.py:120
  45.5 1.8 %multiply_reduce_fusion.4 = (f32[128]{0:T(128)S(1)}, f32[128,1024]{0,1:T(8,128)S(1)}) fusion(f32[128,16,64]{0,2,1:T(8,128)S(1)} %get-tuple-element.26, f32[1024]{0:T(1024)S(1)} %bitcast.290, bf16[128,1024]{0,1:T(8,128)(2,1)} %collective-permute-done.9, bf16[128,1024]{0,1:T(8,128)(2,1)} %collective-permute-done.7, bf16[1,128,512]{2,1,0:T(8,128)(2,1)S(1)} %copy-done.5, ...), kind=kOutput, calls=%fused_computation.135 | convolution fusion | flops 135135104 | bytes 2757124 | tf_op jit(solution)/shard_map/dot_general | solution.py:127
  48.6 1.3 %collective-permute-start.11 = (f32[2,128]{1,0:T(2,128)S(1)}, f32[2,128]{1,0:T(2,128)S(1)}, u32[]{:S(2)}, u32[]{:S(2)}) collective-permute-start(f32[2,128]{1,0:T(2,128)S(1)} %fusion.218), channel_id=1, source_target_pairs={{0,2},{1,3},{2,0},{3,1},{4,6},{5,7},{6,4},{7,5},{8,10},{9,11},{10,... | collective-permute-start | bytes 3080 | tf_op jit(solution)/shard_map/ppermute | solution.py:22
  49.8 1.5 %fusion.170 = f32[16,128]{1,0:T(8,128)} fusion(f32[16]{0:T(128)S(1)} %copy-done.54, f32[128,64]{0,1:T(8,128)} %copy-done.23, s32[]{:T(128)S(6)} %select_n.199, f32[16]{0:T(128)S(1)} %bitcast.313), kind=kOutput, calls=%fused_computation.252 | convolution fusion | flops 3178496 | bytes 16516 | tf_op jit(solution)/shard_map/jvp()/dot_general | solution.py:112
  52.2 2.1 %multiply_convert_fusion = (bf16[128,1024]{0,1:T(8,128)(2,1)}, f32[128,1024]{0,1:T(8,128)S(1)}) fusion(f32[128,16,64]{0,2,1:T(8,128)S(1)} %get-tuple-element.26, f32[128]{0:T(128)S(1)} %get-tuple-element.24, f32[1024]{0:T(1024)S(1)} %bitcast.291, f32[128]{0:T(128)S(1)} %slice_bitcast_fusion.2, f32[128]{0:T(128)S(1)} %get-tuple-element.23, ...), kind=kLoop, calls=%fused_computation.133 | loop fusion | flops 1703936 | bytes 2364928 | tf_op jit(solution)/shard_map/convert_element_type | solution.py:226
  57.9 1.3 %collective-permute-start.12 = (bf16[128,2048]{0,1:T(8,128)(2,1)S(1)}, bf16[128,2048]{0,1:T(8,128)(2,1)}, u32[]{:S(2)}, u32[]{:S(2)}) collective-permute-start(bf16[128,2048]{0,1:T(8,128)(2,1)S(1)} %bitcast.259), channel_id=1, source_target_pairs={{0,2},{1,3},{2,0},{3,1},{4,6},{5,7},{6,4},{7,5},{8,10},{9,11},{10,... | collective-permute-start | bytes 1572872 | tf_op jit(solution)/shard_map/ppermute | solution.py:22
  59.1 3.1 %fusion.87 = (f32[16,128]{1,0:T(8,128)S(1)}, f32[16,128]{1,0:T(8,128)S(1)}, f32[16,128]{1,0:T(8,128)S(1)}, f32[128,128]{1,0:T(8,128)S(1)}) fusion(f32[16,128]{1,0:T(8,128)S(1)} %copy-done.41, f32[128,128]{1,0:T(8,128)} %fusion.176, f32[16,128]{1,0:T(8,128)S(1)} %copy-done.57, pred[128,128]{1,0:T(8,128)(4,1)S(1)} %copy-done.29, ...), kind=kOutput, calls=%fused_computation.96 | convolution fusion | flops 105228288 | bytes 1769472 | tf_op jit(solution)/shard_map/transpose(jvp(hts,shp->thp))/dot_general | solution.py:120
  64.8 1.7 %collective-permute-done.3 = bf16[128,2048]{1,0:T(8,128)(2,1)} collective-permute-done((bf16[128,2048]{1,0:T(8,128)(2,1)}, bf16[128,2048]{1,0:T(8,128)(2,1)}, u32[]{:S(2)}, u32[]{:S(2)}) %collective-permute-start.3) | collective-permute-done | bytes 524320 | tf_op jit(solution)/shard_map/ppermute | solution.py:22
  66.5 2.8 %multiply_reduce_fusion = (f32[128]{0:T(128)}, f32[128,2048]{1,0:T(8,128)}) fusion(bf16[128,2048]{1,0:T(8,128)(2,1)S(1)} %copy-done.7, bf16[128,2048]{1,0:T(8,128)(2,1)S(1)} %copy-done.9, f32[256,2048]{1,0:T(8,128)S(1)} %convert_add_fusion, f32[128]{0:T(128)S(1)} %copy-done.45, bf16[128,2048]{1,0:T(8,128)(2,1)} %collective-permute-done.3), kind=kLoop, calls=%fused_computation.74 | loop fusion | flops 2097024 | bytes 4719616 | tf_op jit(solution)/shard_map/reduce_sum | solution.py:241
  69.3 1.6 %copy.24 = f32[128,2048]{0,1:T(8,128)S(1)} copy(f32[128,2048]{1,0:T(8,128)} %get-tuple-element.36) | data formatting | bytes 2097152 | tf_op jit(solution)/shard_map/mul | solution.py:202
  71.0 1.4 %divide_multiply_fusion = f32[128,1024]{0,1:T(8,128)S(1)} fusion(f32[128,1024]{0,1:T(8,128)S(1)} %bitcast.271, f32[1024]{0:T(1024)S(1)} %bitcast.286, f32[1024]{0:T(1024)S(1)} %bitcast.289, f32[1024]{0:T(1024)S(1)} %bitcast.283, f32[1024]{0:T(1024)S(1)} %bitcast.280), kind=kLoop, calls=%fused_computation.158 | loop fusion | flops 1441792 | bytes 1064960 | tf_op jit(solution)/shard_map/jvp(jit(silu))/mul | solution.py:108
  76.0 1.3 %collective-permute-start.22 = (f32[128,321]{0,1:T(8,128)S(1)}, f32[128,321]{0,1:T(8,128)S(1)}, u32[]{:S(2)}, u32[]{:S(2)}) collective-permute-start(f32[128,321]{0,1:T(8,128)S(1)} %fusion.221), channel_id=1, source_target_pairs={{0,2},{1,3},{2,0},{3,1},{4,6},{5,7},{6,4},{7,5},{8,10},{9,11},{10,... | collective-permute-start | bytes 493064 | tf_op jit(solution)/shard_map/ppermute | solution.py:22
  77.3 1.4 %collective-permute-done.18 = f32[1,128]{1,0:T(1,128)S(1)} collective-permute-done((f32[1,128]{1,0:T(1,128)S(1)}, f32[1,128]{1,0:T(1,128)S(1)}, u32[]{:S(2)}, u32[]{:S(2)}) %collective-permute-start.18) | collective-permute-done | bytes 544 | tf_op jit(solution)/shard_map/ppermute | solution.py:22
  78.8 3.5 %collective-permute-done.22 = f32[128,321]{0,1:T(8,128)S(1)} collective-permute-done((f32[128,321]{0,1:T(8,128)S(1)}, f32[128,321]{0,1:T(8,128)S(1)}, u32[]{:S(2)}, u32[]{:S(2)}) %collective-permute-start.22) | collective-permute-done | bytes 164384 | tf_op jit(solution)/shard_map/ppermute | solution.py:22
  85.5 1.4 %broadcast_select_fusion.7 = (bf16[128,2048]{0,1:T(8,128)(2,1)S(1)}, bf16[128,2048]{0,1:T(8,128)(2,1)S(1)}, bf16[128,2048]{0,1:T(8,128)(2,1)S(1)}, bf16[128,2048]{0,1:T(8,128)(2,1)S(1)}) fusion(pred[]{:T(512)S(6)} %ne.19, bf16[128,2048]{0,1:T(8,128)(2,1)S(1)} %collective-permute-done.13, bf16[128,2048]{0,1:T(8,128)(2,1)} %collective-permute-done.12, ...), kind=kLoop, calls=%fused_computation.167 | loop fusion | flops 2097152 | bytes 4194306 | tf_op jit(solution)/shard_map/jit(_where)/select_n | solution.py:90
  87.0 2.9 %fusion.42 = bf16[128,512]{1,0:T(8,128)(2,1)S(1)} fusion(f32[128,512]{1,0:T(8,128)S(1)} %fusion.133, bf16[1,512,8192]{2,1,0:T(8,128)(2,1)S(1)} %bitcast.251, bf16[128,2048]{0,1:T(8,128)(2,1)S(1)} %get-tuple-element.34, bf16[128,2048]{0,1:T(8,128)(2,1)S(1)} %get-tuple-element.33, bf16[128,2048]{0,1:T(8,128)(2,1)S(1)} %get-tuple-element.32, ...), kind=kOutput, calls=%fused_computation.47 | convolution fusion | flops 1082785792 | bytes 11142656 | tf_op jit(solution)/shard_map/dot_general | solution.py:127
  89.9 4.6 %collective-permute-start.23 = (bf16[128,512]{1,0:T(8,128)(2,1)S(1)}, bf16[128,512]{1,0:T(8,128)(2,1)S(1)}, u32[]{:S(2)}, u32[]{:S(2)}) collective-permute-start(bf16[128,512]{1,0:T(8,128)(2,1)S(1)} %fusion.42), channel_id=1, source_target_pairs={{0,28},{4,0},{8,4},{12,8},{16,12},{20,16},{24,20},{28,24},{1,29},{... | collective-permute-start | bytes 393224 | tf_op jit(solution)/shard_map/ppermute | solution.py:17
  95.5 8.6 %convolution_bitcast_fusion = f32[1,512,8192]{2,1,0:T(8,128)} fusion(bf16[128,2048]{0,1:T(8,128)(2,1)S(1)} %get-tuple-element.34, bf16[128,2048]{0,1:T(8,128)(2,1)S(1)} %get-tuple-element.33, bf16[128,2048]{0,1:T(8,128)(2,1)S(1)} %get-tuple-element.32, bf16[128,2048]{0,1:T(8,128)(2,1)S(1)} %get-tuple-element.31, f32[128]{0:T(128)S(1)} %copy-done.27, ...), kind=kOutput, calls=%fused_computation | convolution fusion | flops 1082327040 | bytes 19005952 | tf_op jit(solution)/shard_map/dot_general | solution.py:133
  106.2 4.6 %convolution_bitcast_fusion.1 = f32[1,4096,512]{2,1,0:T(8,128)} fusion(bf16[128,1024]{0,1:T(8,128)(2,1)S(1)} %get-tuple-element.40, bf16[128,1024]{0,1:T(8,128)(2,1)S(1)} %get-tuple-element.39, bf16[128,1024]{0,1:T(8,128)(2,1)S(1)} %get-tuple-element.38, bf16[128,1024]{0,1:T(8,128)(2,1)S(1)} %get-tuple-element.37, bf16[1,128,512]{2,1,0:T(8,128)(2,1)S(1)} %copy-done.5), kind=kOutput, calls=%fused_computation.3 | convolution fusion | flops 541065216 | bytes 9568256 | tf_op jit(solution)/shard_map/dot_general | solution.py:133
  110.8 3.3 %collective-permute-done.19 = bf16[128,512]{1,0:T(8,128)(2,1)S(1)} collective-permute-done((bf16[128,512]{1,0:T(8,128)(2,1)S(1)}, bf16[128,512]{1,0:T(8,128)(2,1)S(1)}, u32[]{:S(2)}, u32[]{:S(2)}) %collective-permute-start.19) | collective-permute-done | bytes 131104 | tf_op jit(solution)/shard_map/ppermute | solution.py:17
  (230 shorter events, 31.1 us)
Async XLA Ops:
  4.2 10.8 %collective-permute-start.1 = (bf16[256,2048]{1,0:T(8,128)(2,1)}, bf16[256,2048]{1,0:T(8,128)(2,1)S(1)}, u32[]{:S(2)}, u32[]{:S(2)}) collective-permute-start(bf16[256,2048]{1,0:T(8,128)(2,1)} %convolution_convert_fusion), channel_id=1, source_target_pairs={{0,1},{1,0},{2,3},{3,2},{4,5},{5,4},{6,7},{7,6},{8,9},{9,8},{10,11... | collective-permute-start | bytes 3145736 | tf_op jit(solution)/shard_map/ppermute | solution.py:22
  7.9 17.9 %collective-permute-start = (bf16[256,2048]{1,0:T(8,128)(2,1)}, bf16[256,2048]{1,0:T(8,128)(2,1)}, u32[]{:S(2)}, u32[]{:S(2)}) collective-permute-start(bf16[256,2048]{1,0:T(8,128)(2,1)} %convolution_convert_fusion.1), channel_id=1, source_target_pairs={{0,1},{1,0},{2,3},{3,2},{4,5},{5,4},{6,7},{7,6},{8,9},{9,8},{10,11... | collective-permute-start | bytes 3145736 | tf_op jit(solution)/shard_map/ppermute | solution.py:22
  8.5 6.4 %collective-permute-start.4 = (f32[256,321]{0,1:T(8,128)S(1)}, f32[256,321]{0,1:T(8,128)S(1)}, u32[]{:S(2)}, u32[]{:S(2)}) collective-permute-start(f32[256,321]{0,1:T(8,128)S(1)} %pad_maximum_fusion.4), channel_id=1, source_target_pairs={{0,1},{1,0},{2,3},{3,2},{4,5},{5,4},{6,7},{7,6},{8,9},{9,8},{10,11... | collective-permute-start | bytes 986120 | tf_op jit(solution)/shard_map/ppermute | solution.py:22
  10.7 10.1 %collective-permute-start.8 = (bf16[128,1024]{0,1:T(8,128)(2,1)S(1)}, bf16[128,1024]{0,1:T(8,128)(2,1)S(1)}, u32[]{:S(2)}, u32[]{:S(2)}) collective-permute-start(bf16[128,1024]{0,1:T(8,128)(2,1)S(1)} %fusion.23), channel_id=1, source_target_pairs={{0,1},{1,0},{2,3},{3,2},{4,5},{5,4},{6,7},{7,6},{8,9},{9,8},{10,11... | collective-permute-start | bytes 786440 | tf_op jit(solution)/shard_map/ppermute | solution.py:22
  13.2 32.3 %collective-permute-start.7 = (bf16[128,1024]{0,1:T(8,128)(2,1)}, bf16[128,1024]{0,1:T(8,128)(2,1)}, u32[]{:S(2)}, u32[]{:S(2)}) collective-permute-start(bf16[128,1024]{0,1:T(8,128)(2,1)} %fusion.22), channel_id=1, source_target_pairs={{0,1},{1,0},{2,3},{3,2},{4,5},{5,4},{6,7},{7,6},{8,9},{9,8},{10,11... | collective-permute-start | bytes 786440 | tf_op jit(solution)/shard_map/ppermute | solution.py:22
  14.2 16.5 %copy-start.31 = (f32[1,1,256]{2,1,0:T(1,128)}, f32[1,1,256]{2,1,0:T(1,128)S(1)}, u32[]{:S(2)}) copy-start(f32[1,1,256]{2,1,0:T(1,128)S(1)} %get-tuple-element.64) | copy-start | bytes 3076
  14.2 16.5 %copy-start.33 = (f32[1,1,256]{2,1,0:T(1,128)}, f32[1,1,256]{2,1,0:T(1,128)S(1)}, u32[]{:S(2)}) copy-start(f32[1,1,256]{2,1,0:T(1,128)S(1)} %get-tuple-element.65) | copy-start | bytes 3076
  14.2 16.5 %copy-start.35 = (f32[1,1,256]{2,1,0:T(1,128)}, f32[1,1,256]{2,1,0:T(1,128)S(1)}, u32[]{:S(2)}) copy-start(f32[1,1,256]{2,1,0:T(1,128)S(1)} %get-tuple-element.67) | copy-start | bytes 3076
  14.2 16.5 %copy-start.37 = (f32[1,1,256]{2,1,0:T(1,128)}, f32[1,1,256]{2,1,0:T(1,128)S(1)}, u32[]{:S(2)}) copy-start(f32[1,1,256]{2,1,0:T(1,128)S(1)} %get-tuple-element.66) | copy-start | bytes 3076
  14.9 40.9 %copy-start.18 = (f32[1,1,1024]{2,1,0:T(1,128)}, f32[1,1,1024]{2,1,0:T(1,128)S(1)}, u32[]{:S(2)}) copy-start(f32[1,1,1024]{2,1,0:T(1,128)S(1)} %get-tuple-element.62) | copy-start | bytes 12292
  18.2 7.5 %collective-permute-start.5 = (f32[128,321]{0,1:T(8,128)S(1)}, f32[128,321]{0,1:T(8,128)S(1)}, u32[]{:S(2)}, u32[]{:S(2)}) collective-permute-start(f32[128,321]{0,1:T(8,128)S(1)} %slice_select_fusion), channel_id=1, source_target_pairs={{0,2},{1,3},{2,0},{3,1},{4,6},{5,7},{6,4},{7,5},{8,10},{9,11},{10,... | collective-permute-start | bytes 493064 | tf_op jit(solution)/shard_map/ppermute | solution.py:22
  23.1 14.8 %collective-permute-start.2 = (bf16[128,2048]{1,0:T(8,128)(2,1)S(1)}, bf16[128,2048]{1,0:T(8,128)(2,1)S(1)}, u32[]{:S(2)}, u32[]{:S(2)}) collective-permute-start(bf16[128,2048]{1,0:T(8,128)(2,1)S(1)} %get-tuple-element.45), channel_id=1, source_target_pairs={{0,2},{1,3},{2,0},{3,1},{4,6},{5,7},{6,4},{7,5},{8,10},{9,11},{10,... | collective-permute-start | bytes 1572872 | tf_op jit(solution)/shard_map/ppermute | solution.py:22
  23.1 22.4 %collective-permute-start.9 = (bf16[128,1024]{0,1:T(8,128)(2,1)}, bf16[128,1024]{0,1:T(8,128)(2,1)}, u32[]{:S(2)}, u32[]{:S(2)}) collective-permute-start(bf16[128,1024]{0,1:T(8,128)(2,1)} %add_convert_fusion.1), channel_id=1, source_target_pairs={{0,2},{1,3},{2,0},{3,1},{4,6},{5,7},{6,4},{7,5},{8,10},{9,11},{10,... | collective-permute-start | bytes 786440 | tf_op jit(solution)/shard_map/ppermute | solution.py:22
  25.7 2.7 %collective-permute-start.6 = (f32[128,321]{0,1:T(8,128)S(1)}, f32[128,321]{0,1:T(8,128)S(1)}, u32[]{:S(2)}, u32[]{:S(2)}) collective-permute-start(f32[128,321]{0,1:T(8,128)S(1)} %add.237), channel_id=1, source_target_pairs={{0,1},{1,0},{2,3},{3,2},{4,5},{5,4},{6,7},{7,6},{8,9},{9,8},{10,11... | collective-permute-start | bytes 493064 | tf_op jit(solution)/shard_map/ppermute | solution.py:22
  47.3 1.2 %collective-permute-start.10 = (f32[2,128]{1,0:T(2,128)S(1)}, f32[2,128]{1,0:T(2,128)S(1)}, u32[]{:S(2)}, u32[]{:S(2)}) collective-permute-start(f32[2,128]{1,0:T(2,128)S(1)} %pad_maximum_fusion.10), channel_id=1, source_target_pairs={{0,1},{1,0},{2,3},{3,2},{4,5},{5,4},{6,7},{7,6},{8,9},{9,8},{10,11... | collective-permute-start | bytes 3080 | tf_op jit(solution)/shard_map/ppermute | solution.py:22
  48.6 3.6 %collective-permute-start.11 = (f32[2,128]{1,0:T(2,128)S(1)}, f32[2,128]{1,0:T(2,128)S(1)}, u32[]{:S(2)}, u32[]{:S(2)}) collective-permute-start(f32[2,128]{1,0:T(2,128)S(1)} %fusion.218), channel_id=1, source_target_pairs={{0,2},{1,3},{2,0},{3,1},{4,6},{5,7},{6,4},{7,5},{8,10},{9,11},{10,... | collective-permute-start | bytes 3080 | tf_op jit(solution)/shard_map/ppermute | solution.py:22
  51.4 15.1 %collective-permute-start.3 = (bf16[128,2048]{1,0:T(8,128)(2,1)}, bf16[128,2048]{1,0:T(8,128)(2,1)}, u32[]{:S(2)}, u32[]{:S(2)}) collective-permute-start(bf16[128,2048]{1,0:T(8,128)(2,1)} %get-tuple-element.10), channel_id=1, source_target_pairs={{0,2},{1,3},{2,0},{3,1},{4,6},{5,7},{6,4},{7,5},{8,10},{9,11},{10,... | collective-permute-start | bytes 1572872 | tf_op jit(solution)/shard_map/ppermute | solution.py:22
  57.9 20.9 %collective-permute-start.12 = (bf16[128,2048]{0,1:T(8,128)(2,1)S(1)}, bf16[128,2048]{0,1:T(8,128)(2,1)}, u32[]{:S(2)}, u32[]{:S(2)}) collective-permute-start(bf16[128,2048]{0,1:T(8,128)(2,1)S(1)} %bitcast.259), channel_id=1, source_target_pairs={{0,2},{1,3},{2,0},{3,1},{4,6},{5,7},{6,4},{7,5},{8,10},{9,11},{10,... | collective-permute-start | bytes 1572872 | tf_op jit(solution)/shard_map/ppermute | solution.py:22
  62.2 23.3 %collective-permute-start.20 = (bf16[128,2048]{0,1:T(8,128)(2,1)S(1)}, bf16[128,2048]{0,1:T(8,128)(2,1)}, u32[]{:S(2)}, u32[]{:S(2)}) collective-permute-start(bf16[128,2048]{0,1:T(8,128)(2,1)S(1)} %bitcast.260), channel_id=1, source_target_pairs={{0,1},{1,0},{2,3},{3,2},{4,5},{5,4},{6,7},{7,6},{8,9},{9,8},{10,11... | collective-permute-start | bytes 1572872 | tf_op jit(solution)/shard_map/ppermute | solution.py:22
  74.0 1.2 %collective-permute-start.17 = (f32[1,128]{1,0:T(1,128)S(1)}, f32[1,128]{1,0:T(1,128)S(1)}, u32[]{:S(2)}, u32[]{:S(2)}) collective-permute-start(f32[1,128]{1,0:T(1,128)S(1)} %bitcast.318), channel_id=1, source_target_pairs={{0,1},{1,0},{2,3},{3,2},{4,5},{5,4},{6,7},{7,6},{8,9},{9,8},{10,11... | collective-permute-start | bytes 1544 | tf_op jit(solution)/shard_map/ppermute | solution.py:22
  74.1 1.9 %collective-permute-start.21 = (f32[128,321]{0,1:T(8,128)S(1)}, f32[128,321]{0,1:T(8,128)S(1)}, u32[]{:S(2)}, u32[]{:S(2)}) collective-permute-start(f32[128,321]{0,1:T(8,128)S(1)} %pad_maximum_fusion.6), channel_id=1, source_target_pairs={{0,1},{1,0},{2,3},{3,2},{4,5},{5,4},{6,7},{7,6},{8,9},{9,8},{10,11... | collective-permute-start | bytes 493064 | tf_op jit(solution)/shard_map/ppermute | solution.py:22
  75.2 3.5 %collective-permute-start.18 = (f32[1,128]{1,0:T(1,128)S(1)}, f32[1,128]{1,0:T(1,128)S(1)}, u32[]{:S(2)}, u32[]{:S(2)}) collective-permute-start(f32[1,128]{1,0:T(1,128)S(1)} %bitcast_add_fusion), channel_id=1, source_target_pairs={{0,2},{1,3},{2,0},{3,1},{4,6},{5,7},{6,4},{7,5},{8,10},{9,11},{10,... | collective-permute-start | bytes 1544 | tf_op jit(solution)/shard_map/ppermute | solution.py:22
  76.0 6.3 %collective-permute-start.22 = (f32[128,321]{0,1:T(8,128)S(1)}, f32[128,321]{0,1:T(8,128)S(1)}, u32[]{:S(2)}, u32[]{:S(2)}) collective-permute-start(f32[128,321]{0,1:T(8,128)S(1)} %fusion.221), channel_id=1, source_target_pairs={{0,2},{1,3},{2,0},{3,1},{4,6},{5,7},{6,4},{7,5},{8,10},{9,11},{10,... | collective-permute-start | bytes 493064 | tf_op jit(solution)/shard_map/ppermute | solution.py:22
  78.7 5.6 %collective-permute-start.13 = (bf16[128,2048]{0,1:T(8,128)(2,1)}, bf16[128,2048]{0,1:T(8,128)(2,1)S(1)}, u32[]{:S(2)}, u32[]{:S(2)}) collective-permute-start(bf16[128,2048]{0,1:T(8,128)(2,1)} %collective-permute-done.12), channel_id=1, source_target_pairs={{0,1},{1,0},{2,3},{3,2},{4,5},{5,4},{6,7},{7,6},{8,9},{9,8},{10,11... | collective-permute-start | bytes 1572872 | tf_op jit(solution)/shard_map/ppermute | solution.py:22
  84.4 11.1 %collective-permute-start.14 = (bf16[128,1024]{0,1:T(8,128)(2,1)S(1)}, bf16[128,1024]{0,1:T(8,128)(2,1)S(1)}, u32[]{:S(2)}, u32[]{:S(2)}) collective-permute-start(bf16[128,1024]{0,1:T(8,128)(2,1)S(1)} %fusion.112), channel_id=1, source_target_pairs={{0,2},{1,3},{2,0},{3,1},{4,6},{5,7},{6,4},{7,5},{8,10},{9,11},{10,... | collective-permute-start | bytes 786440 | tf_op jit(solution)/shard_map/ppermute | solution.py:22
  85.5 19.1 %collective-permute-start.16 = (bf16[128,1024]{0,1:T(8,128)(2,1)S(1)}, bf16[128,1024]{0,1:T(8,128)(2,1)S(1)}, u32[]{:S(2)}, u32[]{:S(2)}) collective-permute-start(bf16[128,1024]{0,1:T(8,128)(2,1)S(1)} %fusion.112), channel_id=1, source_target_pairs={{0,1},{1,0},{2,3},{3,2},{4,5},{5,4},{6,7},{7,6},{8,9},{9,8},{10,11... | collective-permute-start | bytes 786440 | tf_op jit(solution)/shard_map/ppermute | solution.py:22
  89.9 14.7 %collective-permute-start.23 = (bf16[128,512]{1,0:T(8,128)(2,1)S(1)}, bf16[128,512]{1,0:T(8,128)(2,1)S(1)}, u32[]{:S(2)}, u32[]{:S(2)}) collective-permute-start(bf16[128,512]{1,0:T(8,128)(2,1)S(1)} %fusion.42), channel_id=1, source_target_pairs={{0,28},{4,0},{8,4},{12,8},{16,12},{20,16},{24,20},{28,24},{1,29},{... | collective-permute-start | bytes 393224 | tf_op jit(solution)/shard_map/ppermute | solution.py:17
  94.5 10.1 %collective-permute-start.24 = (bf16[128,1024]{0,1:T(8,128)(2,1)S(1)}, bf16[128,1024]{0,1:T(8,128)(2,1)S(1)}, u32[]{:S(2)}, u32[]{:S(2)}) collective-permute-start(bf16[128,1024]{0,1:T(8,128)(2,1)S(1)} %copy-done.10), channel_id=1, source_target_pairs={{0,2},{1,3},{2,0},{3,1},{4,6},{5,7},{6,4},{7,5},{8,10},{9,11},{10,... | collective-permute-start | bytes 786440 | tf_op jit(solution)/shard_map/ppermute | solution.py:22
  95.5 9.2 %collective-permute-start.15 = (bf16[128,1024]{0,1:T(8,128)(2,1)S(1)}, bf16[128,1024]{0,1:T(8,128)(2,1)S(1)}, u32[]{:S(2)}, u32[]{:S(2)}) collective-permute-start(bf16[128,1024]{0,1:T(8,128)(2,1)S(1)} %collective-permute-done.14), channel_id=1, source_target_pairs={{0,1},{1,0},{2,3},{3,2},{4,5},{5,4},{6,7},{7,6},{8,9},{9,8},{10,11... | collective-permute-start | bytes 786440 | tf_op jit(solution)/shard_map/ppermute | solution.py:22
  104.1 1.7 %collective-permute-start.26 = (bf16[128,1024]{0,1:T(8,128)(2,1)S(1)}, bf16[128,1024]{0,1:T(8,128)(2,1)S(1)}, u32[]{:S(2)}, u32[]{:S(2)}) collective-permute-start(bf16[128,1024]{0,1:T(8,128)(2,1)S(1)} %copy-done.10), channel_id=1, source_target_pairs={{0,1},{1,0},{2,3},{3,2},{4,5},{5,4},{6,7},{7,6},{8,9},{9,8},{10,11... | collective-permute-start | bytes 786440 | tf_op jit(solution)/shard_map/ppermute | solution.py:22
  104.6 1.5 %collective-permute-start.25 = (bf16[128,1024]{0,1:T(8,128)(2,1)S(1)}, bf16[128,1024]{0,1:T(8,128)(2,1)S(1)}, u32[]{:S(2)}, u32[]{:S(2)}) collective-permute-start(bf16[128,1024]{0,1:T(8,128)(2,1)S(1)} %collective-permute-done.24), channel_id=1, source_target_pairs={{0,1},{1,0},{2,3},{3,2},{4,5},{5,4},{6,7},{7,6},{8,9},{9,8},{10,11... | collective-permute-start | bytes 786440 | tf_op jit(solution)/shard_map/ppermute | solution.py:22
  105.5 8.6 %collective-permute-start.19 = (bf16[128,512]{1,0:T(8,128)(2,1)S(1)}, bf16[128,512]{1,0:T(8,128)(2,1)S(1)}, u32[]{:S(2)}, u32[]{:S(2)}) collective-permute-start(bf16[128,512]{1,0:T(8,128)(2,1)S(1)} %fusion.45), channel_id=1, source_target_pairs={{0,4},{4,8},{8,12},{12,16},{16,20},{20,24},{24,28},{28,0},{1,5},{5... | collective-permute-start | bytes 393224 | tf_op jit(solution)/shard_map/ppermute | solution.py:17
  (56 other events, 272.1 us)

commit v5 on v4

--- a/solution.py
+++ b/solution.py
@@ -250,7 +250,8 @@
     d_dt_full = lax.dynamic_update_slice_in_dim(
         jnp.zeros((SEQ, HEADS), jnp.float32), d_pdt, head_first, 1
     )
-    summed = sum_all(jnp.concatenate([d_maps, d_dt_full, inner_own], axis=1))
+    map_part = jnp.concatenate([d_maps, d_dt_full, inner_own], axis=1)
+    summed = sum_all(map_part)
     conv_out, conv_back = jax.vjp(whole_act, pre_part)
     d_pre = conv_back(summed[:, :MAPS])[0]
     round_bcdt = jnp.concatenate([d_pre, summed[:, MAPS : MAPS + HEADS]], axis=1).astype(
@@ -260,7 +261,8 @@
         round_bcdt.astype(jnp.float32) * raw_cols, axis=1, keepdims=True
     )
 
-    fwd_gated = gate_parts(forward_proj)[0]
+    late_raw = tied(forward_proj[2], map_part)
+    fwd_gated = gate_parts(forward_proj[:2] + (late_raw,) + forward_proj[3:])[0]
     fwd_all, _ = gather_cols((fwd_gated * gain_local).astype(jnp.bfloat16), round_last)
     fwd_sum = sum_all(jnp.sum(fwd_gated * fwd_gated, axis=1)[None])
     fwd_inverse = lax.rsqrt(fwd_sum[0] / INNER + 1e-05)[:, None]

time: 116 us -> 116 us (level)
  local copies, waits for them, and re-layouts: 9.6 us -> 8.28 us
  other arithmetic: 16.6 us -> 17.9 us
    mul x2, local copies, waits for them, and re-layouts: 4.17 us -> 2.88 us  [gate_parts(): own_xz = raw_xz * scales]
  transfers between devices with their start and end apart: 27 -> 27, of which waited for: 10 -> 10; matrix products, arithmetic and copies ran while one was open for 61% -> 60% of each run, Pallas kernels for 0% -> 0%
where the time goes in v5:
time: 116 us
  matrix products  50.8 us (44%)
  starting transfers between devices  19.7 us (17%)
  other arithmetic  17.9 us (15%)
  waiting for transfers between devices  17.2 us (15%)
  local copies, waits for them, and re-layouts  8.28 us (7%)
  between operations  1.68 us (1%)
    ppermute x25, starting transfers between devices, swap(): return lax.ppermute(x, 'dp', [(i, i ^ mask) for i in range(length)])  15.1 us
    dot_general x3, matrix products, transposed_times(): lax.dot_general(left, right, (((0,), (0,)), ((), ())), preferred_element_...  14.4 us
    ppermute x25, waiting for transfers between devices, swap(): return lax.ppermute(x, 'dp', [(i, i ^ mask) for i in range(length)])  13.9 us
    dot_general x8, matrix products, times_transposed(): lax.dot_general(left, right, (((1,), (1,)), ((), ())), preferred_element_...  13 us
    dot_general x4, matrix products, xz_part(): return jnp.dot(both, cols, preferred_element_type=jnp.float32)  11.7 us
    dot_general x4, matrix products, mixer(): jnp.einsum('hts,shp->thp', weights, heads_in, precision=lax.Precision.HIGH)  5.5 us
    ppermute x2, starting transfers between devices, from_behind(): lax.ppermute(x, axis, [(i, (i + by) % length) for i in range(length)])  4.6 us
    mul x2, other arithmetic, mixer(): xconv = jax.nn.silu(causal_conv(proj_x, conv_taps))  3.62 us
  transfers between devices with their start and end apart: 27, of which 10 were waited for; matrix products, arithmetic and copies ran while one was open for 60% of the time, Pallas kernels for 0%

profile of v5, /device:TPU:0, one launch (start us, length us, event | category | flops | bytes accessed | tf_op | source)
XLA Modules:
  0.0 115.6 jit_solution(12686943776462006692)
XLA Ops:
  0.7 3.5 %convolution_convert_fusion = bf16[256,2048]{1,0:T(8,128)(2,1)} fusion(bf16[1,512,8192]{2,1,0:T(8,128)(2,1)} %param.15, s32[]{:T(128)S(6)} %select_n.195, bf16[128,512]{1,0:T(8,128)(2,1)} %bitcast.252, bf16[128,512]{1,0:T(8,128)(2,1)} %bitcast.244), kind=kOutput, calls=%fused_computation.6 | convolution fusion | flops 537919488 | bytes 3407876 | tf_op jit(solution)/shard_map/dot_general | solution.py:177
  4.6 3.3 %convolution_convert_fusion.1 = bf16[256,2048]{1,0:T(8,128)(2,1)} fusion(bf16[1,512,8192]{2,1,0:T(8,128)(2,1)} %param.15, s32[]{:T(128)S(6)} %select_n.193, bf16[128,512]{1,0:T(8,128)(2,1)S(1)} %bitcast.253, bf16[128,512]{1,0:T(8,128)(2,1)S(1)} %bitcast.245), kind=kOutput, calls=%fused_computation.7 | convolution fusion | flops 537919488 | bytes 3407876 | tf_op jit(solution)/shard_map/dot_general | solution.py:177
  9.0 1.7 %fusion.23 = bf16[128,1024]{0,1:T(8,128)(2,1)S(1)} fusion(bf16[1,4096,512]{2,1,0:T(8,128)(2,1)} %param.17, s32[]{:T(128)S(6)} %select_n.206, bf16[1,128,512]{2,1,0:T(8,128)(2,1)S(1)} %copy-done.5), kind=kOutput, calls=%fused_computation.40 | convolution fusion | flops 134348800 | bytes 1441796 | tf_op jit(solution)/shard_map/dot_general | solution.py:127
  10.8 2.3 %fusion.22 = bf16[128,1024]{0,1:T(8,128)(2,1)} fusion(bf16[1,4096,512]{2,1,0:T(8,128)(2,1)} %param.17, s32[]{:T(128)S(6)} %select_n.204, bf16[1,128,512]{2,1,0:T(8,128)(2,1)S(1)} %copy-done.5), kind=kOutput, calls=%fused_computation.39 | convolution fusion | flops 134348800 | bytes 1441796 | tf_op jit(solution)/shard_map/dot_general | solution.py:127
  14.9 2.3 %add_convert_fusion = bf16[256,2048]{1,0:T(8,128)(2,1)S(1)} fusion(bf16[256,2048]{1,0:T(8,128)(2,1)S(1)} %collective-permute-done.1, bf16[1,512,8192]{2,1,0:T(8,128)(2,1)} %param.15, s32[]{:T(128)S(6)} %select_n.194, bf16[128,512]{1,0:T(8,128)(2,1)S(1)} %bitcast.256, bf16[128,512]{1,0:T(8,128)(2,1)S(1)} %bitcast.248), kind=kOutput, calls=%fused_computation.15 | convolution fusion | flops 538968064 | bytes 4456452 | tf_op jit(solution)/shard_map/dot_general | solution.py:177
  18.1 2.5 %collective-permute-start.5 = (f32[128,321]{0,1:T(8,128)S(1)}, f32[128,321]{0,1:T(8,128)S(1)}, u32[]{:S(2)}, u32[]{:S(2)}) collective-permute-start(f32[128,321]{0,1:T(8,128)S(1)} %slice_select_fusion), channel_id=1, source_target_pairs={{0,2},{1,3},{2,0},{3,1},{4,6},{5,7},{6,4},{7,5},{8,10},{9,11},{10,... | collective-permute-start | bytes 493064 | tf_op jit(solution)/shard_map/ppermute | solution.py:22
  20.7 2.4 %add_convert_fusion.1 = bf16[128,1024]{0,1:T(8,128)(2,1)} fusion(bf16[128,1024]{0,1:T(8,128)(2,1)S(1)} %collective-permute-done.8, bf16[1,128,512]{2,1,0:T(8,128)(2,1)S(1)} %copy-done.5, bf16[1,4096,512]{2,1,0:T(8,128)(2,1)} %param.17, s32[]{:T(128)S(6)} %select_n.205), kind=kOutput, calls=%fused_computation.142 | convolution fusion | flops 134610944 | bytes 1703940 | tf_op jit(solution)/shard_map/dot_general | solution.py:127
  23.0 2.0 %collective-permute-start.9 = (bf16[128,1024]{0,1:T(8,128)(2,1)}, bf16[128,1024]{0,1:T(8,128)(2,1)}, u32[]{:S(2)}, u32[]{:S(2)}) collective-permute-start(bf16[128,1024]{0,1:T(8,128)(2,1)} %add_convert_fusion.1), channel_id=1, source_target_pairs={{0,2},{1,3},{2,0},{3,1},{4,6},{5,7},{6,4},{7,5},{8,10},{9,11},{10,... | collective-permute-start | bytes 786440 | tf_op jit(solution)/shard_map/ppermute | solution.py:22
  25.7 2.6 %convert_add_fusion = f32[256,2048]{1,0:T(8,128)S(1)} fusion(bf16[256,2048]{1,0:T(8,128)(2,1)} %collective-permute-done, bf16[1,512,8192]{2,1,0:T(8,128)(2,1)} %param.15, s32[]{:T(128)S(6)} %select_n.192, bf16[128,512]{1,0:T(8,128)(2,1)S(1)} %bitcast.257, bf16[128,512]{1,0:T(8,128)(2,1)S(1)} %bitcast.249), kind=kOutput, calls=%fused_computation.18 | convolution fusion | flops 538443776 | bytes 5505028 | tf_op jit(solution)/shard_map/dot_general | solution.py:177
  33.1 4.7 %collective-permute-done.2 = bf16[128,2048]{1,0:T(8,128)(2,1)S(1)} collective-permute-done((bf16[128,2048]{1,0:T(8,128)(2,1)S(1)}, bf16[128,2048]{1,0:T(8,128)(2,1)S(1)}, u32[]{:S(2)}, u32[]{:S(2)}) %collective-permute-start.2) | collective-permute-done | bytes 524320 | tf_op jit(solution)/shard_map/ppermute | solution.py:22
  38.9 2.6 %copy.24 = f32[128,2048]{0,1:T(8,128)} copy(f32[128,2048]{1,0:T(8,128)} %fusion.84) | data formatting | bytes 2097152 | tf_op jit(solution)/shard_map/mul | solution.py:202
  42.7 1.4 %fusion.121 = (f32[128,1024]{0,1:T(8,128)S(1)}, f32[128,1024]{0,1:T(8,128)S(1)}) fusion(f32[128,1024]{0,1:T(8,128)S(1)} %bitcast.270, f32[1024]{0:T(1024)S(1)} %bitcast.284, f32[1024]{0:T(1024)S(1)} %bitcast.287, f32[1024]{0:T(1024)S(1)} %bitcast.281, f32[1024]{0:T(1024)S(1)} %bitcast.278), kind=kLoop, calls=%fused_computation.151 | loop fusion | flops 1441792 | bytes 1589248 | tf_op jit(solution)/shard_map/jvp(jit(silu))/mul | solution.py:108
  44.2 1.2 %multiply_reduce_fusion.5 = (f32[128]{0:T(128)S(1)}, f32[128,16,64]{0,2,1:T(8,128)S(1)}, f32[128,16,64]{0,2,1:T(8,128)S(1)}) fusion(f32[128,16,2,64]{0,3,2,1:T(8,128)S(1)} %bitcast.262, f32[128,16,64]{0,2,1:T(8,128)S(1)} %bitcast.273, f32[16]{0:T(128)S(1)} %bitcast.315, f32[16,128]{1,0:T(8,128)S(1)} %copy-done.36, f32[128,128]{1,0:T(8,128)S(1)} %copy-done.17, ...), kind=kOutput, calls=%fused_computation.143 | convolution fusion | flops 103153536 | bytes 2728960 | tf_op jit(solution)/shard_map/jvp(hts,shp->thp)/dot_general | solution.py:120
  45.4 1.8 %multiply_reduce_fusion.4 = (f32[128]{0:T(128)S(1)}, f32[128,1024]{0,1:T(8,128)S(1)}) fusion(f32[128,16,64]{0,2,1:T(8,128)S(1)} %get-tuple-element.28, f32[1024]{0:T(1024)S(1)} %bitcast.290, bf16[128,1024]{0,1:T(8,128)(2,1)} %collective-permute-done.9, bf16[128,1024]{0,1:T(8,128)(2,1)} %collective-permute-done.7, bf16[1,128,512]{2,1,0:T(8,128)(2,1)S(1)} %copy-done.5, ...), kind=kOutput, calls=%fused_computation.140 | convolution fusion | flops 135135104 | bytes 2757124 | tf_op jit(solution)/shard_map/dot_general | solution.py:127
  48.5 1.3 %collective-permute-start.11 = (f32[2,128]{1,0:T(2,128)S(1)}, f32[2,128]{1,0:T(2,128)S(1)}, u32[]{:S(2)}, u32[]{:S(2)}) collective-permute-start(f32[2,128]{1,0:T(2,128)S(1)} %fusion.217), channel_id=1, source_target_pairs={{0,2},{1,3},{2,0},{3,1},{4,6},{5,7},{6,4},{7,5},{8,10},{9,11},{10,... | collective-permute-start | bytes 3080 | tf_op jit(solution)/shard_map/ppermute | solution.py:22
  49.7 1.5 %fusion.168 = f32[16,128]{1,0:T(8,128)} fusion(f32[16]{0:T(128)S(1)} %copy-done.50, f32[128,64]{0,1:T(8,128)} %copy-done.19, s32[]{:T(128)S(6)} %select_n.199, f32[16]{0:T(128)S(1)} %bitcast.313), kind=kOutput, calls=%fused_computation.251 | convolution fusion | flops 3178496 | bytes 16516 | tf_op jit(solution)/shard_map/jvp()/dot_general | solution.py:112
  52.1 2.1 %multiply_convert_fusion = (bf16[128,1024]{0,1:T(8,128)(2,1)}, f32[128,1024]{0,1:T(8,128)S(1)}) fusion(f32[128,16,64]{0,2,1:T(8,128)S(1)} %get-tuple-element.28, f32[128]{0:T(128)S(1)} %get-tuple-element.26, f32[1024]{0:T(1024)S(1)} %bitcast.291, f32[128]{0:T(128)S(1)} %slice_bitcast_fusion.2, f32[128]{0:T(128)S(1)} %get-tuple-element.25, ...), kind=kLoop, calls=%fused_computation.132 | loop fusion | flops 1703936 | bytes 2364928 | tf_op jit(solution)/shard_map/convert_element_type | solution.py:226
  55.1 2.2 %fusion.86 = (f32[16,128]{1,0:T(8,128)S(1)}, f32[16,128]{1,0:T(8,128)S(1)}, f32[16,128]{1,0:T(8,128)S(1)}, f32[128,128]{1,0:T(8,128)}) fusion(f32[16,128]{1,0:T(8,128)S(1)} %copy-done.37, f32[128,128]{1,0:T(8,128)S(1)} %copy-done.17, f32[16,128]{1,0:T(8,128)S(1)} %copy-done.52, pred[128,128]{1,0:T(8,128)(4,1)S(1)} %copy-done.25, ...), kind=kOutput, calls=%fused_computation.95 | convolution fusion | flops 105228288 | bytes 1769472 | tf_op jit(solution)/shard_map/transpose(jvp(hts,shp->thp))/dot_general | solution.py:120
  58.9 1.3 %collective-permute-start.12 = (bf16[128,2048]{0,1:T(8,128)(2,1)S(1)}, bf16[128,2048]{0,1:T(8,128)(2,1)}, u32[]{:S(2)}, u32[]{:S(2)}) collective-permute-start(bf16[128,2048]{0,1:T(8,128)(2,1)S(1)} %bitcast.258), channel_id=1, source_target_pairs={{0,2},{1,3},{2,0},{3,1},{4,6},{5,7},{6,4},{7,5},{8,10},{9,11},{10,... | collective-permute-start | bytes 1572872 | tf_op jit(solution)/shard_map/ppermute | solution.py:22
  64.1 2.3 %collective-permute-done.3 = bf16[128,2048]{1,0:T(8,128)(2,1)} collective-permute-done((bf16[128,2048]{1,0:T(8,128)(2,1)}, bf16[128,2048]{1,0:T(8,128)(2,1)}, u32[]{:S(2)}, u32[]{:S(2)}) %collective-permute-start.3) | collective-permute-done | bytes 524320 | tf_op jit(solution)/shard_map/ppermute | solution.py:22
  66.4 1.7 %multiply_reduce_fusion = (f32[128]{0:T(128)S(1)}, f32[128,2048]{1,0:T(8,128)S(1)}) fusion(bf16[128,2048]{1,0:T(8,128)(2,1)} %copy.27, bf16[128,2048]{1,0:T(8,128)(2,1)} %copy-done.6, f32[256,2048]{1,0:T(8,128)S(1)} %convert_add_fusion, bf16[128,2048]{1,0:T(8,128)(2,1)} %collective-permute-done.3), kind=kLoop, calls=%fused_computation.79 | loop fusion | flops 1834880 | bytes 4719104 | tf_op jit(solution)/shard_map/reduce_sum | solution.py:241
  69.4 2.3 %divide_multiply_fusion = f32[128,1024]{0,1:T(8,128)S(1)} fusion(f32[128,1024]{0,1:T(8,128)S(1)} %bitcast.271, f32[1024]{0:T(1024)S(1)} %bitcast.286, f32[1024]{0:T(1024)} %bitcast.289, f32[1024]{0:T(1024)S(1)} %bitcast.283, f32[1024]{0:T(1024)S(1)} %bitcast.280), kind=kLoop, calls=%fused_computation.138 | loop fusion | flops 1441792 | bytes 1064960 | tf_op jit(solution)/shard_map/jvp(jit(silu))/mul | solution.py:108
  71.8 1.2 %multiply_reduce_fusion.3 = (f32[128]{0:T(128)S(1)}, f32[128,16,64]{0,2,1:T(8,128)S(1)}) fusion(f32[128,16,2,64]{0,3,2,1:T(8,128)S(1)} %bitcast.267, f32[128,16,64]{0,2,1:T(8,128)S(1)} %bitcast.275, f32[16]{0:T(128)S(1)} %bitcast.317, f32[16,128]{1,0:T(8,128)S(1)} %copy-done.35, f32[128,128]{1,0:T(8,128)S(1)} %copy-done.16, f32[16,128]{1,0:T(8,128)S(1)} %copy-done.51, ...), kind=kOutput, calls=%fused_computation.133 | convolution fusion | flops 103153536 | bytes 2204672 | tf_op jit(solution)/shard_map/jvp(hts,shp->thp)/dot_general | solution.py:120
  76.2 1.3 %collective-permute-start.22 = (f32[128,321]{0,1:T(8,128)S(1)}, f32[128,321]{0,1:T(8,128)S(1)}, u32[]{:S(2)}, u32[]{:S(2)}) collective-permute-start(f32[128,321]{0,1:T(8,128)S(1)} %fusion.220), channel_id=1, source_target_pairs={{0,2},{1,3},{2,0},{3,1},{4,6},{5,7},{6,4},{7,5},{8,10},{9,11},{10,... | collective-permute-start | bytes 493064 | tf_op jit(solution)/shard_map/ppermute | solution.py:22
  78.0 4.4 %collective-permute-done.22 = f32[128,321]{0,1:T(8,128)S(1)} collective-permute-done((f32[128,321]{0,1:T(8,128)S(1)}, f32[128,321]{0,1:T(8,128)S(1)}, u32[]{:S(2)}, u32[]{:S(2)}) %collective-permute-start.22) | collective-permute-done | bytes 164384 | tf_op jit(solution)/shard_map/ppermute | solution.py:22
  84.5 1.3 %collective-permute-start.14 = (bf16[128,1024]{0,1:T(8,128)(2,1)S(1)}, bf16[128,1024]{0,1:T(8,128)(2,1)S(1)}, u32[]{:S(2)}, u32[]{:S(2)}) collective-permute-start(bf16[128,1024]{0,1:T(8,128)(2,1)S(1)} %fusion.105), channel_id=1, source_target_pairs={{0,2},{1,3},{2,0},{3,1},{4,6},{5,7},{6,4},{7,5},{8,10},{9,11},{10,... | collective-permute-start | bytes 786440 | tf_op jit(solution)/shard_map/ppermute | solution.py:22
  85.8 1.4 %broadcast_select_fusion.7 = (bf16[128,2048]{0,1:T(8,128)(2,1)S(1)}, bf16[128,2048]{0,1:T(8,128)(2,1)S(1)}, bf16[128,2048]{0,1:T(8,128)(2,1)S(1)}, bf16[128,2048]{0,1:T(8,128)(2,1)S(1)}) fusion(pred[]{:T(512)S(6)} %ne.19, bf16[128,2048]{0,1:T(8,128)(2,1)S(1)} %collective-permute-done.13, bf16[128,2048]{0,1:T(8,128)(2,1)} %collective-permute-done.12, ...), kind=kLoop, calls=%fused_computation.167 | loop fusion | flops 2097152 | bytes 4194306 | tf_op jit(solution)/shard_map/jit(_where)/select_n | solution.py:90
  87.3 2.9 %fusion.42 = bf16[128,512]{1,0:T(8,128)(2,1)S(1)} fusion(f32[128,512]{1,0:T(8,128)S(1)} %fusion.132, bf16[1,512,8192]{2,1,0:T(8,128)(2,1)S(1)} %bitcast.251, bf16[128,2048]{0,1:T(8,128)(2,1)S(1)} %get-tuple-element.36, bf16[128,2048]{0,1:T(8,128)(2,1)S(1)} %get-tuple-element.35, bf16[128,2048]{0,1:T(8,128)(2,1)S(1)} %get-tuple-element.34, ...), kind=kOutput, calls=%fused_computation.47 | convolution fusion | flops 1082785792 | bytes 11142656 | tf_op jit(solution)/shard_map/dot_general | solution.py:127
  90.2 4.5 %collective-permute-start.23 = (bf16[128,512]{1,0:T(8,128)(2,1)S(1)}, bf16[128,512]{1,0:T(8,128)(2,1)S(1)}, u32[]{:S(2)}, u32[]{:S(2)}) collective-permute-start(bf16[128,512]{1,0:T(8,128)(2,1)S(1)} %fusion.42), channel_id=1, source_target_pairs={{0,28},{4,0},{8,4},{12,8},{16,12},{20,16},{24,20},{28,24},{1,29},{... | collective-permute-start | bytes 393224 | tf_op jit(solution)/shard_map/ppermute | solution.py:17
  95.6 8.6 %convolution_bitcast_fusion = f32[1,512,8192]{2,1,0:T(8,128)} fusion(bf16[128,2048]{0,1:T(8,128)(2,1)S(1)} %get-tuple-element.36, bf16[128,2048]{0,1:T(8,128)(2,1)S(1)} %get-tuple-element.35, bf16[128,2048]{0,1:T(8,128)(2,1)S(1)} %get-tuple-element.34, bf16[128,2048]{0,1:T(8,128)(2,1)S(1)} %get-tuple-element.33, f32[128]{0:T(128)S(1)} %copy-done.23, ...), kind=kOutput, calls=%fused_computation | convolution fusion | flops 1082327040 | bytes 19005952 | tf_op jit(solution)/shard_map/dot_general | solution.py:133
  106.4 4.6 %convolution_bitcast_fusion.1 = f32[1,4096,512]{2,1,0:T(8,128)} fusion(bf16[128,1024]{0,1:T(8,128)(2,1)S(1)} %get-tuple-element.42, bf16[128,1024]{0,1:T(8,128)(2,1)S(1)} %get-tuple-element.41, bf16[128,1024]{0,1:T(8,128)(2,1)S(1)} %get-tuple-element.40, bf16[128,1024]{0,1:T(8,128)(2,1)S(1)} %get-tuple-element.39, bf16[1,128,512]{2,1,0:T(8,128)(2,1)S(1)} %copy-done.5), kind=kOutput, calls=%fused_computation.3 | convolution fusion | flops 541065216 | bytes 9568256 | tf_op jit(solution)/shard_map/dot_general | solution.py:133
  111.0 3.3 %collective-permute-done.19 = bf16[128,512]{1,0:T(8,128)(2,1)S(1)} collective-permute-done((bf16[128,512]{1,0:T(8,128)(2,1)S(1)}, bf16[128,512]{1,0:T(8,128)(2,1)S(1)}, u32[]{:S(2)}, u32[]{:S(2)}) %collective-permute-start.19) | collective-permute-done | bytes 131104 | tf_op jit(solution)/shard_map/ppermute | solution.py:17
  (219 shorter events, 31.5 us)
Async XLA Ops:
  4.2 10.8 %collective-permute-start.1 = (bf16[256,2048]{1,0:T(8,128)(2,1)}, bf16[256,2048]{1,0:T(8,128)(2,1)S(1)}, u32[]{:S(2)}, u32[]{:S(2)}) collective-permute-start(bf16[256,2048]{1,0:T(8,128)(2,1)} %convolution_convert_fusion), channel_id=1, source_target_pairs={{0,1},{1,0},{2,3},{3,2},{4,5},{5,4},{6,7},{7,6},{8,9},{9,8},{10,11... | collective-permute-start | bytes 3145736 | tf_op jit(solution)/shard_map/ppermute | solution.py:22
  7.9 17.8 %collective-permute-start = (bf16[256,2048]{1,0:T(8,128)(2,1)}, bf16[256,2048]{1,0:T(8,128)(2,1)}, u32[]{:S(2)}, u32[]{:S(2)}) collective-permute-start(bf16[256,2048]{1,0:T(8,128)(2,1)} %convolution_convert_fusion.1), channel_id=1, source_target_pairs={{0,1},{1,0},{2,3},{3,2},{4,5},{5,4},{6,7},{7,6},{8,9},{9,8},{10,11... | collective-permute-start | bytes 3145736 | tf_op jit(solution)/shard_map/ppermute | solution.py:22
  8.5 6.3 %collective-permute-start.4 = (f32[256,321]{0,1:T(8,128)S(1)}, f32[256,321]{0,1:T(8,128)S(1)}, u32[]{:S(2)}, u32[]{:S(2)}) collective-permute-start(f32[256,321]{0,1:T(8,128)S(1)} %pad_maximum_fusion.4), channel_id=1, source_target_pairs={{0,1},{1,0},{2,3},{3,2},{4,5},{5,4},{6,7},{7,6},{8,9},{9,8},{10,11... | collective-permute-start | bytes 986120 | tf_op jit(solution)/shard_map/ppermute | solution.py:22
  10.7 10.0 %collective-permute-start.8 = (bf16[128,1024]{0,1:T(8,128)(2,1)S(1)}, bf16[128,1024]{0,1:T(8,128)(2,1)S(1)}, u32[]{:S(2)}, u32[]{:S(2)}) collective-permute-start(bf16[128,1024]{0,1:T(8,128)(2,1)S(1)} %fusion.23), channel_id=1, source_target_pairs={{0,1},{1,0},{2,3},{3,2},{4,5},{5,4},{6,7},{7,6},{8,9},{9,8},{10,11... | collective-permute-start | bytes 786440 | tf_op jit(solution)/shard_map/ppermute | solution.py:22
  13.1 32.3 %collective-permute-start.7 = (bf16[128,1024]{0,1:T(8,128)(2,1)}, bf16[128,1024]{0,1:T(8,128)(2,1)}, u32[]{:S(2)}, u32[]{:S(2)}) collective-permute-start(bf16[128,1024]{0,1:T(8,128)(2,1)} %fusion.22), channel_id=1, source_target_pairs={{0,1},{1,0},{2,3},{3,2},{4,5},{5,4},{6,7},{7,6},{8,9},{9,8},{10,11... | collective-permute-start | bytes 786440 | tf_op jit(solution)/shard_map/ppermute | solution.py:22
  14.1 16.5 %copy-start.29 = (f32[1,1,256]{2,1,0:T(1,128)}, f32[1,1,256]{2,1,0:T(1,128)S(1)}, u32[]{:S(2)}) copy-start(f32[1,1,256]{2,1,0:T(1,128)S(1)} %get-tuple-element.67) | copy-start | bytes 3076
  14.1 16.5 %copy-start.31 = (f32[1,1,256]{2,1,0:T(1,128)}, f32[1,1,256]{2,1,0:T(1,128)S(1)}, u32[]{:S(2)}) copy-start(f32[1,1,256]{2,1,0:T(1,128)S(1)} %get-tuple-element.69) | copy-start | bytes 3076
  14.2 16.5 %copy-start.33 = (f32[1,1,256]{2,1,0:T(1,128)}, f32[1,1,256]{2,1,0:T(1,128)S(1)}, u32[]{:S(2)}) copy-start(f32[1,1,256]{2,1,0:T(1,128)S(1)} %get-tuple-element.68) | copy-start | bytes 3076
  14.8 43.0 %copy-start.15 = (f32[1,1,1024]{2,1,0:T(1,128)}, f32[1,1,1024]{2,1,0:T(1,128)S(1)}, u32[]{:S(2)}) copy-start(f32[1,1,1024]{2,1,0:T(1,128)S(1)} %get-tuple-element.64) | copy-start | bytes 12292
  18.1 7.5 %collective-permute-start.5 = (f32[128,321]{0,1:T(8,128)S(1)}, f32[128,321]{0,1:T(8,128)S(1)}, u32[]{:S(2)}, u32[]{:S(2)}) collective-permute-start(f32[128,321]{0,1:T(8,128)S(1)} %slice_select_fusion), channel_id=1, source_target_pairs={{0,2},{1,3},{2,0},{3,1},{4,6},{5,7},{6,4},{7,5},{8,10},{9,11},{10,... | collective-permute-start | bytes 493064 | tf_op jit(solution)/shard_map/ppermute | solution.py:22
  23.0 14.8 %collective-permute-start.2 = (bf16[128,2048]{1,0:T(8,128)(2,1)S(1)}, bf16[128,2048]{1,0:T(8,128)(2,1)S(1)}, u32[]{:S(2)}, u32[]{:S(2)}) collective-permute-start(bf16[128,2048]{1,0:T(8,128)(2,1)S(1)} %get-tuple-element.47), channel_id=1, source_target_pairs={{0,2},{1,3},{2,0},{3,1},{4,6},{5,7},{6,4},{7,5},{8,10},{9,11},{10,... | collective-permute-start | bytes 1572872 | tf_op jit(solution)/shard_map/ppermute | solution.py:22
  23.0 22.3 %collective-permute-start.9 = (bf16[128,1024]{0,1:T(8,128)(2,1)}, bf16[128,1024]{0,1:T(8,128)(2,1)}, u32[]{:S(2)}, u32[]{:S(2)}) collective-permute-start(bf16[128,1024]{0,1:T(8,128)(2,1)} %add_convert_fusion.1), channel_id=1, source_target_pairs={{0,2},{1,3},{2,0},{3,1},{4,6},{5,7},{6,4},{7,5},{8,10},{9,11},{10,... | collective-permute-start | bytes 786440 | tf_op jit(solution)/shard_map/ppermute | solution.py:22
  25.6 2.7 %collective-permute-start.6 = (f32[128,321]{0,1:T(8,128)S(1)}, f32[128,321]{0,1:T(8,128)S(1)}, u32[]{:S(2)}, u32[]{:S(2)}) collective-permute-start(f32[128,321]{0,1:T(8,128)S(1)} %add.237), channel_id=1, source_target_pairs={{0,1},{1,0},{2,3},{3,2},{4,5},{5,4},{6,7},{7,6},{8,9},{9,8},{10,11... | collective-permute-start | bytes 493064 | tf_op jit(solution)/shard_map/ppermute | solution.py:22
  47.3 1.2 %collective-permute-start.10 = (f32[2,128]{1,0:T(2,128)S(1)}, f32[2,128]{1,0:T(2,128)S(1)}, u32[]{:S(2)}, u32[]{:S(2)}) collective-permute-start(f32[2,128]{1,0:T(2,128)S(1)} %pad_maximum_fusion.10), channel_id=1, source_target_pairs={{0,1},{1,0},{2,3},{3,2},{4,5},{5,4},{6,7},{7,6},{8,9},{9,8},{10,11... | collective-permute-start | bytes 3080 | tf_op jit(solution)/shard_map/ppermute | solution.py:22
  48.5 3.6 %collective-permute-start.11 = (f32[2,128]{1,0:T(2,128)S(1)}, f32[2,128]{1,0:T(2,128)S(1)}, u32[]{:S(2)}, u32[]{:S(2)}) collective-permute-start(f32[2,128]{1,0:T(2,128)S(1)} %fusion.217), channel_id=1, source_target_pairs={{0,2},{1,3},{2,0},{3,1},{4,6},{5,7},{6,4},{7,5},{8,10},{9,11},{10,... | collective-permute-start | bytes 3080 | tf_op jit(solution)/shard_map/ppermute | solution.py:22
  51.3 15.1 %collective-permute-start.3 = (bf16[128,2048]{1,0:T(8,128)(2,1)}, bf16[128,2048]{1,0:T(8,128)(2,1)}, u32[]{:S(2)}, u32[]{:S(2)}) collective-permute-start(bf16[128,2048]{1,0:T(8,128)(2,1)} %get-tuple-element.11), channel_id=1, source_target_pairs={{0,2},{1,3},{2,0},{3,1},{4,6},{5,7},{6,4},{7,5},{8,10},{9,11},{10,... | collective-permute-start | bytes 1572872 | tf_op jit(solution)/shard_map/ppermute | solution.py:22
  58.9 19.1 %collective-permute-start.12 = (bf16[128,2048]{0,1:T(8,128)(2,1)S(1)}, bf16[128,2048]{0,1:T(8,128)(2,1)}, u32[]{:S(2)}, u32[]{:S(2)}) collective-permute-start(bf16[128,2048]{0,1:T(8,128)(2,1)S(1)} %bitcast.258), channel_id=1, source_target_pairs={{0,2},{1,3},{2,0},{3,1},{4,6},{5,7},{6,4},{7,5},{8,10},{9,11},{10,... | collective-permute-start | bytes 1572872 | tf_op jit(solution)/shard_map/ppermute | solution.py:22
  60.2 25.6 %collective-permute-start.20 = (bf16[128,2048]{0,1:T(8,128)(2,1)S(1)}, bf16[128,2048]{0,1:T(8,128)(2,1)}, u32[]{:S(2)}, u32[]{:S(2)}) collective-permute-start(bf16[128,2048]{0,1:T(8,128)(2,1)S(1)} %bitcast.259), channel_id=1, source_target_pairs={{0,1},{1,0},{2,3},{3,2},{4,5},{5,4},{6,7},{7,6},{8,9},{9,8},{10,11... | collective-permute-start | bytes 1572872 | tf_op jit(solution)/shard_map/ppermute | solution.py:22
  68.8 6.4 %collective-permute-start.21 = (f32[128,321]{0,1:T(8,128)}, f32[128,321]{0,1:T(8,128)}, u32[]{:S(2)}, u32[]{:S(2)}) collective-permute-start(f32[128,321]{0,1:T(8,128)} %pad_maximum_fusion.6), channel_id=1, source_target_pairs={{0,1},{1,0},{2,3},{3,2},{4,5},{5,4},{6,7},{7,6},{8,9},{9,8},{10,11... | collective-permute-start | bytes 493064 | tf_op jit(solution)/shard_map/ppermute | solution.py:22
  69.4 17.8 %slice-start = ((s8[8388608]{0:T(1024)(128)(4,1)}), s8[4194304]{0:T(1024)(128)(4,1)S(1)}, s32[]{:S(2)}) async-start(s8[8388608]{0:T(1024)(128)(4,1)} %bitcast.250), calls=%async_computation | async-start | bytes 8388608
  73.0 1.4 %collective-permute-start.17 = (f32[1,128]{1,0:T(1,128)S(1)}, f32[1,128]{1,0:T(1,128)S(1)}, u32[]{:S(2)}, u32[]{:S(2)}) collective-permute-start(f32[1,128]{1,0:T(1,128)S(1)} %bitcast.318), channel_id=1, source_target_pairs={{0,1},{1,0},{2,3},{3,2},{4,5},{5,4},{6,7},{7,6},{8,9},{9,8},{10,11... | collective-permute-start | bytes 1544 | tf_op jit(solution)/shard_map/ppermute | solution.py:22
  74.4 3.5 %collective-permute-start.18 = (f32[1,128]{1,0:T(1,128)S(1)}, f32[1,128]{1,0:T(1,128)S(1)}, u32[]{:S(2)}, u32[]{:S(2)}) collective-permute-start(f32[1,128]{1,0:T(1,128)S(1)} %bitcast_add_fusion), channel_id=1, source_target_pairs={{0,2},{1,3},{2,0},{3,1},{4,6},{5,7},{6,4},{7,5},{8,10},{9,11},{10,... | collective-permute-start | bytes 1544 | tf_op jit(solution)/shard_map/ppermute | solution.py:22
  76.2 6.3 %collective-permute-start.22 = (f32[128,321]{0,1:T(8,128)S(1)}, f32[128,321]{0,1:T(8,128)S(1)}, u32[]{:S(2)}, u32[]{:S(2)}) collective-permute-start(f32[128,321]{0,1:T(8,128)S(1)} %fusion.220), channel_id=1, source_target_pairs={{0,2},{1,3},{2,0},{3,1},{4,6},{5,7},{6,4},{7,5},{8,10},{9,11},{10,... | collective-permute-start | bytes 493064 | tf_op jit(solution)/shard_map/ppermute | solution.py:22
  78.0 6.5 %collective-permute-start.13 = (bf16[128,2048]{0,1:T(8,128)(2,1)}, bf16[128,2048]{0,1:T(8,128)(2,1)S(1)}, u32[]{:S(2)}, u32[]{:S(2)}) collective-permute-start(bf16[128,2048]{0,1:T(8,128)(2,1)} %collective-permute-done.12), channel_id=1, source_target_pairs={{0,1},{1,0},{2,3},{3,2},{4,5},{5,4},{6,7},{7,6},{8,9},{9,8},{10,11... | collective-permute-start | bytes 1572872 | tf_op jit(solution)/shard_map/ppermute | solution.py:22
  84.5 11.1 %collective-permute-start.14 = (bf16[128,1024]{0,1:T(8,128)(2,1)S(1)}, bf16[128,1024]{0,1:T(8,128)(2,1)S(1)}, u32[]{:S(2)}, u32[]{:S(2)}) collective-permute-start(bf16[128,1024]{0,1:T(8,128)(2,1)S(1)} %fusion.105), channel_id=1, source_target_pairs={{0,2},{1,3},{2,0},{3,1},{4,6},{5,7},{6,4},{7,5},{8,10},{9,11},{10,... | collective-permute-start | bytes 786440 | tf_op jit(solution)/shard_map/ppermute | solution.py:22
  85.8 19.0 %collective-permute-start.16 = (bf16[128,1024]{0,1:T(8,128)(2,1)S(1)}, bf16[128,1024]{0,1:T(8,128)(2,1)S(1)}, u32[]{:S(2)}, u32[]{:S(2)}) collective-permute-start(bf16[128,1024]{0,1:T(8,128)(2,1)S(1)} %fusion.105), channel_id=1, source_target_pairs={{0,1},{1,0},{2,3},{3,2},{4,5},{5,4},{6,7},{7,6},{8,9},{9,8},{10,11... | collective-permute-start | bytes 786440 | tf_op jit(solution)/shard_map/ppermute | solution.py:22
  90.2 14.5 %collective-permute-start.23 = (bf16[128,512]{1,0:T(8,128)(2,1)S(1)}, bf16[128,512]{1,0:T(8,128)(2,1)S(1)}, u32[]{:S(2)}, u32[]{:S(2)}) collective-permute-start(bf16[128,512]{1,0:T(8,128)(2,1)S(1)} %fusion.42), channel_id=1, source_target_pairs={{0,28},{4,0},{8,4},{12,8},{16,12},{20,16},{24,20},{28,24},{1,29},{... | collective-permute-start | bytes 393224 | tf_op jit(solution)/shard_map/ppermute | solution.py:17
  94.7 10.0 %collective-permute-start.24 = (bf16[128,1024]{0,1:T(8,128)(2,1)S(1)}, bf16[128,1024]{0,1:T(8,128)(2,1)S(1)}, u32[]{:S(2)}, u32[]{:S(2)}) collective-permute-start(bf16[128,1024]{0,1:T(8,128)(2,1)S(1)} %copy-done.7), channel_id=1, source_target_pairs={{0,2},{1,3},{2,0},{3,1},{4,6},{5,7},{6,4},{7,5},{8,10},{9,11},{10,... | collective-permute-start | bytes 786440 | tf_op jit(solution)/shard_map/ppermute | solution.py:22
  95.6 9.2 %collective-permute-start.15 = (bf16[128,1024]{0,1:T(8,128)(2,1)S(1)}, bf16[128,1024]{0,1:T(8,128)(2,1)S(1)}, u32[]{:S(2)}, u32[]{:S(2)}) collective-permute-start(bf16[128,1024]{0,1:T(8,128)(2,1)S(1)} %collective-permute-done.14), channel_id=1, source_target_pairs={{0,1},{1,0},{2,3},{3,2},{4,5},{5,4},{6,7},{7,6},{8,9},{9,8},{10,11... | collective-permute-start | bytes 786440 | tf_op jit(solution)/shard_map/ppermute | solution.py:22
  104.2 1.7 %collective-permute-start.26 = (bf16[128,1024]{0,1:T(8,128)(2,1)S(1)}, bf16[128,1024]{0,1:T(8,128)(2,1)S(1)}, u32[]{:S(2)}, u32[]{:S(2)}) collective-permute-start(bf16[128,1024]{0,1:T(8,128)(2,1)S(1)} %copy-done.7), channel_id=1, source_target_pairs={{0,1},{1,0},{2,3},{3,2},{4,5},{5,4},{6,7},{7,6},{8,9},{9,8},{10,11... | collective-permute-start | bytes 786440 | tf_op jit(solution)/shard_map/ppermute | solution.py:22
  104.7 1.5 %collective-permute-start.25 = (bf16[128,1024]{0,1:T(8,128)(2,1)S(1)}, bf16[128,1024]{0,1:T(8,128)(2,1)S(1)}, u32[]{:S(2)}, u32[]{:S(2)}) collective-permute-start(bf16[128,1024]{0,1:T(8,128)(2,1)S(1)} %collective-permute-done.24), channel_id=1, source_target_pairs={{0,1},{1,0},{2,3},{3,2},{4,5},{5,4},{6,7},{7,6},{8,9},{9,8},{10,11... | collective-permute-start | bytes 786440 | tf_op jit(solution)/shard_map/ppermute | solution.py:22
  105.7 8.6 %collective-permute-start.19 = (bf16[128,512]{1,0:T(8,128)(2,1)S(1)}, bf16[128,512]{1,0:T(8,128)(2,1)S(1)}, u32[]{:S(2)}, u32[]{:S(2)}) collective-permute-start(bf16[128,512]{1,0:T(8,128)(2,1)S(1)} %fusion.45), channel_id=1, source_target_pairs={{0,4},{4,8},{8,12},{12,16},{16,20},{20,24},{24,28},{28,0},{1,5},{5... | collective-permute-start | bytes 393224 | tf_op jit(solution)/shard_map/ppermute | solution.py:17
  (50 other events, 257.9 us)
